TPU v7x, 32 devices: a whole 2x2x4 slice. The times are simulated.
32 devices in a mesh: scene: 2 (over x), space: 8 (over z, y), sub: 2 (over core).
Axes of the slice: x: 2, y: 2, z: 4, core: 2. Of those that a mesh axis runs over, the one named last changes fastest.
Arguments:
- features: bfloat16 [64, 1728, 128], P(('scene', 'space', 'sub')), parts along dimension 0, may hold values from -6 to 6
- out_grad: bfloat16 [64, 1728, 128], P(('scene', 'space', 'sub')), parts along dimension 0, may hold values from -6 to 6
- weight: bfloat16 [27, 128, 128], replicated, may hold values from -0.109375 to 0.109375
- neighbours: int32 [64, 6], P(('scene', 'space', 'sub')), parts along dimension 0, may hold values from -1 to 31, as said below
- active: int32 [64, 1728], P(('scene', 'space', 'sub')), parts along dimension 0, may hold values from 0 to 1
Outputs:
- input_grad: bfloat16 [64, 1728, 128], P(('scene', 'space', 'sub')), parts along dimension 0
- weight_grad: float32 [6912, 128], P(('scene', 'space', 'sub')), parts along dimension 0
There are 2 independent parts, one for each index of `scene`. A program takes and returns all parts, laid end to end along the dimension named above; an argument that names none is the same for every part. Nothing has to cross between parts.
Inputs may be any that keep to these rules, and one draw needn't show every extreme that they name: The bricks form a full grid of 2 x 2 x 8; slots s * 2 * 2 to (s + 1) * 2 * 2 - 1 hold layer s of the third dimension in some order, so neighbours along the first two dimensions lie in the same layer and along the third in the layer below or above.
All inputs are finite; a program needn't handle non-finite values.
Results may differ from a plain program's by a relative error of at most 0.001.
Values may be sent and summed in bfloat16 or wider, within the bound.
No kernel may reach another device: no remote copies, remote signals or barrier semaphores. Data moves between devices by JAX's collectives and lax.ppermute only.
A program may use at most 192 MiB of HBM per device.

v0:
```python
import jax
import jax.numpy as jnp
import numpy as np
from jax import lax
from jax.experimental import pallas as pl
from jax.experimental.pallas import tpu as pltpu
from jax.sharding import PartitionSpec as P

BSIDE = 12
PLANE = BSIDE * BSIDE
VOX = BSIDE * PLANE
EXT = BSIDE + 2
C = 128
KROWS = 256
LIMIT = 56 * 2**20
BF = jnp.bfloat16
F32 = jnp.float32


def strip_matrix():
    m = np.zeros((64, PLANE), np.float32)
    for i in range(BSIDE):
        m[i, i * BSIDE] = 1
        m[16 + i, i * BSIDE + 11] = 1
        m[32 + i, i] = 1
        m[48 + i, 11 * BSIDE + i] = 1
    m[12, 0] = m[28, 11] = 1
    m[13, 11 * BSIDE] = m[29, 11 * BSIDE + 11] = 1
    return m.astype(jnp.bfloat16)


def shift_matrix():
    m = np.zeros((9, BSIDE, BSIDE, KROWS), np.float32)
    for k in range(9):
        for b in range(BSIDE):
            for c in range(BSIDE):
                sb, sc = b - (k // 3 - 1), c - (k % 3 - 1)
                if sc in (-1, 12):
                    row = {-1: 13, 12: 12}.get(sb, sb) + (176 if sc < 0 else 192)
                elif sb in (-1, 12):
                    row = sc + (144 if sb < 0 else 160)
                else:
                    row = sb * BSIDE + sc
                m[k, b, c, row] = 1
    return m.reshape(9 * PLANE, KROWS).astype(jnp.bfloat16)


def mask_spread():
    m = np.zeros((2, BSIDE, BSIDE, 2, C), np.float32)
    for j in range(2):
        for p in range(BSIDE):
            m[j, p, p, j] = 1
    return m.reshape(2 * BSIDE, BSIDE * 2 * C).astype(jnp.bfloat16)


def dot(a, b):
    return lax.dot_general(a, b, (((1,), (0,)), ((), ())), preferred_element_type=F32)


def dot_t(a, b):
    return lax.dot_general(a, b, (((1,), (1,)), ((), ())), preferred_element_type=F32)


def halves(x):
    return jnp.concatenate([x[:, C:], x[:, :C]], axis=1)


def per_half(first, second, rows=16):
    lane = lax.broadcasted_iota(jnp.int32, (rows, 2 * C), 1)
    return jnp.where(lane < C, first, second)


def prep_kernel(nb, act, spread, strips, g, gm, subm, up, dn):
    mask = dot(act[...], spread[...]).astype(BF)
    a0 = per_half((nb[0, 0] >= 0).astype(F32), (nb[1, 0] >= 0).astype(F32))
    b0 = per_half((nb[0, 2] >= 0).astype(F32), (nb[1, 2] >= 0).astype(F32))
    code = (2 * a0 + b0).astype(BF)
    a0, b0 = a0.astype(BF), b0.astype(BF)
    for p in range(BSIDE):
        rows = pl.ds(p * PLANE, PLANE)
        plane = jnp.concatenate([g[0, rows, :], g[1, rows, :]], axis=1) * mask[:, p * 256 : p * 256 + 256]
        gm[p] = plane
        s = dot(strips[...], plane).astype(BF)
        dn[pl.ds(p * 16, 16), :] = s[0:16]
        up[pl.ds(p * 16, 16), :] = s[16:32]
        subm[pl.ds(PLANE + p * 16, 16), :] = s[32:48] * b0 + s[48:64] * (1 - b0)
    for r in range(0, PLANE, 16):
        subm[pl.ds(r, 16), :] = gm[0, pl.ds(r, 16), :] * a0 + gm[11, pl.ds(r, 16), :] * (1 - a0)
    subm[pl.ds(PLANE + 192, 16), :] = code
    up[pl.ds(192, 16), :] = code
    dn[pl.ds(192, 16), :] = code


def features_kernel(act, spread, eye, f, ft, pad):
    mask = dot(act[...], spread[...]).astype(BF)
    zero = jnp.zeros((2 * PLANE, C), BF)
    for j in range(2):
        pad[pl.ds(0, 2 * PLANE), :] = zero
        pad[pl.ds(EXT * PLANE, 2 * PLANE), :] = zero
        for p in range(BSIDE):
            pad[pl.ds((p + 2) * PLANE, PLANE), :] = (
                f[j, pl.ds(p * PLANE, PLANE), :] * mask[:, p * 256 + j * C : p * 256 + j * C + C]
            )
        for d in range(3):
            ft[j, pl.ds(d * C, C), :] = dot_t(eye[...], pad[pl.ds(d * PLANE, EXT * PLANE), :]).astype(BF)


def operands(gm, own, other, zs, kop):
    code = own[pl.ds(336, 16), :].astype(F32)
    a0 = jnp.where(code >= 2, 1.0, 0.0)
    b0 = code - 2 * a0
    to_a, to_b, to_d = code + 2 - 4 * a0, code + 1 - 2 * b0, 3 - code

    def weights(refs, at):
        tiles = []
        for ref, swaps in refs:
            t = ref[pl.ds(at, 16), :].astype(F32)
            tiles += [(ref, False, t)] if not swaps else [(ref, True, halves(t))]
        return tiles

    layer = weights([(own, True), (other, False), (other, True)], 336)

    def hits(cands, q):
        return [(ref, sw, jnp.where(t == q, 1.0, 0.0).astype(BF)) for ref, sw, t in cands]

    def gather(picks, row):
        total = None
        for ref, sw, w in picks:
            x = ref[pl.ds(row, 16), :]
            x = (halves(x) if sw else x) * w
            total = x if total is None else total + x
        return total

    row16 = lax.broadcasted_iota(jnp.int32, (16, 2 * C), 0)
    inner = jnp.where(row16 < 12, 1.0, 0.0).astype(BF)
    edge = jnp.where(row16 == 12, 1 - b0, jnp.where(row16 == 13, b0, 0.0)).astype(BF)
    a0h, b0h = a0.astype(BF), b0.astype(BF)
    a1h, b1h = 1 - a0h, 1 - b0h

    pick_a, pick_b, pick_d = hits(layer, to_a), hits(layer, to_b), hits(layer, to_d)
    vert = []
    for first, second in zs:
        cands = weights([(first, False), (first, True), (second, False), (second, True)], 192)
        vert.append(
            (
                [(r, s, w * inner) for r, s, w in hits(cands, code)],
                [(r, s, w * edge) for r, s, w in hits(cands, to_b)],
                [(r, s, w * inner) for r, s, w in hits(cands, to_a)],
                [(r, s, w * edge) for r, s, w in hits(cands, to_d)],
            )
        )
    pad = jnp.zeros((KROWS - 208, 2 * C), BF)
    for p in range(BSIDE):
        kop[p + 1, pl.ds(0, PLANE), :] = gm[p]
        side = gather(pick_b, PLANE + p * 16)
        kop[p + 1, pl.ds(144, 16), :] = side * b0h
        kop[p + 1, pl.ds(160, 16), :] = side * b1h
        for n, (self_, nb_, _, _) in enumerate(vert):
            kop[p + 1, pl.ds(176 + 16 * n, 16), :] = gather(self_, p * 16) + gather(nb_, p * 16)
        kop[p + 1, pl.ds(208, KROWS - 208), :] = pad

    def outer(at, plane, w):
        for r in range(0, PLANE, 16):
            kop[at, pl.ds(r, 16), :] = gather(pick_a, r) * w
        side = gather(pick_d, PLANE + plane * 16) * w
        kop[at, pl.ds(144, 16), :] = side * b0h
        kop[at, pl.ds(160, 16), :] = side * b1h
        for n, (_, _, self_, nb_) in enumerate(vert):
            kop[at, pl.ds(176 + 16 * n, 16), :] = (gather(self_, plane * 16) + gather(nb_, plane * 16)) * w
        kop[at, pl.ds(208, KROWS - 208), :] = pad

    outer(0, 11, a0h)
    outer(EXT - 1, 0, a1h)


def shifted(shift, kop, x):
    for p in range(EXT):
        for k in range(9):
            y = dot(shift[pl.ds(k * PLANE, PLANE), :], kop[p]).astype(BF)
            for j in range(2):
                x[j, pl.ds(p * PLANE, PLANE), pl.ds(k * C, C)] = y[:, j * C : j * C + C]


def wgrad_kernel(sub, shift, ft, gm, own, other, d0, d1, u0, u1, keep, send, kop, x, acc):
    operands(gm, own, other, ((d0, d1), (u0, u1)), kop)
    shifted(shift, kop, x)
    acc[...] = dot(ft[0], x[0])
    acc[...] += dot(ft[1], x[1])
    blocks = keep.shape[0]
    size = keep.shape[1]
    for parity in range(2):

        @pl.when(sub[0] == parity)
        def _(parity=parity):
            for t in range(27):
                da, k = divmod(t, 9)
                row = t * C
                while row < (t + 1) * C:
                    n = row // size
                    end = min((n + 1) * size, (t + 1) * C)
                    v = acc[pl.ds(da * C + row - t * C, end - row), pl.ds(k * C, C)] * (1.0 / VOX)
                    ref = keep if n % 2 == parity else send
                    ref[n // 2, pl.ds(row - n * size, end - row), :] = v
                    row = end


def dgrad_kernel(act, spread, shift, w, kop, out, x, y):
    shifted(shift, kop, x)
    mask = dot(act[...], spread[...])
    for j in range(2):
        for d in range(3):
            wd = jnp.concatenate([w[d * 9 + k] for k in range(9)], axis=1)
            y[:, pl.ds(d * C, C)] = dot_t(x[j], wd)
        for p in range(BSIDE):
            total = y[pl.ds((p + 2) * PLANE, PLANE), pl.ds(0, C)]
            total = total + y[pl.ds((p + 1) * PLANE, PLANE), pl.ds(C, C)]
            total = total + y[pl.ds(p * PLANE, PLANE), pl.ds(2 * C, C)]
            out[j, pl.ds(p * PLANE, PLANE), :] = (total * mask[:, p * 256 + j * C : p * 256 + j * C + C]).astype(BF)


VMEM = pl.BlockSpec(memory_space=pltpu.MemorySpace.VMEM)
SMEM = pl.BlockSpec(memory_space=pltpu.MemorySpace.SMEM)


def call(kernel, name, ins, outs, scratch=(), flops=0, size=0):
    return pl.pallas_call(
        kernel,
        name=name,
        out_shape=[jax.ShapeDtypeStruct(s, d) for s, d in outs],
        in_specs=ins,
        out_specs=[VMEM] * len(outs),
        scratch_shapes=list(scratch),
        compiler_params=pltpu.CompilerParams(vmem_limit_bytes=LIMIT),
        cost_estimate=pl.CostEstimate(flops=flops, transcendentals=0, bytes_accessed=size),
    )


def exchange(value, axis, bit):
    pairs = [(i, i ^ bit) for i in range(lax.axis_size(axis))]
    return lax.ppermute(value, axis, pairs)


def part(value, index, dim):
    return lax.dynamic_index_in_dim(value, index, dim, keepdims=False)


def halve(value, axis_bit, mine, dim):
    return part(value, mine, dim) + exchange(part(value, 1 - mine, dim), "space", axis_bit)


def reduce_blocks(blocks):
    s = lax.axis_index("space")
    rows = blocks.shape[1]
    cut = rows // 16 * 8
    b2, b1, b0 = (s >> 2) & 1, (s >> 1) & 1, s & 1
    v = blocks.reshape(2, 2, 2, rows, C)
    one = halve(v[:, :, :, :cut], 1, b0, 2)
    two = halve(v[:, :, :, cut:], 2, b1, 1)
    one = halve(one, 2, b1, 1)
    two = halve(two, 1, b0, 1)
    both = jnp.concatenate([one, two], axis=1)
    return halve(both, 4, b2, 0)


def on_device(features, out_grad, weight, neighbours, active):
    layers = lax.axis_size("space")
    sub = lax.axis_index("sub").astype(jnp.int32).reshape(1)
    act = active.reshape(2 * BSIDE, PLANE).T.astype(BF)
    spread, strips, shift = jnp.asarray(mask_spread()), jnp.asarray(strip_matrix()), jnp.asarray(shift_matrix())
    eye = jnp.asarray(np.eye(C, dtype=np.float32).astype(jnp.bfloat16))

    gm, own, up, dn = call(
        prep_kernel,
        "prep",
        [SMEM] + [VMEM] * 4,
        [((BSIDE, PLANE, 2 * C), BF), ((352, 2 * C), BF), ((208, 2 * C), BF), ((208, 2 * C), BF)],
    )(neighbours, act, spread, strips, out_grad)

    other = exchange(own, "sub", 1)
    both = ("space", "sub")
    vertical = []
    for step, message in ((1, up), (-1, dn)):
        for target in range(2):
            pairs = [
                (2 * i + j, 2 * (i + step) + (j ^ target))
                for i in range(layers)
                for j in range(2)
                if 0 <= i + step < layers
            ]
            vertical.append(lax.ppermute(message, both, pairs))

    (ft,) = call(
        features_kernel,
        "features",
        [VMEM] * 4,
        [((2, 3 * C, EXT * PLANE), BF)],
        [pltpu.VMEM(((EXT + 2) * PLANE, C), BF)],
        flops=2 * 2 * 3 * C * C * EXT * PLANE,
        size=4 * 2**20,
    )(act, spread, eye, features)

    size = 27 * C // (2 * layers)
    custom = layers == 8
    rows = (layers, size, C) if custom else (8, 216, C)
    keep, send, kop = call(
        wgrad_kernel,
        "wgrad",
        [SMEM] + [VMEM] * 9,
        [(rows, F32), (rows, F32), ((EXT, KROWS, 2 * C), BF)],
        [pltpu.VMEM((2, EXT * PLANE, 9 * C), BF), pltpu.VMEM((3 * C, 9 * C), F32)],
        flops=2 * 3 * C * 9 * C * 2 * EXT * PLANE,
        size=8 * 2**20,
    )(sub, shift, ft, gm, own, other, *vertical)

    if custom:
        weight_grad = reduce_blocks(keep + exchange(send, "sub", 1))
    else:
        even = jnp.where(sub[0] == 0, keep, send)
        odd = jnp.where(sub[0] == 0, send, keep)
        kernel_term = jnp.stack([even, odd], axis=1).reshape(27 * C, C)
        weight_grad = lax.psum_scatter(kernel_term, both, scatter_dimension=0, tiled=True)

    (input_grad,) = call(
        dgrad_kernel,
        "dgrad",
        [VMEM] * 5,
        [((2, VOX, C), BF)],
        [pltpu.VMEM((2, EXT * PLANE, 9 * C), BF), pltpu.VMEM((EXT * PLANE, 3 * C), F32)],
        flops=2 * 3 * C * 9 * C * 2 * EXT * PLANE,
        size=4 * 2**20,
    )(act, spread, shift, weight, kop)
    return input_grad, weight_grad


def solution(mesh):
    in_specs = (
        P(("scene", "space", "sub"), None, None),
        P(("scene", "space", "sub"), None, None),
        P(),
        P(("scene", "space", "sub"), None),
        P(("scene", "space", "sub"), None),
    )
    out_specs = (P(("scene", "space", "sub"), None, None), P(("scene", "space", "sub"), None))
    return jax.shard_map(
        on_device, mesh=mesh, in_specs=in_specs, out_specs=out_specs, check_vma=False
    )
```

profile of v0, /device:TPU:0, one launch (start us, length us, event | category | flops | bytes accessed | tf_op | source)
XLA Modules:
  0.0 70.1 jit_solution(16669352051349242715)
XLA Ops:
  0.6 0.7 %convert_element_type.7 = bf16[2,1728]{1,0:T(2,128)(2,1)S(1)} convert(s32[2,1728]{1,0:T(2,128)} %param.13) | non-fusion elementwise | flops 3456 | bytes 20736 | tf_op jit(solution)/shard_map/convert_element_type | solution.py:268
  1.3 0.1 convert_element_type.8
  1.5 0.7 %copy.11 = bf16[24,144]{0,1:T(8,128)(2,1)} copy(bf16[24,144]{1,0:T(8,128)(2,1)S(1)} %convert_element_type.8) | data formatting | bytes 13824 | tf_op jit(solution)/shard_map/convert_element_type | solution.py:268
  2.2 2.7 %prep.1 = (bf16[12,144,256]{2,1,0:T(8,128)(2,1)}, bf16[352,256]{1,0:T(8,128)(2,1)}, bf16[208,256]{1,0:T(8,128)(2,1)}, bf16[208,256]{1,0:T(8,128)(2,1)}) custom-call(s32[2,6]{1,0:T(2,128)} %nb.1, bf16[144,24]{1,0:T(8,128)(2,1)} %bitcast.27, bf16[24,3072]{1,0:T(8,128)(2,1)} %constant.55.clone.spread, bf16[64,144]{1,0:T(8,128)(2,1)} %constant.56.clone.strips, ...), custom_call_target="tpu_custom_call" | custom-call | tf_op jit(solution)/shard_map/prep/pallas_call | solution.py:272
  4.9 0.5 collective-permute-start
  5.3 4.4 %collective-permute-start.1 = (bf16[208,256]{1,0:T(8,128)(2,1)}, bf16[208,256]{1,0:T(8,128)(2,1)S(1)}, u32[]{:S(2)}, u32[]{:S(2)}) collective-permute-start(bf16[208,256]{1,0:T(8,128)(2,1)} %get-tuple-element.11), channel_id=1, source_target_pairs={{0,2},{1,3},{2,4},{3,5},{4,6},{5,7},{6,8},{7,9},{8,10},{9,11},{10,... | collective-permute-start | bytes 319496 | tf_op jit(solution)/shard_map/ppermute | solution.py:290
  9.7 3.3 %collective-permute-start.2 = (bf16[208,256]{1,0:T(8,128)(2,1)}, bf16[208,256]{1,0:T(8,128)(2,1)S(1)}, u32[]{:S(2)}, u32[]{:S(2)}) collective-permute-start(bf16[208,256]{1,0:T(8,128)(2,1)} %get-tuple-element.11), channel_id=1, source_target_pairs={{0,3},{1,2},{2,5},{3,4},{4,7},{5,6},{6,9},{7,8},{8,11},{9,10},{10,... | collective-permute-start | bytes 319496 | tf_op jit(solution)/shard_map/ppermute | solution.py:290
  13.0 1.3 %collective-permute-start.3 = (bf16[208,256]{1,0:T(8,128)(2,1)}, bf16[208,256]{1,0:T(8,128)(2,1)S(1)}, u32[]{:S(2)}, u32[]{:S(2)}) collective-permute-start(bf16[208,256]{1,0:T(8,128)(2,1)} %get-tuple-element.12), channel_id=1, source_target_pairs={{2,0},{3,1},{4,2},{5,3},{6,4},{7,5},{8,6},{9,7},{10,8},{11,9},{12,... | collective-permute-start | bytes 319496 | tf_op jit(solution)/shard_map/ppermute | solution.py:290
  14.3 1.3 %collective-permute-start.4 = (bf16[208,256]{1,0:T(8,128)(2,1)}, bf16[208,256]{1,0:T(8,128)(2,1)S(1)}, u32[]{:S(2)}, u32[]{:S(2)}) collective-permute-start(bf16[208,256]{1,0:T(8,128)(2,1)} %get-tuple-element.12), channel_id=1, source_target_pairs={{2,1},{3,0},{4,3},{5,2},{6,5},{7,4},{8,7},{9,6},{10,9},{11,8},{12,... | collective-permute-start | bytes 319496 | tf_op jit(solution)/shard_map/ppermute | solution.py:290
  15.6 4.4 %features.1.ft = bf16[2,384,2016]{2,1,0:T(8,128)(2,1)} custom-call(bf16[144,24]{1,0:T(8,128)(2,1)} %bitcast.28, bf16[24,3072]{1,0:T(8,128)(2,1)} %constant.55.clone.spread, bf16[128,128]{1,0:T(8,128)(2,1)} %constant.58.clone.eye, bf16[2,1728,128]{2,1,0:T(8,128)(2,1)} %f.1), custom_call_target="tpu_custom_call" | custom-call | flops 396361728 | bytes 4194304 | tf_op jit(solution)/shard_map/features/pallas_call | solution.py:292
  20.0 0.0 collective-permute-done.1.d0
  20.0 0.0 copy-start.1
  20.0 0.0 collective-permute-done.2.d1
  20.0 0.0 copy-start.2
  20.0 0.6 collective-permute-done.3.u0
  20.6 0.0 copy-start.3
  20.6 1.6 %collective-permute-done.4.u1 = bf16[208,256]{1,0:T(8,128)(2,1)S(1)} collective-permute-done((bf16[208,256]{1,0:T(8,128)(2,1)}, bf16[208,256]{1,0:T(8,128)(2,1)S(1)}, u32[]{:S(2)}, u32[]{:S(2)}) %collective-permute-start.4) | collective-permute-done | bytes 106528 | tf_op jit(solution)/shard_map/ppermute | solution.py:290
  22.2 0.0 copy-start.4
  22.2 0.0 collective-permute-done.other
  22.2 0.0 copy-start
  22.2 0.0 copy-done.1
  22.2 0.0 copy-done.2
  22.2 0.0 copy-done.3
  22.3 0.6 copy-done.4
  22.9 0.1 copy-done
  23.0 11.4 %wgrad.1 = (f32[8,216,128]{2,1,0:T(8,128)}, f32[8,216,128]{2,1,0:T(8,128)}, bf16[14,256,256]{2,1,0:T(8,128)(2,1)}) custom-call(s32[1]{0:T(128)} %bitcast.1.sub, bf16[1296,256]{1,0:T(8,128)(2,1)} %constant.57.clone.shift, bf16[2,384,2016]{2,1,0:T(8,128)(2,1)} %features.1.ft, bf16[12,144,256]{2,1,0:T(8,128)(2,1)} %get-tuple-element.9.gm, ...), custom_call_target="tpu_custom_call" | custom-call | flops 3567255552 | bytes 8388608 | tf_op jit(solution)/shard_map/wgrad/pallas_call | solution.py:305
  34.4 0.2 collective-permute-start.5
  34.6 2.5 %collective-permute-done.5 = f32[8,216,128]{2,1,0:T(8,128)S(1)} collective-permute-done((f32[8,216,128]{2,1,0:T(8,128)}, f32[8,216,128]{2,1,0:T(8,128)S(1)}, u32[]{:S(2)}, u32[]{:S(2)}) %collective-permute-start.5) | collective-permute-done | bytes 884768 | tf_op jit(solution)/shard_map/ppermute | solution.py:240
  37.0 1.3 %add.48 = f32[8,216,128]{2,1,0:T(8,128)S(1)} add(f32[8,216,128]{2,1,0:T(8,128)} %get-tuple-element.14, f32[8,216,128]{2,1,0:T(8,128)S(1)} %collective-permute-done.5) | non-fusion elementwise | flops 221184 | bytes 2654208 | tf_op jit(solution)/shard_map/add | solution.py:316
  38.4 2.9 %collective-permute-start.6 = (f32[2,2,104,128]{3,2,1,0:T(8,128)S(1)}, f32[2,2,104,128]{3,2,1,0:T(8,128)S(1)}, u32[]{:S(2)}, u32[]{:S(2)}) collective-permute-start(f32[2,2,104,128]{3,2,1,0:T(8,128)S(1)} %dynamic-slice_bitcast_fusion.1), channel_id=1, source_target_pairs={{0,2},{2,0},{4,6},{6,4},{8,10},{10,8},{12,14},{14,12},{1,3},{3,1},... | collective-permute-start | bytes 638984 | tf_op jit(solution)/shard_map/ppermute | solution.py:240
  41.3 1.7 %collective-permute-start.8 = (f32[2,2,112,128]{3,2,1,0:T(8,128)S(1)}, f32[2,2,112,128]{3,2,1,0:T(8,128)S(1)}, u32[]{:S(2)}, u32[]{:S(2)}) collective-permute-start(f32[2,2,112,128]{3,2,1,0:T(8,128)S(1)} %dynamic-slice_bitcast_fusion), channel_id=1, source_target_pairs={{0,4},{2,6},{4,0},{6,2},{8,12},{10,14},{12,8},{14,10},{1,5},{3,7},... | collective-permute-start | bytes 688136 | tf_op jit(solution)/shard_map/ppermute | solution.py:240
  43.0 3.8 %collective-permute-done.6 = f32[2,2,104,128]{3,2,1,0:T(8,128)S(1)} collective-permute-done((f32[2,2,104,128]{3,2,1,0:T(8,128)S(1)}, f32[2,2,104,128]{3,2,1,0:T(8,128)S(1)}, u32[]{:S(2)}, u32[]{:S(2)}) %collective-permute-start.6) | collective-permute-done | bytes 213024 | tf_op jit(solution)/shard_map/ppermute | solution.py:240
  46.8 1.9 %collective-permute-start.7 = (f32[2,104,128]{2,1,0:T(8,128)S(1)}, f32[2,104,128]{2,1,0:T(8,128)S(1)}, u32[]{:S(2)}, u32[]{:S(2)}) collective-permute-start(f32[2,104,128]{2,1,0:T(8,128)S(1)} %dynamic-slice_bitcast_fusion.3), channel_id=1, source_target_pairs={{0,4},{2,6},{4,0},{6,2},{8,12},{10,14},{12,8},{14,10},{1,5},{3,7},... | collective-permute-start | bytes 319496 | tf_op jit(solution)/shard_map/ppermute | solution.py:240
  48.7 0.0 collective-permute-done.8
  48.8 1.6 %collective-permute-start.9 = (f32[2,112,128]{2,1,0:T(8,128)S(1)}, f32[2,112,128]{2,1,0:T(8,128)S(1)}, u32[]{:S(2)}, u32[]{:S(2)}) collective-permute-start(f32[2,112,128]{2,1,0:T(8,128)S(1)} %dynamic-slice_bitcast_fusion.2), channel_id=1, source_target_pairs={{0,2},{2,0},{4,6},{6,4},{8,10},{10,8},{12,14},{14,12},{1,3},{3,1},... | collective-permute-start | bytes 344072 | tf_op jit(solution)/shard_map/ppermute | solution.py:240
  50.4 1.3 %collective-permute-done.7 = f32[2,104,128]{2,1,0:T(8,128)S(1)} collective-permute-done((f32[2,104,128]{2,1,0:T(8,128)S(1)}, f32[2,104,128]{2,1,0:T(8,128)S(1)}, u32[]{:S(2)}, u32[]{:S(2)}) %collective-permute-start.7) | collective-permute-done | bytes 106528 | tf_op jit(solution)/shard_map/ppermute | solution.py:240
  51.6 2.0 %collective-permute-done.9 = f32[2,112,128]{2,1,0:T(8,128)S(1)} collective-permute-done((f32[2,112,128]{2,1,0:T(8,128)S(1)}, f32[2,112,128]{2,1,0:T(8,128)S(1)}, u32[]{:S(2)}, u32[]{:S(2)}) %collective-permute-start.9) | collective-permute-done | bytes 114720 | tf_op jit(solution)/shard_map/ppermute | solution.py:240
  53.7 2.7 %collective-permute-start.10 = (f32[216,128]{1,0:T(8,128)S(1)}, f32[216,128]{1,0:T(8,128)S(1)}, u32[]{:S(2)}, u32[]{:S(2)}) collective-permute-start(f32[216,128]{1,0:T(8,128)S(1)} %fusion.1), channel_id=1, source_target_pairs={{0,8},{2,10},{4,12},{6,14},{8,0},{10,2},{12,4},{14,6},{1,9},{3,11}... | collective-permute-start | bytes 331784 | tf_op jit(solution)/shard_map/ppermute | solution.py:240
  56.4 13.1 %dgrad.1 = bf16[2,1728,128]{2,1,0:T(8,128)(2,1)} custom-call(bf16[144,24]{1,0:T(8,128)(2,1)} %bitcast.29, bf16[24,3072]{1,0:T(8,128)(2,1)} %constant.55.clone.spread, bf16[1296,256]{1,0:T(8,128)(2,1)} %constant.57.clone.shift, bf16[27,128,128]{2,1,0:T(8,128)(2,1)} %w.1, bf16[14,256,256]{2,1,0:T(8,128)(2,1)} %get-tuple-element.13.kop), custom_call_target="tpu_custom_call" | custom-call | flops 3567255552 | bytes 4194304 | tf_op jit(solution)/shard_map/dgrad/pallas_call | solution.py:323
  69.5 0.0 collective-permute-done.10
  69.5 0.7 fusion.4
  (11 shorter events, 0.2 us)
Async XLA Ops:
  4.9 17.4 %collective-permute-start = (bf16[352,256]{1,0:T(8,128)(2,1)}, bf16[352,256]{1,0:T(8,128)(2,1)S(1)}, u32[]{:S(2)}, u32[]{:S(2)}) collective-permute-start(bf16[352,256]{1,0:T(8,128)(2,1)} %get-tuple-element.10.own), channel_id=1, source_target_pairs={{0,1},{1,0},{2,3},{3,2},{4,5},{5,4},{6,7},{7,6},{8,9},{9,8},{10,11... | collective-permute-start | bytes 540680 | tf_op jit(solution)/shard_map/ppermute | solution.py:240
  5.3 14.7 %collective-permute-start.1 = (bf16[208,256]{1,0:T(8,128)(2,1)}, bf16[208,256]{1,0:T(8,128)(2,1)S(1)}, u32[]{:S(2)}, u32[]{:S(2)}) collective-permute-start(bf16[208,256]{1,0:T(8,128)(2,1)} %get-tuple-element.11), channel_id=1, source_target_pairs={{0,2},{1,3},{2,4},{3,5},{4,6},{5,7},{6,8},{7,9},{8,10},{9,11},{10,... | collective-permute-start | bytes 319496 | tf_op jit(solution)/shard_map/ppermute | solution.py:290
  9.7 10.3 %collective-permute-start.2 = (bf16[208,256]{1,0:T(8,128)(2,1)}, bf16[208,256]{1,0:T(8,128)(2,1)S(1)}, u32[]{:S(2)}, u32[]{:S(2)}) collective-permute-start(bf16[208,256]{1,0:T(8,128)(2,1)} %get-tuple-element.11), channel_id=1, source_target_pairs={{0,3},{1,2},{2,5},{3,4},{4,7},{5,6},{6,9},{7,8},{8,11},{9,10},{10,... | collective-permute-start | bytes 319496 | tf_op jit(solution)/shard_map/ppermute | solution.py:290
  13.0 7.6 %collective-permute-start.3 = (bf16[208,256]{1,0:T(8,128)(2,1)}, bf16[208,256]{1,0:T(8,128)(2,1)S(1)}, u32[]{:S(2)}, u32[]{:S(2)}) collective-permute-start(bf16[208,256]{1,0:T(8,128)(2,1)} %get-tuple-element.12), channel_id=1, source_target_pairs={{2,0},{3,1},{4,2},{5,3},{6,4},{7,5},{8,6},{9,7},{10,8},{11,9},{12,... | collective-permute-start | bytes 319496 | tf_op jit(solution)/shard_map/ppermute | solution.py:290
  14.3 7.9 %collective-permute-start.4 = (bf16[208,256]{1,0:T(8,128)(2,1)}, bf16[208,256]{1,0:T(8,128)(2,1)S(1)}, u32[]{:S(2)}, u32[]{:S(2)}) collective-permute-start(bf16[208,256]{1,0:T(8,128)(2,1)} %get-tuple-element.12), channel_id=1, source_target_pairs={{2,1},{3,0},{4,3},{5,2},{6,5},{7,4},{8,7},{9,6},{10,9},{11,8},{12,... | collective-permute-start | bytes 319496 | tf_op jit(solution)/shard_map/ppermute | solution.py:290
  20.0 2.2 %copy-start.1 = (bf16[208,256]{1,0:T(8,128)(2,1)}, bf16[208,256]{1,0:T(8,128)(2,1)S(1)}, u32[]{:S(2)}) copy-start(bf16[208,256]{1,0:T(8,128)(2,1)S(1)} %collective-permute-done.1.d0) | copy-start | bytes 319492
  20.0 2.2 %copy-start.2 = (bf16[208,256]{1,0:T(8,128)(2,1)}, bf16[208,256]{1,0:T(8,128)(2,1)S(1)}, u32[]{:S(2)}) copy-start(bf16[208,256]{1,0:T(8,128)(2,1)S(1)} %collective-permute-done.2.d1) | copy-start | bytes 319492
  20.6 1.7 %copy-start.3 = (bf16[208,256]{1,0:T(8,128)(2,1)}, bf16[208,256]{1,0:T(8,128)(2,1)S(1)}, u32[]{:S(2)}) copy-start(bf16[208,256]{1,0:T(8,128)(2,1)S(1)} %collective-permute-done.3.u0) | copy-start | bytes 319492
  22.2 0.7 copy-start.4
  22.2 0.7 %copy-start = (bf16[352,256]{1,0:T(8,128)(2,1)}, bf16[352,256]{1,0:T(8,128)(2,1)S(1)}, u32[]{:S(2)}) copy-start(bf16[352,256]{1,0:T(8,128)(2,1)S(1)} %collective-permute-done.other) | copy-start | bytes 540676
  34.4 2.6 %collective-permute-start.5 = (f32[8,216,128]{2,1,0:T(8,128)}, f32[8,216,128]{2,1,0:T(8,128)S(1)}, u32[]{:S(2)}, u32[]{:S(2)}) collective-permute-start(f32[8,216,128]{2,1,0:T(8,128)} %get-tuple-element.15), channel_id=1, source_target_pairs={{0,1},{1,0},{2,3},{3,2},{4,5},{5,4},{6,7},{7,6},{8,9},{9,8},{10,11... | collective-permute-start | bytes 2654216 | tf_op jit(solution)/shard_map/ppermute | solution.py:240
  38.4 8.4 %collective-permute-start.6 = (f32[2,2,104,128]{3,2,1,0:T(8,128)S(1)}, f32[2,2,104,128]{3,2,1,0:T(8,128)S(1)}, u32[]{:S(2)}, u32[]{:S(2)}) collective-permute-start(f32[2,2,104,128]{3,2,1,0:T(8,128)S(1)} %dynamic-slice_bitcast_fusion.1), channel_id=1, source_target_pairs={{0,2},{2,0},{4,6},{6,4},{8,10},{10,8},{12,14},{14,12},{1,3},{3,1},... | collective-permute-start | bytes 638984 | tf_op jit(solution)/shard_map/ppermute | solution.py:240
  41.3 7.4 %collective-permute-start.8 = (f32[2,2,112,128]{3,2,1,0:T(8,128)S(1)}, f32[2,2,112,128]{3,2,1,0:T(8,128)S(1)}, u32[]{:S(2)}, u32[]{:S(2)}) collective-permute-start(f32[2,2,112,128]{3,2,1,0:T(8,128)S(1)} %dynamic-slice_bitcast_fusion), channel_id=1, source_target_pairs={{0,4},{2,6},{4,0},{6,2},{8,12},{10,14},{12,8},{14,10},{1,5},{3,7},... | collective-permute-start | bytes 688136 | tf_op jit(solution)/shard_map/ppermute | solution.py:240
  46.8 4.8 %collective-permute-start.7 = (f32[2,104,128]{2,1,0:T(8,128)S(1)}, f32[2,104,128]{2,1,0:T(8,128)S(1)}, u32[]{:S(2)}, u32[]{:S(2)}) collective-permute-start(f32[2,104,128]{2,1,0:T(8,128)S(1)} %dynamic-slice_bitcast_fusion.3), channel_id=1, source_target_pairs={{0,4},{2,6},{4,0},{6,2},{8,12},{10,14},{12,8},{14,10},{1,5},{3,7},... | collective-permute-start | bytes 319496 | tf_op jit(solution)/shard_map/ppermute | solution.py:240
  48.8 4.9 %collective-permute-start.9 = (f32[2,112,128]{2,1,0:T(8,128)S(1)}, f32[2,112,128]{2,1,0:T(8,128)S(1)}, u32[]{:S(2)}, u32[]{:S(2)}) collective-permute-start(f32[2,112,128]{2,1,0:T(8,128)S(1)} %dynamic-slice_bitcast_fusion.2), channel_id=1, source_target_pairs={{0,2},{2,0},{4,6},{6,4},{8,10},{10,8},{12,14},{14,12},{1,3},{3,1},... | collective-permute-start | bytes 344072 | tf_op jit(solution)/shard_map/ppermute | solution.py:240
  53.7 15.8 %collective-permute-start.10 = (f32[216,128]{1,0:T(8,128)S(1)}, f32[216,128]{1,0:T(8,128)S(1)}, u32[]{:S(2)}, u32[]{:S(2)}) collective-permute-start(f32[216,128]{1,0:T(8,128)S(1)} %fusion.1), channel_id=1, source_target_pairs={{0,8},{2,10},{4,12},{6,14},{8,0},{10,2},{12,4},{14,6},{1,9},{3,11}... | collective-permute-start | bytes 331784 | tf_op jit(solution)/shard_map/ppermute | solution.py:240
where the time goes:
time: 70.5 us; the launch traced here: 70.1 us
  Pallas kernels  31.6 us (45%)
  starting transfers between devices  21.5 us (30%)
  waiting for transfers between devices  11.8 us (17%)
  other arithmetic  2.73 us (4%)
  local copies, waits for them, and re-layouts  1.69 us (2%)
  between operations  0.78 us (1%)
    pallas_call x1, Pallas kernels, on_device(): call(dgrad_kernel, 'dgrad', [VMEM] * 5, [((2, VOX, C), BF)], [pltpu.VMEM(...  13.1 us
    pallas_call x1, Pallas kernels, on_device(): call(wgrad_kernel, 'wgrad', [SMEM] + [VMEM] * 9, [(rows, F32), (rows, F32...  11.4 us
    ppermute x7, starting transfers between devices, exchange(): return lax.ppermute(value, axis, pairs)  11.2 us
    ppermute x4, starting transfers between devices, on_device(): vertical.append(lax.ppermute(message, both, pairs))  10.3 us
    ppermute x7, waiting for transfers between devices, exchange(): return lax.ppermute(value, axis, pairs)  9.61 us
    pallas_call x1, Pallas kernels, on_device(): call(features_kernel, 'features', [VMEM] * 4, [((2, 3 * C, EXT * PLANE),...  4.37 us
    pallas_call x1, Pallas kernels, on_device(): call(prep_kernel, 'prep', [SMEM] + [VMEM] * 4, [((BSIDE, PLANE, 2 * C), B...  2.7 us
    ppermute x4, waiting for transfers between devices, on_device(): vertical.append(lax.ppermute(message, both, pairs))  2.21 us
  transfers between devices with their start and end apart: 11, of which 6 were waited for; matrix products, arithmetic and copies ran while one was open for 0% of the time, Pallas kernels for 25%

commit v1 on v0

v1 whole, which is shorter than its diff:
```python
import jax
import jax.numpy as jnp
import numpy as np
from jax import lax
from jax.experimental import pallas as pl
from jax.experimental.pallas import tpu as pltpu
from jax.sharding import PartitionSpec as P

BSIDE = 12
PLANE = BSIDE * BSIDE
VOX = BSIDE * PLANE
EXT = BSIDE + 2
C = 128
KROWS = 256
MINE = PLANE + 208
LIMIT = 16 * 2**20
BF = jnp.bfloat16
F32 = jnp.float32


def strip_matrix():
    m = np.zeros((64, PLANE), np.float32)
    for i in range(BSIDE):
        m[i, i * BSIDE] = 1
        m[16 + i, i * BSIDE + 11] = 1
        m[32 + i, i] = 1
        m[48 + i, 11 * BSIDE + i] = 1
    m[12, 0] = m[28, 11] = 1
    m[13, 11 * BSIDE] = m[29, 11 * BSIDE + 11] = 1
    return m.astype(jnp.bfloat16)


def shift_matrix():
    m = np.zeros((9, BSIDE, BSIDE, KROWS), np.float32)
    for k in range(9):
        for b in range(BSIDE):
            for c in range(BSIDE):
                sb, sc = b - (k // 3 - 1), c - (k % 3 - 1)
                if sc in (-1, 12):
                    row = {-1: 13, 12: 12}.get(sb, sb) + (176 if sc < 0 else 192)
                elif sb in (-1, 12):
                    row = sc + (144 if sb < 0 else 160)
                else:
                    row = sb * BSIDE + sc
                m[k, b, c, row] = 1
    return m.reshape(9 * PLANE, KROWS).astype(jnp.bfloat16)


def band_matrix():
    m = np.zeros((3, EXT, 16, EXT, 16), np.float32)
    for q in range(3):
        for b in range(BSIDE):
            source = b - (q - 1)
            for p in range(EXT):
                m[q, p, b, p, 13 if source < 0 else source] = 1
    return m.reshape(3 * EXT * 16, EXT * 16).astype(jnp.bfloat16)


def dot(a, b):
    return lax.dot_general(a, b, (((1,), (0,)), ((), ())), preferred_element_type=F32)


def dot_t(a, b):
    return lax.dot_general(a, b, (((1,), (1,)), ((), ())), preferred_element_type=F32)


def halves(x):
    return jnp.concatenate([x[:, C:], x[:, :C]], axis=1)


def per_half(first, second, rows=16):
    lane = lax.broadcasted_iota(jnp.int32, (rows, 2 * C), 1)
    return jnp.where(lane < C, first, second)


def masks(act, out):
    r = lax.broadcasted_iota(jnp.int32, (C, C), 0)
    eye = jnp.where(r == lax.broadcasted_iota(jnp.int32, (C, C), 1), 1.0, 0.0)
    wide = lax.broadcasted_iota(jnp.int32, (2 * C, 2 * C), 0) < C
    ones = jnp.where(wide == (lax.broadcasted_iota(jnp.int32, (2 * C, 2 * C), 1) < C), 1.0, 0.0).astype(BF)
    for n in range(0, VOX, C):
        cols = []
        for j in range(2):
            a = act[pl.ds(j, 1), pl.ds(n, min(C, VOX - n))].astype(F32)
            if n + C > VOX:
                a = jnp.concatenate([a, jnp.zeros((1, n + C - VOX), F32)], axis=1)
            cols.append((eye * a).astype(BF))
        out[pl.ds(n, C), :] = dot(jnp.concatenate(cols, axis=1), ones).astype(BF)


def prep_kernel(sub, nb, act_hbm, strips_hbm, g_hbm, gm, message, mine, mask, act, strips, g, sem):
    loads = [
        pltpu.make_async_copy(act_hbm, act, sem.at[0]),
        pltpu.make_async_copy(strips_hbm, strips, sem.at[1]),
        pltpu.make_async_copy(g_hbm, g, sem.at[2]),
    ]
    for load in loads:
        load.start()
    loads[0].wait()
    masks(act, mask)
    a0 = per_half((nb[0, 0] >= 0).astype(F32), (nb[1, 0] >= 0).astype(F32))
    b0 = per_half((nb[0, 2] >= 0).astype(F32), (nb[1, 2] >= 0).astype(F32))
    code = (2 * a0 + b0).astype(BF)
    a0, b0 = a0.astype(BF), b0.astype(BF)
    second = jnp.full((16, 2 * C), sub[0].astype(F32), F32).astype(BF)
    loads[1].wait()
    loads[2].wait()
    for p in range(BSIDE):
        rows = pl.ds(p * PLANE, PLANE)
        plane = jnp.concatenate([g[0, rows, :], g[1, rows, :]], axis=1) * mask[rows, :]
        gm[p] = plane
        s = dot(strips[...], plane).astype(BF)
        mine[pl.ds(p * 16, 16), :] = s[0:16] * second + s[16:32] * (1 - second)
        message[pl.ds(MINE + p * 16, 16), :] = s[16:32] * second + s[0:16] * (1 - second)
        message[pl.ds(PLANE + p * 16, 16), :] = s[32:48] * b0 + s[48:64] * (1 - b0)
    for r in range(0, PLANE, 16):
        message[pl.ds(r, 16), :] = gm[0, pl.ds(r, 16), :] * a0 + gm[11, pl.ds(r, 16), :] * (1 - a0)
    message[pl.ds(PLANE + 192, 16), :] = code
    message[pl.ds(MINE + 192, 16), :] = code
    mine[pl.ds(192, 16), :] = code


def features_kernel(mask, strips, f, pad, fs):
    zero = jnp.zeros((2 * PLANE, C), BF)
    edge = jnp.zeros((32, 2 * C), BF)
    for j in range(2):
        pad[j, pl.ds(0, 2 * PLANE), :] = zero
        pad[j, pl.ds(EXT * PLANE, 2 * PLANE), :] = zero
        pad[j, pl.ds(2 * PLANE, VOX), :] = f[j] * mask[pl.ds(0, VOX), pl.ds(j * C, C)]
    for n in range(2):
        fs[n, pl.ds(0, 32), :] = edge
        fs[n, pl.ds(EXT * 16, 32), :] = edge
    for p in range(BSIDE):
        rows = pl.ds((p + 2) * PLANE, PLANE)
        s = dot(strips[pl.ds(0, 32), :], jnp.concatenate([pad[0, rows, :], pad[1, rows, :]], axis=1)).astype(BF)
        for n in range(2):
            fs[n, pl.ds((p + 2) * 16, 16), :] = s[16 * n : 16 * n + 16]


def position(own):
    code = own[pl.ds(336, 16), :].astype(F32)
    a0 = jnp.where(code >= 2, 1.0, 0.0)
    b0 = code - 2 * a0
    return code, a0, b0


def candidates(refs, at):
    tiles = []
    for ref, base, swapped in refs:
        t = ref[pl.ds(base + at, 16), :].astype(F32)
        tiles.append(((ref, base, swapped), halves(t) if swapped else t))
    return tiles


def hits(cands, q):
    return [(*source, jnp.where(t == q, 1.0, 0.0).astype(BF)) for source, t in cands]


def gather(picks, row):
    total = None
    for ref, base, swapped, w in picks:
        x = ref[pl.ds(base + row, 16), :]
        x = (halves(x) if swapped else x) * w
        total = x if total is None else total + x
    return total


def layer_operands(gm, own, other, kop):
    code, a0, b0 = position(own)
    layer = candidates([(own, 0, True), (other, 0, False), (other, 0, True)], 336)
    pick_a = hits(layer, code + 2 - 4 * a0)
    pick_b = hits(layer, code + 1 - 2 * b0)
    pick_d = hits(layer, 3 - code)
    a0h, b0h = a0.astype(BF), b0.astype(BF)
    a1h, b1h = 1 - a0h, 1 - b0h
    rest = jnp.zeros((KROWS - 176, 2 * C), BF)
    for p in range(BSIDE):
        kop[p + 1, pl.ds(0, PLANE), :] = gm[p]
        side = gather(pick_b, PLANE + p * 16)
        kop[p + 1, pl.ds(144, 16), :] = side * b0h
        kop[p + 1, pl.ds(160, 16), :] = side * b1h
        kop[p + 1, pl.ds(176, KROWS - 176), :] = rest
    for at, plane, w in ((0, 11, a0h), (EXT - 1, 0, a1h)):
        for r in range(0, PLANE, 16):
            kop[at, pl.ds(r, 16), :] = gather(pick_a, r) * w
        side = gather(pick_d, PLANE + plane * 16) * w
        kop[at, pl.ds(144, 16), :] = side * b0h
        kop[at, pl.ds(160, 16), :] = side * b1h
        kop[at, pl.ds(176, KROWS - 176), :] = rest


def vertical_operands(own, zs, z):
    code, a0, b0 = position(own)
    row16 = lax.broadcasted_iota(jnp.int32, (16, 2 * C), 0)
    inner = jnp.where(row16 < 12, 1.0, 0.0).astype(BF)
    edge = jnp.where(row16 == 12, 1 - b0, jnp.where(row16 == 13, b0, 0.0)).astype(BF)
    a0h = a0.astype(BF)
    for n, ref in enumerate(zs):
        cands = candidates([(ref, base, swapped) for base in (0, 208) for swapped in (False, True)], 192)
        near = [(*q, w * inner) for *q, w in hits(cands, code)]
        near += [(*q, w * edge) for *q, w in hits(cands, code + 1 - 2 * b0)]
        far = [(*q, w * inner) for *q, w in hits(cands, code + 2 - 4 * a0)]
        far += [(*q, w * edge) for *q, w in hits(cands, 3 - code)]
        for p in range(BSIDE):
            z[n, pl.ds((p + 1) * 16, 16), :] = gather(near, p * 16)
        z[n, pl.ds(0, 16), :] = gather(far, 11 * 16) * a0h
        z[n, pl.ds((EXT - 1) * 16, 16), :] = gather(far, 0) * (1 - a0h)


def shifted(shift, kop, x, ks, first, count):
    for p in range(count):
        for n, k in enumerate(ks):
            y = dot(shift[pl.ds(k * PLANE, PLANE), :], kop[first + p]).astype(BF)
            for j in range(2):
                x[j, pl.ds(p * PLANE, PLANE), pl.ds(n * C, C)] = y[:, j * C : j * C + C]


def stacked(ref, j, width, lanes):
    return jnp.concatenate([ref[j, pl.ds(d * width, EXT * width), lanes] for d in range(3)], axis=1)


def dot_rows(a, b):
    return lax.dot_general(a, b, (((0,), (0,)), ((), ())), preferred_element_type=F32)


def first_kernel(shift, gm, own, other, pad, x, acc, kop):
    layer_operands(gm, own, other, kop)
    shifted(shift, kop, x, range(9), 0, EXT)
    acc[...] = dot_rows(stacked(pad, 0, PLANE, slice(None)), x[0])


def second_kernel(pad, x, before, acc):
    acc[...] = before[...] + dot_rows(stacked(pad, 1, PLANE, slice(None)), x[1])


def tilt_kernel(sub, own, got, got2, fs, bands, acc, keep, send, zs, z, more):
    for parity in range(2):

        @pl.when(sub[0] == parity)
        def _(parity=parity):
            vertical_operands(own, (got2, got) if parity else (got, got2), z)

    for n in range(2):
        v = dot(bands[...], z[n]).astype(BF)
        rows = EXT * 16
        total = None
        for j in range(2):
            lanes = slice(j * C, j * C + C)
            zs[n, j] = jnp.concatenate([v[q * rows : q * rows + rows, lanes] for q in range(3)], axis=1)
            f3 = jnp.concatenate([fs[n, pl.ds(d * 16, rows), lanes] for d in range(3)], axis=1)
            part_ = dot_rows(f3, zs[n, j])
            total = part_ if total is None else total + part_
        more[n] = total
    size = keep.shape[1]
    for parity in range(2):

        @pl.when(sub[0] == parity)
        def _(parity=parity):
            for t in range(27):
                da, k = divmod(t, 9)
                row = t * C
                while row < (t + 1) * C:
                    block = row // size
                    end = min((block + 1) * size, (t + 1) * C)
                    at = pl.ds(da * C + row - t * C, end - row)
                    v = acc[at, pl.ds(k * C, C)]
                    if k % 3 != 1:
                        v = v + more[0 if k % 3 == 2 else 1, at, pl.ds(k // 3 * C, C)]
                    ref = keep if block % 2 == parity else send
                    ref[block // 2, pl.ds(row - block * size, end - row), :] = v * (1.0 / VOX)
                    row = end


def columns(w, ks):
    return jnp.concatenate([jnp.concatenate([w[d * 9 + k] for k in ks], axis=1) for d in range(3)], axis=0)


def joined(y, p, rows):
    total = y[pl.ds((p + 2) * rows, rows), pl.ds(0, C)]
    total = total + y[pl.ds((p + 1) * rows, rows), pl.ds(C, C)]
    return total + y[pl.ds(p * rows, rows), pl.ds(2 * C, C)]


def dgrad_kernel(j, mask, w, x, zs, before, out, y, yz, plane, res, sem):
    del before
    y[...] = dot_t(x[j], columns(w, range(9)))
    for n in range(2):
        yz[n] = dot_t(zs[n, j], columns(w, (2, 5, 8) if n == 0 else (0, 3, 6)))
    for p in range(BSIDE):
        plane[pl.ds(0, PLANE), :] = joined(y, p, PLANE)
        for n in range(2):
            at = pl.ds(11 * n, BSIDE, stride=BSIDE)
            plane[at, :] = plane[at, :] + joined(yz.at[n], p, 16)[:BSIDE]
        m = mask[pl.ds(p * PLANE, PLANE), pl.ds(j * C, C)].astype(F32)
        res[pl.ds(p * PLANE, PLANE), :] = (plane[pl.ds(0, PLANE), :] * m).astype(BF)
    store = pltpu.make_async_copy(res, out.at[j], sem)
    store.start()
    store.wait()


def blocks_kernel(bits, keep, got, send1, keep1, send2, keep2):
    b0, b1 = bits[0], bits[1]
    cut = send1.shape[2]
    for z1 in range(2):
        for n in range(2):
            for flip, ref1, ref2 in ((0, keep1, keep2), (1, send1, send2)):
                i = z1 * 4 + n * 2 + jnp.bitwise_xor(b0, flip)
                ref1[z1, n] = keep[i, pl.ds(0, cut), :] + got[i, pl.ds(0, cut), :]
                i = z1 * 4 + jnp.bitwise_xor(b1, flip) * 2 + n
                rest = pl.ds(cut, keep.shape[1] - cut)
                ref2[z1, n] = keep[i, rest, :] + got[i, rest, :]


def halves_kernel(bits, one, got1, two, got2, send1, keep1, send2, keep2):
    b0, b1 = bits[0], bits[1]
    for z1 in range(2):
        for flip, ref1, ref2 in ((0, keep1, keep2), (1, send1, send2)):
            i, k = jnp.bitwise_xor(b1, flip), jnp.bitwise_xor(b0, flip)
            ref1[z1] = one[z1, i] + got1[z1, i]
            ref2[z1] = two[z1, k] + got2[z1, k]


def last_kernel(bits, one, got1, two, got2, send, keep):
    cut = one.shape[1]
    for flip, ref in ((0, keep), (1, send)):
        i = jnp.bitwise_xor(bits[2], flip)
        ref[pl.ds(0, cut), :] = one[i] + got1[i]
        ref[pl.ds(cut, two.shape[1]), :] = two[i] + got2[i]


VMEM = pl.BlockSpec(memory_space=pltpu.MemorySpace.VMEM)
SMEM = pl.BlockSpec(memory_space=pltpu.MemorySpace.SMEM)
ANY = pl.BlockSpec(memory_space=pl.ANY)
HBM = pl.BlockSpec(memory_space=pltpu.MemorySpace.HBM)


def call(kernel, name, ins, outs, scratch=(), aliases=None, flops=0, size=0):
    return pl.pallas_call(
        kernel,
        name=name,
        out_shape=[jax.ShapeDtypeStruct(s, d) for s, d, _ in outs],
        in_specs=ins,
        out_specs=[o for _, _, o in outs],
        scratch_shapes=list(scratch),
        input_output_aliases=aliases or {},
        compiler_params=pltpu.CompilerParams(vmem_limit_bytes=LIMIT),
        cost_estimate=pl.CostEstimate(flops=flops, transcendentals=0, bytes_accessed=size),
    )


def exchange(value, axis, bit):
    pairs = [(i, i ^ bit) for i in range(lax.axis_size(axis))]
    return lax.ppermute(value, axis, pairs)


def tied(*values):
    return lax.optimization_barrier(values)


def reduce_blocks(keep, got, fillers):
    s = lax.axis_index("space").astype(jnp.int32)
    bits = jnp.stack([s & 1, (s >> 1) & 1, (s >> 2) & 1])
    rows = keep.shape[1]
    cut = rows // 16 * 8

    def sums(kernel, name, lead, *values):
        shapes = [((*lead, cut, C), F32, VMEM)] * 2 + [((*lead, rows - cut, C), F32, VMEM)] * 2
        return call(kernel, name, [SMEM] + [VMEM] * len(values), shapes)(bits, *values)

    send1, keep1, send2, keep2 = sums(blocks_kernel, "blocks", (2, 2), keep, got)
    got1, got2 = exchange(send1, "space", 1), exchange(send2, "space", 2)
    got1, got2, fill = tied(got1, got2, fillers[0](None))
    send1, keep1, send2, keep2 = sums(halves_kernel, "halves", (2,), keep1, got1, keep2, got2)
    got1, got2 = exchange(send1, "space", 2), exchange(send2, "space", 1)
    send, keep = call(last_kernel, "last", [SMEM] + [VMEM] * 4, [((rows, C), F32, VMEM)] * 2)(
        bits, keep1, got1, keep2, got2
    )
    got, fill = tied(exchange(send, "space", 4), fillers[1](fill))
    return keep + got, fill


def on_device(features, out_grad, weight, neighbours, active):
    layers = lax.axis_size("space")
    sub = lax.axis_index("sub").astype(jnp.int32).reshape(1)
    strips, shift, bands = jnp.asarray(strip_matrix()), jnp.asarray(shift_matrix()), jnp.asarray(band_matrix())

    gm, own, mine, mask = call(
        prep_kernel,
        "prep",
        [SMEM] * 2 + [HBM] * 3,
        [
            ((BSIDE, PLANE, 2 * C), BF, VMEM),
            ((MINE + 208, 2 * C), BF, VMEM),
            ((208, 2 * C), BF, VMEM),
            ((14 * C, 2 * C), BF, VMEM),
        ],
        [
            pltpu.VMEM((2, VOX), jnp.int32),
            pltpu.VMEM((64, PLANE), BF),
            pltpu.VMEM((2, VOX, C), BF),
            pltpu.SemaphoreType.DMA((3,)),
        ],
    )(sub, neighbours, active, strips, out_grad)

    other = exchange(own, "sub", 1)
    pad, fs = call(
        features_kernel,
        "features",
        [VMEM] * 3,
        [((2, (EXT + 2) * PLANE, C), BF, VMEM), ((2, (EXT + 2) * 16, 2 * C), BF, VMEM)],
        flops=10**7,
        size=10**6,
    )(mask, strips, features)

    ways = [(2 * i, 2 * i + 2) for i in range(layers - 1)] + [(2 * i + 3, 2 * i + 1) for i in range(layers - 1)]
    got = lax.ppermute(jnp.concatenate([mine, other[MINE:]], axis=0), ("space", "sub"), ways)

    kop_shape = (EXT, KROWS, 2 * C)
    work = 2 * 3 * C * 9 * C * EXT * PLANE
    x, acc = call(
        first_kernel,
        "first",
        [VMEM] * 5,
        [((2, EXT * PLANE, 9 * C), BF, VMEM), ((3 * C, 9 * C), F32, VMEM)],
        [pltpu.VMEM(kop_shape, BF)],
        flops=2 * work,
        size=8 * 2**20,
    )(shift, gm, own, other, pad)
    got, acc = tied(got, acc)
    got2 = exchange(got, "sub", 1)
    (acc,) = call(
        second_kernel,
        "second",
        [VMEM, VMEM, VMEM],
        [((3 * C, 9 * C), F32, VMEM)],
        flops=work,
        size=4 * 2**20,
    )(pad, x, acc)

    size = 27 * C // (2 * layers)
    custom = layers == 8
    rows = (layers, size, C) if custom else (8, 216, C)
    keep, send, zs = call(
        tilt_kernel,
        "tilt",
        [SMEM] + [VMEM] * 6,
        [(rows, F32, VMEM), (rows, F32, VMEM), ((2, 2, EXT * 16, 3 * C), BF, VMEM)],
        [pltpu.VMEM((2, EXT * 16, 2 * C), BF), pltpu.VMEM((2, 3 * C, 3 * C), F32)],
        flops=work // 4,
        size=4 * 2**20,
    )(sub, own, got, got2, fs, bands, acc)

    def dgrad(j):
        def run(before):
            fresh = before is None
            return call(
                (lambda m, w, x_, z, *refs: dgrad_kernel(j, m, w, x_, z, None, *refs))
                if fresh
                else (lambda *refs: dgrad_kernel(j, *refs)),
                "dgrad",
                [VMEM] * 4 + ([] if fresh else [ANY]),
                [((2, VOX, C), BF, ANY)],
                [
                    pltpu.VMEM((EXT * PLANE, 3 * C), F32),
                    pltpu.VMEM((2, EXT * 16, 3 * C), F32),
                    pltpu.VMEM((PLANE + 16, C), F32),
                    pltpu.VMEM((VOX, C), BF),
                    pltpu.SemaphoreType.DMA,
                ],
                aliases={} if fresh else {4: 0},
                flops=work,
                size=4 * 2**20,
            )(mask, weight, x, zs, *(() if fresh else (before,)))[0]

        return run

    if custom:
        got = exchange(send, "sub", 1)
        got, zs = tied(got, zs)
        weight_grad, input_grad = reduce_blocks(keep, got, [dgrad(0), dgrad(1)])
    else:
        even = jnp.where(sub[0] == 0, keep, send)
        odd = jnp.where(sub[0] == 0, send, keep)
        kernel_term = jnp.stack([even, odd], axis=1).reshape(27 * C, C)
        weight_grad = lax.psum_scatter(kernel_term, ("space", "sub"), scatter_dimension=0, tiled=True)
        input_grad = dgrad(1)(dgrad(0)(None))
    return input_grad, weight_grad


def solution(mesh):
    in_specs = (
        P(("scene", "space", "sub"), None, None),
        P(("scene", "space", "sub"), None, None),
        P(),
        P(("scene", "space", "sub"), None),
        P(("scene", "space", "sub"), None),
    )
    out_specs = (P(("scene", "space", "sub"), None, None), P(("scene", "space", "sub"), None))
    return jax.shard_map(
        on_device, mesh=mesh, in_specs=in_specs, out_specs=out_specs, check_vma=False
    )
```

time: 70.5 us -> 52.8 us (0.75)
  Pallas kernels: 31.6 us -> 21.7 us
  starting transfers between devices: 21.5 us -> 11.9 us
  local copies, waits for them, and re-layouts: 1.69 us -> 8.55 us
  waiting for transfers between devices: 11.8 us -> 8.73 us
  other arithmetic: 2.73 us -> 0.75 us
    pallas_call x4 -> x10, Pallas kernels: 31.6 us -> 21.7 us  [the longest x2 7.8 us: run(): call((lambda m, w, x_, z, *refs: dgrad_kernel(j, m, w, x_, z, None, *refs...]
    unnamed x10 -> x22, local copies, waits for them, and re-layouts: 0.73 us -> 8.54 us
    ppermute x4 -> x1, starting transfers between devices: 10.3 us -> 4.45 us  [on_device(): lax.ppermute(jnp.concatenate([mine, other[MINE:]], axis=0), ('space', 'su...]
    ppermute x7 -> x8, starting transfers between devices: 11.2 us -> 7.44 us  [exchange(): return lax.ppermute(value, axis, pairs)]
    ppermute x7 -> x8, waiting for transfers between devices: 9.61 us -> 7.83 us  [exchange(): return lax.ppermute(value, axis, pairs)]
    add x6 -> x1, other arithmetic: 1.99 us -> 0.66 us  [reduce_blocks(): return (keep + got, fill)]
    ppermute x4 -> x1, waiting for transfers between devices: 2.21 us -> 0.91 us  [on_device(): lax.ppermute(jnp.concatenate([mine, other[MINE:]], axis=0), ('space', 'su...]
    convert_element_type x2 -> x0, local copies, waits for them, and re-layouts: 0.81 us -> none  [on_device(): act = active.reshape(2 * BSIDE, PLANE).T.astype(BF)]
  transfers between devices with their start and end apart: 11 -> 9, of which waited for: 6 -> 5; matrix products, arithmetic and copies ran while one was open for 0% -> 0% of each run, Pallas kernels for 25% -> 29%
where the time goes in v1:
time: 52.8 us; the launch traced here: 52.4 us
  Pallas kernels  21.7 us (41%)
  starting transfers between devices  11.9 us (23%)
  waiting for transfers between devices  8.73 us (17%)
  local copies, waits for them, and re-layouts  8.55 us (16%)
  between operations  0.78 us (1%)
  other arithmetic  0.75 us (1%)
    unnamed x22, local copies, waits for them, and re-layouts  8.54 us
    ppermute x8, waiting for transfers between devices, exchange(): return lax.ppermute(value, axis, pairs)  7.83 us
    pallas_call x2, Pallas kernels, run(): call((lambda m, w, x_, z, *refs: dgrad_kernel(j, m, w, x_, z, None, *refs...  7.8 us
    ppermute x8, starting transfers between devices, exchange(): return lax.ppermute(value, axis, pairs)  7.44 us
    pallas_call x1, Pallas kernels, on_device(): call(first_kernel, 'first', [VMEM] * 5, [((2, EXT * PLANE, 9 * C), BF, VM...  4.68 us
    ppermute x1, starting transfers between devices, on_device(): lax.ppermute(jnp.concatenate([mine, other[MINE:]], axis=0), ('space', 'su...  4.45 us
    pallas_call x1, Pallas kernels, on_device(): call(tilt_kernel, 'tilt', [SMEM] + [VMEM] * 6, [(rows, F32, VMEM), (rows,...  2.49 us
    pallas_call x1, Pallas kernels, on_device(): call(second_kernel, 'second', [VMEM, VMEM, VMEM], [((3 * C, 9 * C), F32,...  2.26 us
  transfers between devices with their start and end apart: 9, of which 5 were waited for; matrix products, arithmetic and copies ran while one was open for 0% of the time, Pallas kernels for 29%

profile of v1, /device:TPU:0, one launch (start us, length us, event | category | flops | bytes accessed | tf_op | source)
XLA Modules:
  0.0 52.4 jit_solution(8781680177943014169)
XLA Ops:
  0.6 0.0 copy-start.5
  0.6 1.2 %copy-done.5 = bf16[2,1728,128]{2,1,0:T(8,128)(2,1)S(1)} copy-done((bf16[2,1728,128]{2,1,0:T(8,128)(2,1)S(1)}, bf16[2,1728,128]{2,1,0:T(8,128)(2,1)}, u32[]{:S(2)}) %copy-start.5) | copy-done | bytes 884760
  1.8 0.0 copy-start.7
  1.8 0.8 %copy-done.7 = bf16[64,144]{1,0:T(8,128)(2,1)S(1)} copy-done((bf16[64,144]{1,0:T(8,128)(2,1)S(1)}, bf16[64,144]{1,0:T(8,128)(2,1)}, u32[]{:S(2)}) %copy-start.7) | copy-done | bytes 18456
  2.6 0.0 copy-start.8
  2.6 0.7 %copy-done.8 = s32[2,1728]{1,0:T(2,128)S(1)} copy-done((s32[2,1728]{1,0:T(2,128)S(1)}, s32[2,1728]{1,0:T(2,128)}, u32[]{:S(2)}) %copy-start.8) | copy-done | bytes 13848
  3.3 0.0 copy-start.9
  3.3 0.7 %copy-done.9 = s32[2,6]{1,0:T(2,128)S(1)} copy-done((s32[2,6]{1,0:T(2,128)S(1)}, s32[2,6]{1,0:T(2,128)}, u32[]{:S(2)}) %copy-start.9) | copy-done | bytes 72
  4.0 0.0 copy-start.10
  4.0 1.6 %prep.1 = (bf16[12,144,256]{2,1,0:T(8,128)(2,1)S(1)}, bf16[560,256]{1,0:T(8,128)(2,1)S(1)}, bf16[208,256]{1,0:T(8,128)(2,1)S(1)}, bf16[1792,256]{1,0:T(8,128)(2,1)S(1)}) custom-call(s32[1]{0:T(128)} %bitcast.3.sub, s32[2,6]{1,0:T(2,128)S(1)} %copy-done.9, s32[2,1728]{1,0:T(2,128)S(1)} %copy-done.8, bf16[64,144]{1,0:T(8,128)(2,1)S(1)} %copy-done.7, ...), custom_call_target="tpu_custom_call" | custom-call | tf_op jit(solution)/shard_map/prep/pallas_call | solution.py:387
  5.5 0.5 collective-permute-start
  6.0 0.0 copy-start.4
  6.1 1.2 %copy-done.4 = bf16[2,1728,128]{2,1,0:T(8,128)(2,1)S(1)} copy-done((bf16[2,1728,128]{2,1,0:T(8,128)(2,1)S(1)}, bf16[2,1728,128]{2,1,0:T(8,128)(2,1)}, u32[]{:S(2)}) %copy-start.4) | copy-done | bytes 884760
  7.2 0.5 features.1
  7.7 0.0 collective-permute-done.other
  7.8 4.4 %collective-permute-start.1 = (bf16[416,256]{1,0:T(8,128)(2,1)S(1)}, bf16[416,256]{1,0:T(8,128)(2,1)S(1)}, u32[]{:S(2)}, u32[]{:S(2)}) collective-permute-start(bf16[416,256]{1,0:T(8,128)(2,1)S(1)} %pad_maximum_fusion), channel_id=1, source_target_pairs={{0,2},{2,4},{4,6},{6,8},{8,10},{10,12},{12,14},{3,1},{5,3},{7,5},{... | collective-permute-start | bytes 638984 | tf_op jit(solution)/shard_map/ppermute | solution.py:416
  12.2 0.0 copy-done.10
  12.2 4.7 %first.1 = (bf16[2,2016,1152]{2,1,0:T(8,128)(2,1)S(1)}, f32[384,1152]{1,0:T(8,128)S(1)}) custom-call(bf16[1296,256]{1,0:T(8,128)(2,1)S(1)} %copy-done.10, bf16[12,144,256]{2,1,0:T(8,128)(2,1)S(1)} %get-tuple-element.34.gm, bf16[560,256]{1,0:T(8,128)(2,1)S(1)} %get-tuple-element.32.own, bf16[560,256]{1,0:T(8,128)(2,1)S(1)} %collective-permute-done.other, ...), custom_call_target="tpu_custom_call" | custom-call | flops 3567255552 | bytes 8388608 | tf_op jit(solution)/shard_map/first/pallas_call | solution.py:420
  16.9 0.0 copy-start
  16.9 0.9 %collective-permute-done.1.got = bf16[416,256]{1,0:T(8,128)(2,1)S(1)} collective-permute-done((bf16[416,256]{1,0:T(8,128)(2,1)S(1)}, bf16[416,256]{1,0:T(8,128)(2,1)S(1)}, u32[]{:S(2)}, u32[]{:S(2)}) %collective-permute-start.1) | collective-permute-done | bytes 213024 | tf_op jit(solution)/shard_map/ppermute | solution.py:416
  17.8 0.0 collective-permute-start.2
  17.8 2.3 %second.1.acc = f32[384,1152]{1,0:T(8,128)S(1)} custom-call(bf16[2,2304,128]{2,1,0:T(8,128)(2,1)S(1)} %get-tuple-element.36.pad, bf16[2,2016,1152]{2,1,0:T(8,128)(2,1)S(1)} %get-tuple-element.40.x.x_.refs_2_, f32[384,1152]{1,0:T(8,128)S(1)} %get-tuple-element.41.before), custom_call_target="tpu_custom_call" | custom-call | flops 1783627776 | bytes 4194304 | tf_op jit(solution)/shard_map/second/pallas_call | solution.py:431
  20.1 0.4 copy-done
  20.5 0.0 collective-permute-done.2.got2
  20.5 0.0 copy-done.6
  20.5 2.5 %tilt.1 = (f32[8,216,128]{2,1,0:T(8,128)S(1)}, f32[8,216,128]{2,1,0:T(8,128)}, bf16[2,2,224,384]{3,2,1,0:T(8,128)(2,1)S(1)}) custom-call(s32[1]{0:T(128)} %bitcast.3.sub, bf16[560,256]{1,0:T(8,128)(2,1)S(1)} %get-tuple-element.32.own, bf16[416,256]{1,0:T(8,128)(2,1)S(1)} %collective-permute-done.1.got, bf16[416,256]{1,0:T(8,128)(2,1)S(1)} %collective-permute-done.2.got2, ...), custom_call_target="tpu_custom_call" | custom-call | flops 445906944 | bytes 4194304 | tf_op jit(solution)/shard_map/tilt/pallas_call | solution.py:443
  23.0 0.2 collective-permute-start.3
  23.2 0.1 pad_add_fusion.bits
  23.2 2.5 %collective-permute-done.3.got = f32[8,216,128]{2,1,0:T(8,128)} collective-permute-done((f32[8,216,128]{2,1,0:T(8,128)}, f32[8,216,128]{2,1,0:T(8,128)}, u32[]{:S(2)}, u32[]{:S(2)}) %collective-permute-start.3) | collective-permute-done | bytes 884768 | tf_op jit(solution)/shard_map/ppermute | solution.py:353
  25.8 1.3 %blocks.1 = (f32[2,2,104,128]{3,2,1,0:T(8,128)S(1)}, f32[2,2,104,128]{3,2,1,0:T(8,128)S(1)}, f32[2,2,112,128]{3,2,1,0:T(8,128)S(1)}, f32[2,2,112,128]{3,2,1,0:T(8,128)S(1)}) custom-call(s32[3]{0:T(128)S(1)} %pad_add_fusion.bits, f32[8,216,128]{2,1,0:T(8,128)S(1)} %get-tuple-element.42.keep, f32[8,216,128]{2,1,0:T(8,128)} %collective-permute-done.3.got), custom_call_target="tpu_custom_call" | custom-call | tf_op jit(solution)/shard_map/blocks/pallas_call | solution.py:368
  27.1 1.6 %collective-permute-start.5 = (f32[2,2,112,128]{3,2,1,0:T(8,128)S(1)}, f32[2,2,112,128]{3,2,1,0:T(8,128)S(1)}, u32[]{:S(2)}, u32[]{:S(2)}) collective-permute-start(f32[2,2,112,128]{3,2,1,0:T(8,128)S(1)} %get-tuple-element.48), channel_id=1, source_target_pairs={{0,4},{2,6},{4,0},{6,2},{8,12},{10,14},{12,8},{14,10},{1,5},{3,7},... | collective-permute-start | bytes 688136 | tf_op jit(solution)/shard_map/ppermute | solution.py:353
  28.7 2.3 %collective-permute-start.4 = (f32[2,2,104,128]{3,2,1,0:T(8,128)S(1)}, f32[2,2,104,128]{3,2,1,0:T(8,128)S(1)}, u32[]{:S(2)}, u32[]{:S(2)}) collective-permute-start(f32[2,2,104,128]{3,2,1,0:T(8,128)S(1)} %get-tuple-element.47), channel_id=1, source_target_pairs={{0,2},{2,0},{4,6},{6,4},{8,10},{10,8},{12,14},{14,12},{1,3},{3,1},... | collective-permute-start | bytes 638984 | tf_op jit(solution)/shard_map/ppermute | solution.py:353
  31.0 0.0 copy-done.3
  31.0 3.6 %copy-done.1 = bf16[2,2016,1152]{2,1,0:T(8,128)(2,1)S(1)} copy-done((bf16[2,2016,1152]{2,1,0:T(8,128)(2,1)S(1)}, bf16[2,2016,1152]{2,1,0:T(8,128)(2,1)}, u32[]{:S(2)}) %copy-start.1) | copy-done | bytes 9289752
  34.6 3.9 %dgrad.2.refs_4_ = bf16[2,1728,128]{2,1,0:T(8,128)(2,1)} custom-call(bf16[1792,256]{1,0:T(8,128)(2,1)S(1)} %get-tuple-element.35.mask.m.refs_0_, bf16[27,128,128]{2,1,0:T(8,128)(2,1)S(1)} %copy-done.3, bf16[2,2016,1152]{2,1,0:T(8,128)(2,1)S(1)} %copy-done.1, bf16[2,2,224,384]{3,2,1,0:T(8,128)(2,1)S(1)} %get-tuple-element.49.z.refs_3_), custom_call_target="tpu_custom_call" | custom-call | flops 1783627776 | bytes 4194304 | tf_op jit(solution)/shard_map/dgrad/pallas_call | solution.py:456
  38.5 0.0 collective-permute-done.4.got1
  38.5 0.0 collective-permute-done.5.got2
  38.6 0.6 %halves.1 = (f32[2,104,128]{2,1,0:T(8,128)S(1)}, f32[2,104,128]{2,1,0:T(8,128)S(1)}, f32[2,112,128]{2,1,0:T(8,128)S(1)}, f32[2,112,128]{2,1,0:T(8,128)S(1)}) custom-call(s32[3]{0:T(128)S(1)} %pad_add_fusion.bits, f32[2,2,104,128]{3,2,1,0:T(8,128)S(1)} %get-tuple-element.46.one, f32[2,2,104,128]{3,2,1,0:T(8,128)S(1)} %collective-permute-done.4.got1, ...), custom_call_target="tpu_custom_call" | custom-call | tf_op jit(solution)/shard_map/halves/pallas_call | solution.py:368
  39.2 0.1 collective-permute-start.7
  39.2 0.5 collective-permute-start.6
  39.7 4.3 %collective-permute-done.6.got1 = f32[2,104,128]{2,1,0:T(8,128)S(1)} collective-permute-done((f32[2,104,128]{2,1,0:T(8,128)S(1)}, f32[2,104,128]{2,1,0:T(8,128)S(1)}, u32[]{:S(2)}, u32[]{:S(2)}) %collective-permute-start.6) | collective-permute-done | bytes 106528 | tf_op jit(solution)/shard_map/ppermute | solution.py:353
  44.0 0.1 collective-permute-done.7.got2
  44.1 0.6 %last.1 = (f32[216,128]{1,0:T(8,128)S(1)}, f32[216,128]{1,0:T(8,128)S(1)}) custom-call(s32[3]{0:T(128)S(1)} %pad_add_fusion.bits, f32[2,104,128]{2,1,0:T(8,128)S(1)} %get-tuple-element.53.one, f32[2,104,128]{2,1,0:T(8,128)S(1)} %collective-permute-done.6.got1, f32[2,112,128]{2,1,0:T(8,128)S(1)} %get-tuple-element.55.two, ...), custom_call_target="tpu_custom_call" | custom-call | tf_op jit(solution)/shard_map/last/pallas_call | solution.py:375
  44.7 2.3 %collective-permute-start.8 = (f32[216,128]{1,0:T(8,128)S(1)}, f32[216,128]{1,0:T(8,128)S(1)}, u32[]{:S(2)}, u32[]{:S(2)}) collective-permute-start(f32[216,128]{1,0:T(8,128)S(1)} %get-tuple-element.57), channel_id=1, source_target_pairs={{0,8},{2,10},{4,12},{6,14},{8,0},{10,2},{12,4},{14,6},{1,9},{3,11}... | collective-permute-start | bytes 331784 | tf_op jit(solution)/shard_map/ppermute | solution.py:353
  46.9 0.0 copy-done.2
  46.9 3.9 %dgrad.3 = bf16[2,1728,128]{2,1,0:T(8,128)(2,1)} custom-call(bf16[1792,256]{1,0:T(8,128)(2,1)S(1)} %get-tuple-element.35.mask.m.refs_0_, bf16[27,128,128]{2,1,0:T(8,128)(2,1)S(1)} %copy-done.3, bf16[2,2016,1152]{2,1,0:T(8,128)(2,1)S(1)} %copy-done.2, bf16[2,2,224,384]{3,2,1,0:T(8,128)(2,1)S(1)} %get-tuple-element.49.z.refs_3_, ...), custom_call_target="tpu_custom_call", output_to_operand_aliasing={{}: (4, {})} | custom-call | flops 1783627776 | bytes 4194304 | tf_op jit(solution)/shard_map/dgrad/pallas_call | solution.py:456
  50.8 0.9 %collective-permute-done.8 = f32[216,128]{1,0:T(8,128)S(1)} collective-permute-done((f32[216,128]{1,0:T(8,128)S(1)}, f32[216,128]{1,0:T(8,128)S(1)}, u32[]{:S(2)}, u32[]{:S(2)}) %collective-permute-start.8) | collective-permute-done | bytes 110624 | tf_op jit(solution)/shard_map/ppermute | solution.py:353
  51.8 0.7 %add.3 = f32[216,128]{1,0:T(8,128)} add(f32[216,128]{1,0:T(8,128)S(1)} %get-tuple-element.60, f32[216,128]{1,0:T(8,128)S(1)} %collective-permute-done.8) | non-fusion elementwise | flops 27648 | bytes 331776 | tf_op jit(solution)/shard_map/add | solution.py:379
  (6 shorter events, 0.0 us)
Async XLA Ops:
  0.6 1.2 %copy-start.5 = (bf16[2,1728,128]{2,1,0:T(8,128)(2,1)S(1)}, bf16[2,1728,128]{2,1,0:T(8,128)(2,1)}, u32[]{:S(2)}) copy-start(bf16[2,1728,128]{2,1,0:T(8,128)(2,1)} %g_hbm.1) | copy-start | bytes 2654212
  1.8 0.8 %copy-start.7 = (bf16[64,144]{1,0:T(8,128)(2,1)S(1)}, bf16[64,144]{1,0:T(8,128)(2,1)}, u32[]{:S(2)}) copy-start(bf16[64,144]{1,0:T(8,128)(2,1)} %constant.18.clone.strips_hbm.strips) | copy-start | bytes 55300
  2.6 0.7 %copy-start.8 = (s32[2,1728]{1,0:T(2,128)S(1)}, s32[2,1728]{1,0:T(2,128)}, u32[]{:S(2)}) copy-start(s32[2,1728]{1,0:T(2,128)} %act_hbm.1) | copy-start | bytes 41476
  3.3 0.7 %copy-start.9 = (s32[2,6]{1,0:T(2,128)S(1)}, s32[2,6]{1,0:T(2,128)}, u32[]{:S(2)}) copy-start(s32[2,6]{1,0:T(2,128)} %nb.1) | copy-start | bytes 148
  4.0 8.3 %copy-start.10 = (bf16[1296,256]{1,0:T(8,128)(2,1)S(1)}, bf16[1296,256]{1,0:T(8,128)(2,1)}, u32[]{:S(2)}) copy-start(bf16[1296,256]{1,0:T(8,128)(2,1)} %constant.19.clone.shift) | copy-start | bytes 1990660
  5.5 2.2 %collective-permute-start = (bf16[560,256]{1,0:T(8,128)(2,1)S(1)}, bf16[560,256]{1,0:T(8,128)(2,1)S(1)}, u32[]{:S(2)}, u32[]{:S(2)}) collective-permute-start(bf16[560,256]{1,0:T(8,128)(2,1)S(1)} %get-tuple-element.32.own), channel_id=1, source_target_pairs={{0,1},{1,0},{2,3},{3,2},{4,5},{5,4},{6,7},{7,6},{8,9},{9,8},{10,11... | collective-permute-start | bytes 860168 | tf_op jit(solution)/shard_map/ppermute | solution.py:353
  6.0 1.2 %copy-start.4 = (bf16[2,1728,128]{2,1,0:T(8,128)(2,1)S(1)}, bf16[2,1728,128]{2,1,0:T(8,128)(2,1)}, u32[]{:S(2)}) copy-start(bf16[2,1728,128]{2,1,0:T(8,128)(2,1)} %f.1) | copy-start | bytes 2654212
  7.8 10.1 %collective-permute-start.1 = (bf16[416,256]{1,0:T(8,128)(2,1)S(1)}, bf16[416,256]{1,0:T(8,128)(2,1)S(1)}, u32[]{:S(2)}, u32[]{:S(2)}) collective-permute-start(bf16[416,256]{1,0:T(8,128)(2,1)S(1)} %pad_maximum_fusion), channel_id=1, source_target_pairs={{0,2},{2,4},{4,6},{6,8},{8,10},{10,12},{12,14},{3,1},{5,3},{7,5},{... | collective-permute-start | bytes 638984 | tf_op jit(solution)/shard_map/ppermute | solution.py:416
  16.9 3.6 %copy-start = (bf16[2,2016,1152]{2,1,0:T(8,128)(2,1)}, bf16[2,2016,1152]{2,1,0:T(8,128)(2,1)S(1)}, u32[]{:S(2)}) copy-start(bf16[2,2016,1152]{2,1,0:T(8,128)(2,1)S(1)} %get-tuple-element.40.x.x_.refs_2_) | copy-start | bytes 27869188
  17.8 2.7 %collective-permute-start.2 = (bf16[416,256]{1,0:T(8,128)(2,1)S(1)}, bf16[416,256]{1,0:T(8,128)(2,1)S(1)}, u32[]{:S(2)}, u32[]{:S(2)}) collective-permute-start(bf16[416,256]{1,0:T(8,128)(2,1)S(1)} %collective-permute-done.1.got), channel_id=1, source_target_pairs={{0,1},{1,0},{2,3},{3,2},{4,5},{5,4},{6,7},{7,6},{8,9},{9,8},{10,11... | collective-permute-start | bytes 638984 | tf_op jit(solution)/shard_map/ppermute | solution.py:353
  17.8 2.7 %copy-start.6 = (bf16[672,224]{1,0:T(8,128)(2,1)S(1)}, bf16[672,224]{1,0:T(8,128)(2,1)}, u32[]{:S(2)}) copy-start(bf16[672,224]{1,0:T(8,128)(2,1)} %constant.20.clone.bands) | copy-start | bytes 903172
  20.5 10.5 %copy-start.3 = (bf16[27,128,128]{2,1,0:T(8,128)(2,1)S(1)}, bf16[27,128,128]{2,1,0:T(8,128)(2,1)}, u32[]{:S(2)}) copy-start(bf16[27,128,128]{2,1,0:T(8,128)(2,1)} %refs_1_.1) | copy-start | bytes 2654212
  23.0 2.8 %collective-permute-start.3 = (f32[8,216,128]{2,1,0:T(8,128)}, f32[8,216,128]{2,1,0:T(8,128)}, u32[]{:S(2)}, u32[]{:S(2)}) collective-permute-start(f32[8,216,128]{2,1,0:T(8,128)} %get-tuple-element.43), channel_id=1, source_target_pairs={{0,1},{1,0},{2,3},{3,2},{4,5},{5,4},{6,7},{7,6},{8,9},{9,8},{10,11... | collective-permute-start | bytes 2654216 | tf_op jit(solution)/shard_map/ppermute | solution.py:353
  27.1 11.5 %collective-permute-start.5 = (f32[2,2,112,128]{3,2,1,0:T(8,128)S(1)}, f32[2,2,112,128]{3,2,1,0:T(8,128)S(1)}, u32[]{:S(2)}, u32[]{:S(2)}) collective-permute-start(f32[2,2,112,128]{3,2,1,0:T(8,128)S(1)} %get-tuple-element.48), channel_id=1, source_target_pairs={{0,4},{2,6},{4,0},{6,2},{8,12},{10,14},{12,8},{14,10},{1,5},{3,7},... | collective-permute-start | bytes 688136 | tf_op jit(solution)/shard_map/ppermute | solution.py:353
  28.7 9.8 %collective-permute-start.4 = (f32[2,2,104,128]{3,2,1,0:T(8,128)S(1)}, f32[2,2,104,128]{3,2,1,0:T(8,128)S(1)}, u32[]{:S(2)}, u32[]{:S(2)}) collective-permute-start(f32[2,2,104,128]{3,2,1,0:T(8,128)S(1)} %get-tuple-element.47), channel_id=1, source_target_pairs={{0,2},{2,0},{4,6},{6,4},{8,10},{10,8},{12,14},{14,12},{1,3},{3,1},... | collective-permute-start | bytes 638984 | tf_op jit(solution)/shard_map/ppermute | solution.py:353
  31.0 3.6 %copy-start.1 = (bf16[2,2016,1152]{2,1,0:T(8,128)(2,1)S(1)}, bf16[2,2016,1152]{2,1,0:T(8,128)(2,1)}, u32[]{:S(2)}) copy-start(bf16[2,2016,1152]{2,1,0:T(8,128)(2,1)} %copy-done) | copy-start | bytes 27869188
  34.6 12.3 %copy-start.2 = (bf16[2,2016,1152]{2,1,0:T(8,128)(2,1)S(1)}, bf16[2,2016,1152]{2,1,0:T(8,128)(2,1)}, u32[]{:S(2)}) copy-start(bf16[2,2016,1152]{2,1,0:T(8,128)(2,1)} %copy-done) | copy-start | bytes 27869188
  39.2 4.9 %collective-permute-start.7 = (f32[2,112,128]{2,1,0:T(8,128)S(1)}, f32[2,112,128]{2,1,0:T(8,128)S(1)}, u32[]{:S(2)}, u32[]{:S(2)}) collective-permute-start(f32[2,112,128]{2,1,0:T(8,128)S(1)} %get-tuple-element.56), channel_id=1, source_target_pairs={{0,2},{2,0},{4,6},{6,4},{8,10},{10,8},{12,14},{14,12},{1,3},{3,1},... | collective-permute-start | bytes 344072 | tf_op jit(solution)/shard_map/ppermute | solution.py:353
  39.2 4.8 %collective-permute-start.6 = (f32[2,104,128]{2,1,0:T(8,128)S(1)}, f32[2,104,128]{2,1,0:T(8,128)S(1)}, u32[]{:S(2)}, u32[]{:S(2)}) collective-permute-start(f32[2,104,128]{2,1,0:T(8,128)S(1)} %get-tuple-element.54), channel_id=1, source_target_pairs={{0,4},{2,6},{4,0},{6,2},{8,12},{10,14},{12,8},{14,10},{1,5},{3,7},... | collective-permute-start | bytes 319496 | tf_op jit(solution)/shard_map/ppermute | solution.py:353
  44.7 7.1 %collective-permute-start.8 = (f32[216,128]{1,0:T(8,128)S(1)}, f32[216,128]{1,0:T(8,128)S(1)}, u32[]{:S(2)}, u32[]{:S(2)}) collective-permute-start(f32[216,128]{1,0:T(8,128)S(1)} %get-tuple-element.57), channel_id=1, source_target_pairs={{0,8},{2,10},{4,12},{6,14},{8,0},{10,2},{12,4},{14,6},{1,9},{3,11}... | collective-permute-start | bytes 331784 | tf_op jit(solution)/shard_map/ppermute | solution.py:353

commit v2 on v1

--- a/solution.py
+++ b/solution.py
@@ -12,8 +12,8 @@
 EXT = BSIDE + 2
 C = 128
 KROWS = 256
+CUT = 112
 MINE = PLANE + 208
-LIMIT = 16 * 2**20
 BF = jnp.bfloat16
 F32 = jnp.float32
 
@@ -88,24 +88,29 @@
         out[pl.ds(n, C), :] = dot(jnp.concatenate(cols, axis=1), ones).astype(BF)
 
 
-def prep_kernel(sub, nb, act_hbm, strips_hbm, g_hbm, gm, message, mine, mask, act, strips, g, sem):
+def prep_kernel(sub, nb_hbm, act_hbm, strips_hbm, g_hbm, gm, message, mine, mask, strips, nb, act, g, sem):
     loads = [
         pltpu.make_async_copy(act_hbm, act, sem.at[0]),
         pltpu.make_async_copy(strips_hbm, strips, sem.at[1]),
-        pltpu.make_async_copy(g_hbm, g, sem.at[2]),
+        pltpu.make_async_copy(nb_hbm, nb, sem.at[2]),
     ]
+    for n in range(4):
+        rows = pl.ds(n * VOX // 4, VOX // 4)
+        loads.append(pltpu.make_async_copy(g_hbm.at[:, rows], g.at[:, rows], sem.at[3 + n]))
     for load in loads:
         load.start()
     loads[0].wait()
     masks(act, mask)
+    loads[2].wait()
     a0 = per_half((nb[0, 0] >= 0).astype(F32), (nb[1, 0] >= 0).astype(F32))
     b0 = per_half((nb[0, 2] >= 0).astype(F32), (nb[1, 2] >= 0).astype(F32))
     code = (2 * a0 + b0).astype(BF)
     a0, b0 = a0.astype(BF), b0.astype(BF)
     second = jnp.full((16, 2 * C), sub[0].astype(F32), F32).astype(BF)
     loads[1].wait()
-    loads[2].wait()
     for p in range(BSIDE):
+        if p % 3 == 0:
+            loads[3 + p // 3].wait()
         rows = pl.ds(p * PLANE, PLANE)
         plane = jnp.concatenate([g[0, rows, :], g[1, rows, :]], axis=1) * mask[rows, :]
         gm[p] = plane
@@ -120,12 +125,16 @@
     mine[pl.ds(192, 16), :] = code
 
 
-def features_kernel(mask, strips, f, pad, fs):
+def features_kernel(mask, strips, f_hbm, pad, fs, f, sem):
+    load = pltpu.make_async_copy(f_hbm, f, sem)
+    load.start()
     zero = jnp.zeros((2 * PLANE, C), BF)
     edge = jnp.zeros((32, 2 * C), BF)
     for j in range(2):
         pad[j, pl.ds(0, 2 * PLANE), :] = zero
         pad[j, pl.ds(EXT * PLANE, 2 * PLANE), :] = zero
+    load.wait()
+    for j in range(2):
         pad[j, pl.ds(2 * PLANE, VOX), :] = f[j] * mask[pl.ds(0, VOX), pl.ds(j * C, C)]
     for n in range(2):
         fs[n, pl.ds(0, 32), :] = edge
@@ -298,52 +307,78 @@
     store.wait()
 
 
+def encode(ref, at, v):
+    top = jnp.maximum(jnp.max(jnp.abs(v), axis=0, keepdims=True), 1e-33)
+    e = jnp.floor(jnp.log2(top)) - 14
+    q = jnp.clip(jnp.round(v * jnp.exp2(-e)), -32767, 32767)
+    if v.shape[0] < CUT:
+        q = jnp.concatenate([q, jnp.zeros((CUT - v.shape[0], C), F32)], axis=0)
+    ref[(*at, pl.ds(0, CUT), slice(None))] = q.astype(jnp.int32).astype(jnp.int16)
+    e = jnp.broadcast_to(e, (C - CUT, C))
+    ref[(*at, pl.ds(CUT, C - CUT), slice(None))] = e.astype(jnp.int32).astype(jnp.int16)
+
+
+def decoded(ref, at, rows):
+    e = ref[(*at, pl.ds(CUT, C - CUT), slice(None))].astype(jnp.int32).astype(F32)[:1]
+    q = ref[(*at, pl.ds(0, CUT), slice(None))].astype(jnp.int32).astype(F32)
+    return (q * jnp.exp2(e))[:rows]
+
+
 def blocks_kernel(bits, keep, got, send1, keep1, send2, keep2):
-    b0, b1 = bits[0], bits[1]
-    cut = send1.shape[2]
+    b0, b1 = bits[1], bits[2]
+    rest = pl.ds(CUT, keep.shape[1] - CUT)
     for z1 in range(2):
         for n in range(2):
-            for flip, ref1, ref2 in ((0, keep1, keep2), (1, send1, send2)):
-                i = z1 * 4 + n * 2 + jnp.bitwise_xor(b0, flip)
-                ref1[z1, n] = keep[i, pl.ds(0, cut), :] + got[i, pl.ds(0, cut), :]
-                i = z1 * 4 + jnp.bitwise_xor(b1, flip) * 2 + n
-                rest = pl.ds(cut, keep.shape[1] - cut)
-                ref2[z1, n] = keep[i, rest, :] + got[i, rest, :]
+            i, k = z1 * 4 + n * 2 + 1 - b0, z1 * 4 + (1 - b1) * 2 + n
+            encode(send1, (z1, n), keep[i, pl.ds(0, CUT), :] + got[i, pl.ds(0, CUT), :])
+            encode(send2, (z1, n), keep[k, rest, :] + got[k, rest, :])
+            i, k = z1 * 4 + n * 2 + b0, z1 * 4 + b1 * 2 + n
+            keep1[z1, n] = keep[i, pl.ds(0, CUT), :] + got[i, pl.ds(0, CUT), :]
+            keep2[z1, n] = keep[k, rest, :] + got[k, rest, :]
 
 
 def halves_kernel(bits, one, got1, two, got2, send1, keep1, send2, keep2):
-    b0, b1 = bits[0], bits[1]
+    b0, b1 = bits[1], bits[2]
+    rest = two.shape[2]
     for z1 in range(2):
-        for flip, ref1, ref2 in ((0, keep1, keep2), (1, send1, send2)):
-            i, k = jnp.bitwise_xor(b1, flip), jnp.bitwise_xor(b0, flip)
-            ref1[z1] = one[z1, i] + got1[z1, i]
-            ref2[z1] = two[z1, k] + got2[z1, k]
+        encode(send1, (z1,), one[z1, 1 - b1] + decoded(got1, (z1, 1 - b1), CUT))
+        encode(send2, (z1,), two[z1, 1 - b0] + decoded(got2, (z1, 1 - b0), rest))
+        keep1[z1] = one[z1, b1] + decoded(got1, (z1, b1), CUT)
+        keep2[z1] = two[z1, b0] + decoded(got2, (z1, b0), rest)
 
 
 def last_kernel(bits, one, got1, two, got2, send, keep):
-    cut = one.shape[1]
-    for flip, ref in ((0, keep), (1, send)):
-        i = jnp.bitwise_xor(bits[2], flip)
-        ref[pl.ds(0, cut), :] = one[i] + got1[i]
-        ref[pl.ds(cut, two.shape[1]), :] = two[i] + got2[i]
+    b2 = bits[3]
+    rest = two.shape[1]
+    encode(send, (0,), one[1 - b2] + decoded(got1, (1 - b2,), CUT))
+    encode(send, (1,), two[1 - b2] + decoded(got2, (1 - b2,), rest))
+    keep[pl.ds(0, CUT), :] = one[b2] + decoded(got1, (b2,), CUT)
+    keep[pl.ds(CUT, rest), :] = two[b2] + decoded(got2, (b2,), rest)
+
+
+def sum_kernel(keep, got, out):
+    rest = keep.shape[0] - CUT
+    out[pl.ds(0, CUT), :] = keep[pl.ds(0, CUT), :] + decoded(got, (0,), CUT)
+    out[pl.ds(CUT, rest), :] = keep[pl.ds(CUT, rest), :] + decoded(got, (1,), rest)
 
 
 VMEM = pl.BlockSpec(memory_space=pltpu.MemorySpace.VMEM)
 SMEM = pl.BlockSpec(memory_space=pltpu.MemorySpace.SMEM)
 ANY = pl.BlockSpec(memory_space=pl.ANY)
 HBM = pl.BlockSpec(memory_space=pltpu.MemorySpace.HBM)
-
-
-def call(kernel, name, ins, outs, scratch=(), aliases=None, flops=0, size=0):
+FIXED = None
+
+
+def call(kernel, name, ins, outs, scratch=(), aliases=None, flops=0, size=0, limit=4):
     return pl.pallas_call(
         kernel,
         name=name,
-        out_shape=[jax.ShapeDtypeStruct(s, d) for s, d, _ in outs],
+        out_shape=[pltpu.VMEM(s, d) if o is FIXED else jax.ShapeDtypeStruct(s, d) for s, d, o in outs],
         in_specs=ins,
-        out_specs=[o for _, _, o in outs],
+        out_specs=[VMEM if o is FIXED else o for _, _, o in outs],
         scratch_shapes=list(scratch),
         input_output_aliases=aliases or {},
-        compiler_params=pltpu.CompilerParams(vmem_limit_bytes=LIMIT),
+        compiler_params=pltpu.CompilerParams(vmem_limit_bytes=limit * 2**20),
         cost_estimate=pl.CostEstimate(flops=flops, transcendentals=0, bytes_accessed=size),
     )
 
@@ -353,64 +388,73 @@
     return lax.ppermute(value, axis, pairs)
 
 
+def in_hbm(value):
+    return pltpu.with_memory_space_constraint(value, pltpu.MemorySpace.HBM)
+
+
+def in_vmem(value):
+    return pltpu.with_memory_space_constraint(value, pltpu.MemorySpace.VMEM)
+
+
 def tied(*values):
     return lax.optimization_barrier(values)
 
 
-def reduce_blocks(keep, got, fillers):
-    s = lax.axis_index("space").astype(jnp.int32)
-    bits = jnp.stack([s & 1, (s >> 1) & 1, (s >> 2) & 1])
-    rows = keep.shape[1]
-    cut = rows // 16 * 8
+def reduce_blocks(bits, keep, got, fillers):
+    rest = keep.shape[1] - CUT
 
     def sums(kernel, name, lead, *values):
-        shapes = [((*lead, cut, C), F32, VMEM)] * 2 + [((*lead, rows - cut, C), F32, VMEM)] * 2
-        return call(kernel, name, [SMEM] + [VMEM] * len(values), shapes)(bits, *values)
+        code = ((*lead, C, C), jnp.int16, VMEM)
+        shapes = [code, ((*lead, CUT, C), F32, VMEM), code, ((*lead, rest, C), F32, VMEM)]
+        return call(kernel, name, [SMEM] + [VMEM] * len(values), shapes)(bits, *(in_vmem(v) for v in values))
 
     send1, keep1, send2, keep2 = sums(blocks_kernel, "blocks", (2, 2), keep, got)
     got1, got2 = exchange(send1, "space", 1), exchange(send2, "space", 2)
     got1, got2, fill = tied(got1, got2, fillers[0](None))
     send1, keep1, send2, keep2 = sums(halves_kernel, "halves", (2,), keep1, got1, keep2, got2)
     got1, got2 = exchange(send1, "space", 2), exchange(send2, "space", 1)
-    send, keep = call(last_kernel, "last", [SMEM] + [VMEM] * 4, [((rows, C), F32, VMEM)] * 2)(
-        bits, keep1, got1, keep2, got2
-    )
+    send, keep = call(
+        last_kernel, "last", [SMEM] + [VMEM] * 4, [((2, C, C), jnp.int16, VMEM), ((CUT + rest, C), F32, VMEM)]
+    )(bits, keep1, got1, keep2, got2)
     got, fill = tied(exchange(send, "space", 4), fillers[1](fill))
-    return keep + got, fill
+    return call(sum_kernel, "sum", [VMEM] * 2, [((CUT + rest, C), F32, VMEM)])(keep, got)[0], fill
 
 
 def on_device(features, out_grad, weight, neighbours, active):
     layers = lax.axis_size("space")
-    sub = lax.axis_index("sub").astype(jnp.int32).reshape(1)
+    core, layer = lax.axis_index("sub").astype(jnp.int32), lax.axis_index("space").astype(jnp.int32)
+    sub = jnp.stack([core, layer & 1, (layer >> 1) & 1, (layer >> 2) & 1])
     strips, shift, bands = jnp.asarray(strip_matrix()), jnp.asarray(shift_matrix()), jnp.asarray(band_matrix())
 
-    gm, own, mine, mask = call(
+    gm, own, mine, mask, strips = call(
         prep_kernel,
         "prep",
-        [SMEM] * 2 + [HBM] * 3,
+        [SMEM] + [HBM] * 4,
         [
             ((BSIDE, PLANE, 2 * C), BF, VMEM),
             ((MINE + 208, 2 * C), BF, VMEM),
             ((208, 2 * C), BF, VMEM),
             ((14 * C, 2 * C), BF, VMEM),
+            ((64, PLANE), BF, VMEM),
         ],
         [
+            pltpu.SMEM((2, 6), jnp.int32),
             pltpu.VMEM((2, VOX), jnp.int32),
-            pltpu.VMEM((64, PLANE), BF),
             pltpu.VMEM((2, VOX, C), BF),
-            pltpu.SemaphoreType.DMA((3,)),
+            pltpu.SemaphoreType.DMA((7,)),
         ],
-    )(sub, neighbours, active, strips, out_grad)
-
-    other = exchange(own, "sub", 1)
+    )(sub, in_hbm(neighbours), in_hbm(active), in_hbm(strips), in_hbm(out_grad))
+
+    other, mask = tied(exchange(own, "sub", 1), mask)
     pad, fs = call(
         features_kernel,
         "features",
-        [VMEM] * 3,
+        [VMEM] * 2 + [HBM],
         [((2, (EXT + 2) * PLANE, C), BF, VMEM), ((2, (EXT + 2) * 16, 2 * C), BF, VMEM)],
+        [pltpu.VMEM((2, VOX, C), BF), pltpu.SemaphoreType.DMA],
         flops=10**7,
         size=10**6,
-    )(mask, strips, features)
+    )(mask, strips, in_hbm(features))
 
     ways = [(2 * i, 2 * i + 2) for i in range(layers - 1)] + [(2 * i + 3, 2 * i + 1) for i in range(layers - 1)]
     got = lax.ppermute(jnp.concatenate([mine, other[MINE:]], axis=0), ("space", "sub"), ways)
@@ -421,10 +465,11 @@
         first_kernel,
         "first",
         [VMEM] * 5,
-        [((2, EXT * PLANE, 9 * C), BF, VMEM), ((3 * C, 9 * C), F32, VMEM)],
+        [((2, EXT * PLANE, 9 * C), BF, FIXED), ((3 * C, 9 * C), F32, VMEM)],
         [pltpu.VMEM(kop_shape, BF)],
         flops=2 * work,
         size=8 * 2**20,
+        limit=6,
     )(shift, gm, own, other, pad)
     got, acc = tied(got, acc)
     got2 = exchange(got, "sub", 1)
@@ -435,7 +480,7 @@
         [((3 * C, 9 * C), F32, VMEM)],
         flops=work,
         size=4 * 2**20,
-    )(pad, x, acc)
+    )(pad, in_vmem(x), acc)
 
     size = 27 * C // (2 * layers)
     custom = layers == 8
@@ -444,7 +489,7 @@
         tilt_kernel,
         "tilt",
         [SMEM] + [VMEM] * 6,
-        [(rows, F32, VMEM), (rows, F32, VMEM), ((2, 2, EXT * 16, 3 * C), BF, VMEM)],
+        [(rows, F32, FIXED), (rows, F32, FIXED), ((2, 2, EXT * 16, 3 * C), BF, VMEM)],
         [pltpu.VMEM((2, EXT * 16, 2 * C), BF), pltpu.VMEM((2, 3 * C, 3 * C), F32)],
         flops=work // 4,
         size=4 * 2**20,
@@ -470,14 +515,15 @@
                 aliases={} if fresh else {4: 0},
                 flops=work,
                 size=4 * 2**20,
-            )(mask, weight, x, zs, *(() if fresh else (before,)))[0]
+                limit=10,
+            )(mask, weight, in_vmem(x), zs, *(() if fresh else (before,)))[0]
 
         return run
 
     if custom:
         got = exchange(send, "sub", 1)
         got, zs = tied(got, zs)
-        weight_grad, input_grad = reduce_blocks(keep, got, [dgrad(0), dgrad(1)])
+        weight_grad, input_grad = reduce_blocks(sub, keep, got, [dgrad(0), dgrad(1)])
     else:
         even = jnp.where(sub[0] == 0, keep, send)
         odd = jnp.where(sub[0] == 0, send, keep)

time: 52.8 us -> 45.2 us (0.86)
  local copies, waits for them, and re-layouts: 8.55 us -> 0.03 us
  Pallas kernels: 21.7 us -> 23.7 us
  waiting for transfers between devices: 8.73 us -> 7.56 us
  starting transfers between devices: 11.9 us -> 12.8 us
  other arithmetic: 0.75 us -> 0.09 us
    unnamed x22 -> x6, local copies, waits for them, and re-layouts: 8.54 us -> 0.02 us
    pallas_call x7 -> x8, Pallas kernels: 11.7 us -> 13.6 us  [the longest x1 4.68 us: on_device(): call(first_kernel, 'first', [VMEM] * 5, [((2, EXT * PLANE, 9 * C), BF, FI...]
    ppermute x1, waiting for transfers between devices: 0.91 us -> 0.01 us  [on_device(): lax.ppermute(jnp.concatenate([mine, other[MINE:]], axis=0), ('space', 'su...]
    add x1 -> x0, other arithmetic: 0.66 us -> none  [reduce_blocks(): return (keep + got, fill)]
    ppermute x8, starting transfers between devices: 7.44 us -> 8.01 us  [exchange(): return lax.ppermute(value, axis, pairs)]
  transfers between devices with their start and end apart: 9 -> 9, of which waited for: 5 -> 5; matrix products, arithmetic and copies ran while one was open for 0% -> 0% of each run, Pallas kernels for 29% -> 36%
where the time goes in v2:
time: 45.2 us; the launch traced here: 45 us
  Pallas kernels  23.7 us (52%)
  starting transfers between devices  12.8 us (28%)
  waiting for transfers between devices  7.56 us (17%)
  between operations  0.81 us (2%)
    ppermute x8, starting transfers between devices, exchange(): return lax.ppermute(value, axis, pairs)  8.01 us
    pallas_call x2, Pallas kernels, run(): call((lambda m, w, x_, z, *refs: dgrad_kernel(j, m, w, x_, z, None, *refs...  7.8 us
    ppermute x8, waiting for transfers between devices, exchange(): return lax.ppermute(value, axis, pairs)  7.56 us
    ppermute x1, starting transfers between devices, on_device(): lax.ppermute(jnp.concatenate([mine, other[MINE:]], axis=0), ('space', 'su...  4.82 us
    pallas_call x1, Pallas kernels, on_device(): call(first_kernel, 'first', [VMEM] * 5, [((2, EXT * PLANE, 9 * C), BF, FI...  4.68 us
    pallas_call x1, Pallas kernels, on_device(): call(prep_kernel, 'prep', [SMEM] + [HBM] * 4, [((BSIDE, PLANE, 2 * C), BF...  2.5 us
    pallas_call x1, Pallas kernels, on_device(): call(second_kernel, 'second', [VMEM, VMEM, VMEM], [((3 * C, 9 * C), F32,...  2.26 us
    pallas_call x1, Pallas kernels, on_device(): call(tilt_kernel, 'tilt', [SMEM] + [VMEM] * 6, [(rows, F32, FIXED), (rows...  2.13 us
  transfers between devices with their start and end apart: 9, of which 5 were waited for; matrix products, arithmetic and copies ran while one was open for 0% of the time, Pallas kernels for 36%

profile of v2, /device:TPU:0, one launch (start us, length us, event | category | flops | bytes accessed | tf_op | source)
XLA Modules:
  0.0 45.0 jit_solution(11130240155363827410)
XLA Ops:
  0.6 0.0 copy-start.2
  0.6 0.1 pad_add_fusion.sub.bits
  0.7 2.5 %prep.1 = (bf16[12,144,256]{2,1,0:T(8,128)(2,1)S(1)}, bf16[560,256]{1,0:T(8,128)(2,1)S(1)}, bf16[208,256]{1,0:T(8,128)(2,1)S(1)}, bf16[1792,256]{1,0:T(8,128)(2,1)S(1)}, bf16[64,144]{1,0:T(8,128)(2,1)S(1)}) custom-call(s32[4]{0:T(128)S(1)} %pad_add_fusion.sub.bits, s32[2,6]{1,0:T(2,128)} %nb_hbm.1, s32[2,1728]{1,0:T(2,128)} %act_hbm.1, ...), custom_call_target="tpu_custom_call" | custom-call | tf_op jit(solution)/shard_map/prep/pallas_call | solution.py:429
  3.2 0.5 %collective-permute-start = (bf16[560,256]{1,0:T(8,128)(2,1)S(1)}, bf16[560,256]{1,0:T(8,128)(2,1)S(1)}, u32[]{:S(2)}, u32[]{:S(2)}) collective-permute-start(bf16[560,256]{1,0:T(8,128)(2,1)S(1)} %get-tuple-element.35.own), channel_id=1, source_target_pairs={{0,1},{1,0},{2,3},{3,2},{4,5},{5,4},{6,7},{7,6},{8,9},{9,8},{10,11... | collective-permute-start | bytes 860168 | tf_op jit(solution)/shard_map/ppermute | solution.py:388
  3.8 1.2 %collective-permute-done.other = bf16[560,256]{1,0:T(8,128)(2,1)S(1)} collective-permute-done((bf16[560,256]{1,0:T(8,128)(2,1)S(1)}, bf16[560,256]{1,0:T(8,128)(2,1)S(1)}, u32[]{:S(2)}, u32[]{:S(2)}) %collective-permute-start) | collective-permute-done | bytes 286752 | tf_op jit(solution)/shard_map/ppermute | solution.py:388
  5.0 4.8 %collective-permute-start.1 = (bf16[416,256]{1,0:T(8,128)(2,1)S(1)}, bf16[416,256]{1,0:T(8,128)(2,1)S(1)}, u32[]{:S(2)}, u32[]{:S(2)}) collective-permute-start(bf16[416,256]{1,0:T(8,128)(2,1)S(1)} %pad_maximum_fusion), channel_id=1, source_target_pairs={{0,2},{2,4},{4,6},{6,8},{8,10},{10,12},{12,14},{3,1},{5,3},{7,5},{... | collective-permute-start | bytes 638984 | tf_op jit(solution)/shard_map/ppermute | solution.py:460
  9.8 1.6 %features.1 = (bf16[2,2304,128]{2,1,0:T(8,128)(2,1)S(1)}, bf16[2,256,256]{2,1,0:T(8,128)(2,1)S(1)}) custom-call(bf16[1792,256]{1,0:T(8,128)(2,1)S(1)} %get-tuple-element.40.mask.m.refs_0_, bf16[64,144]{1,0:T(8,128)(2,1)S(1)} %get-tuple-element.41.strips, bf16[2,1728,128]{2,1,0:T(8,128)(2,1)} %f_hbm.1), custom_call_target="tpu_custom_call" | custom-call | flops 10000000 | bytes 1000000 | tf_op jit(solution)/shard_map/features/pallas_call | solution.py:449
  11.4 0.0 copy-done.2
  11.5 4.7 %first.1 = (bf16[2,2016,1152]{2,1,0:T(8,128)(2,1)S(1)}, f32[384,1152]{1,0:T(8,128)S(1)}) custom-call(bf16[1296,256]{1,0:T(8,128)(2,1)S(1)} %copy-done.2, bf16[12,144,256]{2,1,0:T(8,128)(2,1)S(1)} %get-tuple-element.39.gm, bf16[560,256]{1,0:T(8,128)(2,1)S(1)} %get-tuple-element.35.own, bf16[560,256]{1,0:T(8,128)(2,1)S(1)} %collective-permute-done.other, ...), custom_call_target="tpu_custom_call" | custom-call | flops 3567255552 | bytes 8388608 | tf_op jit(solution)/shard_map/first/pallas_call | solution.py:464
  16.1 0.0 collective-permute-done.1.got
  16.2 0.1 collective-permute-start.2
  16.2 0.0 copy-start.1
  16.3 2.3 %second.1.acc = f32[384,1152]{1,0:T(8,128)S(1)} custom-call(bf16[2,2304,128]{2,1,0:T(8,128)(2,1)S(1)} %get-tuple-element.42.pad, bf16[2,2016,1152]{2,1,0:T(8,128)(2,1)S(1)} %get-tuple-element.46.x.x_.refs_2_, f32[384,1152]{1,0:T(8,128)S(1)} %get-tuple-element.47.before), custom_call_target="tpu_custom_call" | custom-call | flops 1783627776 | bytes 4194304 | tf_op jit(solution)/shard_map/second/pallas_call | solution.py:476
  18.5 0.0 collective-permute-done.2.got2
  18.5 0.0 copy-done.1
  18.5 0.0 copy-start
  18.5 2.1 %tilt.1 = (f32[8,216,128]{2,1,0:T(8,128)S(1)}, f32[8,216,128]{2,1,0:T(8,128)S(1)}, bf16[2,2,224,384]{3,2,1,0:T(8,128)(2,1)S(1)}) custom-call(s32[4]{0:T(128)S(1)} %pad_add_fusion.sub.bits, bf16[560,256]{1,0:T(8,128)(2,1)S(1)} %get-tuple-element.35.own, bf16[416,256]{1,0:T(8,128)(2,1)S(1)} %collective-permute-done.1.got, ...), custom_call_target="tpu_custom_call" | custom-call | flops 445906944 | bytes 4194304 | tf_op jit(solution)/shard_map/tilt/pallas_call | solution.py:488
  20.7 0.6 %collective-permute-start.3 = (f32[8,216,128]{2,1,0:T(8,128)S(1)}, f32[8,216,128]{2,1,0:T(8,128)S(1)}, u32[]{:S(2)}, u32[]{:S(2)}) collective-permute-start(f32[8,216,128]{2,1,0:T(8,128)S(1)} %get-tuple-element.49), channel_id=1, source_target_pairs={{0,1},{1,0},{2,3},{3,2},{4,5},{5,4},{6,7},{7,6},{8,9},{9,8},{10,11... | collective-permute-start | bytes 2654216 | tf_op jit(solution)/shard_map/ppermute | solution.py:388
  21.3 2.1 %collective-permute-done.3.got = f32[8,216,128]{2,1,0:T(8,128)S(1)} collective-permute-done((f32[8,216,128]{2,1,0:T(8,128)S(1)}, f32[8,216,128]{2,1,0:T(8,128)S(1)}, u32[]{:S(2)}, u32[]{:S(2)}) %collective-permute-start.3) | collective-permute-done | bytes 884768 | tf_op jit(solution)/shard_map/ppermute | solution.py:388
  23.3 0.7 %blocks.1 = (s16[2,2,128,128]{3,2,1,0:T(8,128)(2,1)S(1)}, f32[2,2,112,128]{3,2,1,0:T(8,128)S(1)}, s16[2,2,128,128]{3,2,1,0:T(8,128)(2,1)S(1)}, f32[2,2,104,128]{3,2,1,0:T(8,128)S(1)}) custom-call(s32[4]{0:T(128)S(1)} %pad_add_fusion.sub.bits, f32[8,216,128]{2,1,0:T(8,128)S(1)} %get-tuple-element.48.keep, f32[8,216,128]{2,1,0:T(8,128)S(1)} %collective-permute-done.3.got), custom_call_target="tpu_custom_call" | custom-call | tf_op jit(solution)/shard_map/blocks/pallas_call | solution.py:409
  24.1 1.7 %collective-permute-start.4 = (s16[2,2,128,128]{3,2,1,0:T(8,128)(2,1)S(1)}, s16[2,2,128,128]{3,2,1,0:T(8,128)(2,1)S(1)}, u32[]{:S(2)}, u32[]{:S(2)}) collective-permute-start(s16[2,2,128,128]{3,2,1,0:T(8,128)(2,1)S(1)} %get-tuple-element.53), channel_id=1, source_target_pairs={{0,2},{2,0},{4,6},{6,4},{8,10},{10,8},{12,14},{14,12},{1,3},{3,1},... | collective-permute-start | bytes 393224 | tf_op jit(solution)/shard_map/ppermute | solution.py:388
  25.8 1.6 %collective-permute-start.5 = (s16[2,2,128,128]{3,2,1,0:T(8,128)(2,1)S(1)}, s16[2,2,128,128]{3,2,1,0:T(8,128)(2,1)S(1)}, u32[]{:S(2)}, u32[]{:S(2)}) collective-permute-start(s16[2,2,128,128]{3,2,1,0:T(8,128)(2,1)S(1)} %get-tuple-element.54), channel_id=1, source_target_pairs={{0,4},{2,6},{4,0},{6,2},{8,12},{10,14},{12,8},{14,10},{1,5},{3,7},... | collective-permute-start | bytes 393224 | tf_op jit(solution)/shard_map/ppermute | solution.py:388
  27.4 0.0 copy-done
  27.4 3.9 %dgrad.2.refs_4_ = bf16[2,1728,128]{2,1,0:T(8,128)(2,1)} custom-call(bf16[1792,256]{1,0:T(8,128)(2,1)S(1)} %get-tuple-element.40.mask.m.refs_0_, bf16[27,128,128]{2,1,0:T(8,128)(2,1)S(1)} %copy-done, bf16[2,2016,1152]{2,1,0:T(8,128)(2,1)S(1)} %get-tuple-element.46.x.x_.refs_2_, bf16[2,2,224,384]{3,2,1,0:T(8,128)(2,1)S(1)} %get-tuple-element.55.z.refs_3_), custom_call_target="tpu_custom_call" | custom-call | flops 1783627776 | bytes 4194304 | tf_op jit(solution)/shard_map/dgrad/pallas_call | solution.py:501
  31.3 0.0 collective-permute-done.4.got1
  31.3 0.0 collective-permute-done.5.got2
  31.3 0.7 %halves.1 = (s16[2,128,128]{2,1,0:T(8,128)(2,1)S(1)}, f32[2,112,128]{2,1,0:T(8,128)S(1)}, s16[2,128,128]{2,1,0:T(8,128)(2,1)S(1)}, f32[2,104,128]{2,1,0:T(8,128)S(1)}) custom-call(s32[4]{0:T(128)S(1)} %pad_add_fusion.sub.bits, f32[2,2,112,128]{3,2,1,0:T(8,128)S(1)} %get-tuple-element.52.one, s16[2,2,128,128]{3,2,1,0:T(8,128)(2,1)S(1)} %collective-permute-done.4.got1, ...), custom_call_target="tpu_custom_call" | custom-call | tf_op jit(solution)/shard_map/halves/pallas_call | solution.py:409
  32.0 1.6 %collective-permute-start.6 = (s16[2,128,128]{2,1,0:T(8,128)(2,1)S(1)}, s16[2,128,128]{2,1,0:T(8,128)(2,1)S(1)}, u32[]{:S(2)}, u32[]{:S(2)}) collective-permute-start(s16[2,128,128]{2,1,0:T(8,128)(2,1)S(1)} %get-tuple-element.60), channel_id=1, source_target_pairs={{0,4},{2,6},{4,0},{6,2},{8,12},{10,14},{12,8},{14,10},{1,5},{3,7},... | collective-permute-start | bytes 196616 | tf_op jit(solution)/shard_map/ppermute | solution.py:388
  33.6 0.4 collective-permute-start.7
  34.0 2.4 %collective-permute-done.6.got1 = s16[2,128,128]{2,1,0:T(8,128)(2,1)S(1)} collective-permute-done((s16[2,128,128]{2,1,0:T(8,128)(2,1)S(1)}, s16[2,128,128]{2,1,0:T(8,128)(2,1)S(1)}, u32[]{:S(2)}, u32[]{:S(2)}) %collective-permute-start.6) | collective-permute-done | bytes 65568 | tf_op jit(solution)/shard_map/ppermute | solution.py:388
  36.3 1.5 %collective-permute-done.7.got2 = s16[2,128,128]{2,1,0:T(8,128)(2,1)S(1)} collective-permute-done((s16[2,128,128]{2,1,0:T(8,128)(2,1)S(1)}, s16[2,128,128]{2,1,0:T(8,128)(2,1)S(1)}, u32[]{:S(2)}, u32[]{:S(2)}) %collective-permute-start.7) | collective-permute-done | bytes 65568 | tf_op jit(solution)/shard_map/ppermute | solution.py:388
  37.9 0.6 %last.1 = (s16[2,128,128]{2,1,0:T(8,128)(2,1)S(1)}, f32[216,128]{1,0:T(8,128)S(1)}) custom-call(s32[4]{0:T(128)S(1)} %pad_add_fusion.sub.bits, f32[2,112,128]{2,1,0:T(8,128)S(1)} %get-tuple-element.59.one, s16[2,128,128]{2,1,0:T(8,128)(2,1)S(1)} %collective-permute-done.6.got1, f32[2,104,128]{2,1,0:T(8,128)S(1)} %get-tuple-element.61.two, ...), custom_call_target="tpu_custom_call" | custom-call | tf_op jit(solution)/shard_map/last/pallas_call | solution.py:416
  38.5 1.6 %collective-permute-start.8 = (s16[2,128,128]{2,1,0:T(8,128)(2,1)S(1)}, s16[2,128,128]{2,1,0:T(8,128)(2,1)S(1)}, u32[]{:S(2)}, u32[]{:S(2)}) collective-permute-start(s16[2,128,128]{2,1,0:T(8,128)(2,1)S(1)} %get-tuple-element.63), channel_id=1, source_target_pairs={{0,8},{2,10},{4,12},{6,14},{8,0},{10,2},{12,4},{14,6},{1,9},{3,11}... | collective-permute-start | bytes 196616 | tf_op jit(solution)/shard_map/ppermute | solution.py:388
  40.0 3.9 %dgrad.3 = bf16[2,1728,128]{2,1,0:T(8,128)(2,1)} custom-call(bf16[1792,256]{1,0:T(8,128)(2,1)S(1)} %get-tuple-element.40.mask.m.refs_0_, bf16[27,128,128]{2,1,0:T(8,128)(2,1)S(1)} %copy-done, bf16[2,2016,1152]{2,1,0:T(8,128)(2,1)S(1)} %get-tuple-element.46.x.x_.refs_2_, ...), custom_call_target="tpu_custom_call", output_to_operand_aliasing={{}: (4, {})} | custom-call | flops 1783627776 | bytes 4194304 | tf_op jit(solution)/shard_map/dgrad/pallas_call | solution.py:501
  44.0 0.4 collective-permute-done.8.got
  44.3 0.7 %sum.1 = f32[216,128]{1,0:T(8,128)} custom-call(f32[216,128]{1,0:T(8,128)S(1)} %get-tuple-element.66.keep, s16[2,128,128]{2,1,0:T(8,128)(2,1)S(1)} %collective-permute-done.8.got), custom_call_target="tpu_custom_call" | custom-call | tf_op jit(solution)/shard_map/sum/pallas_call | solution.py:420
  (2 shorter events, 0.0 us)
Async XLA Ops:
  0.6 10.8 %copy-start.2 = (bf16[1296,256]{1,0:T(8,128)(2,1)S(1)}, bf16[1296,256]{1,0:T(8,128)(2,1)}, u32[]{:S(2)}) copy-start(bf16[1296,256]{1,0:T(8,128)(2,1)} %constant.19.clone.shift) | copy-start | bytes 1990660
  3.2 1.7 %collective-permute-start = (bf16[560,256]{1,0:T(8,128)(2,1)S(1)}, bf16[560,256]{1,0:T(8,128)(2,1)S(1)}, u32[]{:S(2)}, u32[]{:S(2)}) collective-permute-start(bf16[560,256]{1,0:T(8,128)(2,1)S(1)} %get-tuple-element.35.own), channel_id=1, source_target_pairs={{0,1},{1,0},{2,3},{3,2},{4,5},{5,4},{6,7},{7,6},{8,9},{9,8},{10,11... | collective-permute-start | bytes 860168 | tf_op jit(solution)/shard_map/ppermute | solution.py:388
  5.0 11.2 %collective-permute-start.1 = (bf16[416,256]{1,0:T(8,128)(2,1)S(1)}, bf16[416,256]{1,0:T(8,128)(2,1)S(1)}, u32[]{:S(2)}, u32[]{:S(2)}) collective-permute-start(bf16[416,256]{1,0:T(8,128)(2,1)S(1)} %pad_maximum_fusion), channel_id=1, source_target_pairs={{0,2},{2,4},{4,6},{6,8},{8,10},{10,12},{12,14},{3,1},{5,3},{7,5},{... | collective-permute-start | bytes 638984 | tf_op jit(solution)/shard_map/ppermute | solution.py:460
  16.2 2.4 %collective-permute-start.2 = (bf16[416,256]{1,0:T(8,128)(2,1)S(1)}, bf16[416,256]{1,0:T(8,128)(2,1)S(1)}, u32[]{:S(2)}, u32[]{:S(2)}) collective-permute-start(bf16[416,256]{1,0:T(8,128)(2,1)S(1)} %collective-permute-done.1.got), channel_id=1, source_target_pairs={{0,1},{1,0},{2,3},{3,2},{4,5},{5,4},{6,7},{7,6},{8,9},{9,8},{10,11... | collective-permute-start | bytes 638984 | tf_op jit(solution)/shard_map/ppermute | solution.py:388
  16.2 2.3 %copy-start.1 = (bf16[672,224]{1,0:T(8,128)(2,1)S(1)}, bf16[672,224]{1,0:T(8,128)(2,1)}, u32[]{:S(2)}) copy-start(bf16[672,224]{1,0:T(8,128)(2,1)} %constant.20.clone.bands) | copy-start | bytes 903172
  18.5 8.9 %copy-start = (bf16[27,128,128]{2,1,0:T(8,128)(2,1)S(1)}, bf16[27,128,128]{2,1,0:T(8,128)(2,1)}, u32[]{:S(2)}) copy-start(bf16[27,128,128]{2,1,0:T(8,128)(2,1)} %refs_1_.1) | copy-start | bytes 2654212
  20.7 2.6 %collective-permute-start.3 = (f32[8,216,128]{2,1,0:T(8,128)S(1)}, f32[8,216,128]{2,1,0:T(8,128)S(1)}, u32[]{:S(2)}, u32[]{:S(2)}) collective-permute-start(f32[8,216,128]{2,1,0:T(8,128)S(1)} %get-tuple-element.49), channel_id=1, source_target_pairs={{0,1},{1,0},{2,3},{3,2},{4,5},{5,4},{6,7},{7,6},{8,9},{9,8},{10,11... | collective-permute-start | bytes 2654216 | tf_op jit(solution)/shard_map/ppermute | solution.py:388
  24.1 7.2 %collective-permute-start.4 = (s16[2,2,128,128]{3,2,1,0:T(8,128)(2,1)S(1)}, s16[2,2,128,128]{3,2,1,0:T(8,128)(2,1)S(1)}, u32[]{:S(2)}, u32[]{:S(2)}) collective-permute-start(s16[2,2,128,128]{3,2,1,0:T(8,128)(2,1)S(1)} %get-tuple-element.53), channel_id=1, source_target_pairs={{0,2},{2,0},{4,6},{6,4},{8,10},{10,8},{12,14},{14,12},{1,3},{3,1},... | collective-permute-start | bytes 393224 | tf_op jit(solution)/shard_map/ppermute | solution.py:388
  25.8 5.5 %collective-permute-start.5 = (s16[2,2,128,128]{3,2,1,0:T(8,128)(2,1)S(1)}, s16[2,2,128,128]{3,2,1,0:T(8,128)(2,1)S(1)}, u32[]{:S(2)}, u32[]{:S(2)}) collective-permute-start(s16[2,2,128,128]{3,2,1,0:T(8,128)(2,1)S(1)} %get-tuple-element.54), channel_id=1, source_target_pairs={{0,4},{2,6},{4,0},{6,2},{8,12},{10,14},{12,8},{14,10},{1,5},{3,7},... | collective-permute-start | bytes 393224 | tf_op jit(solution)/shard_map/ppermute | solution.py:388
  32.0 4.3 %collective-permute-start.6 = (s16[2,128,128]{2,1,0:T(8,128)(2,1)S(1)}, s16[2,128,128]{2,1,0:T(8,128)(2,1)S(1)}, u32[]{:S(2)}, u32[]{:S(2)}) collective-permute-start(s16[2,128,128]{2,1,0:T(8,128)(2,1)S(1)} %get-tuple-element.60), channel_id=1, source_target_pairs={{0,4},{2,6},{4,0},{6,2},{8,12},{10,14},{12,8},{14,10},{1,5},{3,7},... | collective-permute-start | bytes 196616 | tf_op jit(solution)/shard_map/ppermute | solution.py:388
  33.6 4.3 %collective-permute-start.7 = (s16[2,128,128]{2,1,0:T(8,128)(2,1)S(1)}, s16[2,128,128]{2,1,0:T(8,128)(2,1)S(1)}, u32[]{:S(2)}, u32[]{:S(2)}) collective-permute-start(s16[2,128,128]{2,1,0:T(8,128)(2,1)S(1)} %get-tuple-element.62), channel_id=1, source_target_pairs={{0,2},{2,0},{4,6},{6,4},{8,10},{10,8},{12,14},{14,12},{1,3},{3,1},... | collective-permute-start | bytes 196616 | tf_op jit(solution)/shard_map/ppermute | solution.py:388
  38.5 5.8 %collective-permute-start.8 = (s16[2,128,128]{2,1,0:T(8,128)(2,1)S(1)}, s16[2,128,128]{2,1,0:T(8,128)(2,1)S(1)}, u32[]{:S(2)}, u32[]{:S(2)}) collective-permute-start(s16[2,128,128]{2,1,0:T(8,128)(2,1)S(1)} %get-tuple-element.63), channel_id=1, source_target_pairs={{0,8},{2,10},{4,12},{6,14},{8,0},{10,2},{12,4},{14,6},{1,9},{3,11}... | collective-permute-start | bytes 196616 | tf_op jit(solution)/shard_map/ppermute | solution.py:388

commit v3 on v1

--- a/solution.py
+++ b/solution.py
@@ -12,8 +12,9 @@
 EXT = BSIDE + 2
 C = 128
 KROWS = 256
+EARLY = 9
+CUT = 112
 MINE = PLANE + 208
-LIMIT = 16 * 2**20
 BF = jnp.bfloat16
 F32 = jnp.float32
 
@@ -88,24 +89,29 @@
         out[pl.ds(n, C), :] = dot(jnp.concatenate(cols, axis=1), ones).astype(BF)
 
 
-def prep_kernel(sub, nb, act_hbm, strips_hbm, g_hbm, gm, message, mine, mask, act, strips, g, sem):
+def prep_kernel(nb_hbm, act_hbm, strips_hbm, g_hbm, gm, message, mine, mask, strips, nb, act, g, sem):
     loads = [
         pltpu.make_async_copy(act_hbm, act, sem.at[0]),
         pltpu.make_async_copy(strips_hbm, strips, sem.at[1]),
-        pltpu.make_async_copy(g_hbm, g, sem.at[2]),
+        pltpu.make_async_copy(nb_hbm, nb, sem.at[2]),
     ]
+    for n in range(4):
+        rows = pl.ds(n * VOX // 4, VOX // 4)
+        loads.append(pltpu.make_async_copy(g_hbm.at[:, rows], g.at[:, rows], sem.at[3 + n]))
     for load in loads:
         load.start()
     loads[0].wait()
     masks(act, mask)
+    loads[2].wait()
     a0 = per_half((nb[0, 0] >= 0).astype(F32), (nb[1, 0] >= 0).astype(F32))
     b0 = per_half((nb[0, 2] >= 0).astype(F32), (nb[1, 2] >= 0).astype(F32))
     code = (2 * a0 + b0).astype(BF)
     a0, b0 = a0.astype(BF), b0.astype(BF)
-    second = jnp.full((16, 2 * C), sub[0].astype(F32), F32).astype(BF)
+    second = jnp.full((16, 2 * C), lax.axis_index("sub").astype(F32), F32).astype(BF)
     loads[1].wait()
-    loads[2].wait()
     for p in range(BSIDE):
+        if p % 3 == 0:
+            loads[3 + p // 3].wait()
         rows = pl.ds(p * PLANE, PLANE)
         plane = jnp.concatenate([g[0, rows, :], g[1, rows, :]], axis=1) * mask[rows, :]
         gm[p] = plane
@@ -120,12 +126,16 @@
     mine[pl.ds(192, 16), :] = code
 
 
-def features_kernel(mask, strips, f, pad, fs):
+def features_kernel(mask, strips, f_hbm, pad, fs, f, sem):
+    load = pltpu.make_async_copy(f_hbm, f, sem)
+    load.start()
     zero = jnp.zeros((2 * PLANE, C), BF)
     edge = jnp.zeros((32, 2 * C), BF)
     for j in range(2):
         pad[j, pl.ds(0, 2 * PLANE), :] = zero
         pad[j, pl.ds(EXT * PLANE, 2 * PLANE), :] = zero
+    load.wait()
+    for j in range(2):
         pad[j, pl.ds(2 * PLANE, VOX), :] = f[j] * mask[pl.ds(0, VOX), pl.ds(j * C, C)]
     for n in range(2):
         fs[n, pl.ds(0, 32), :] = edge
@@ -210,13 +220,16 @@
 def shifted(shift, kop, x, ks, first, count):
     for p in range(count):
         for n, k in enumerate(ks):
-            y = dot(shift[pl.ds(k * PLANE, PLANE), :], kop[first + p]).astype(BF)
+            if k == 4:
+                y = kop[first + p, pl.ds(0, PLANE), :]
+            else:
+                y = dot(shift[pl.ds(k * PLANE, PLANE), :], kop[first + p]).astype(BF)
             for j in range(2):
                 x[j, pl.ds(p * PLANE, PLANE), pl.ds(n * C, C)] = y[:, j * C : j * C + C]
 
 
-def stacked(ref, j, width, lanes):
-    return jnp.concatenate([ref[j, pl.ds(d * width, EXT * width), lanes] for d in range(3)], axis=1)
+def stacked(ref, j, first, count):
+    return jnp.concatenate([ref[j, pl.ds((d + first) * PLANE, count * PLANE), :] for d in range(3)], axis=1)
 
 
 def dot_rows(a, b):
@@ -226,17 +239,37 @@
 def first_kernel(shift, gm, own, other, pad, x, acc, kop):
     layer_operands(gm, own, other, kop)
     shifted(shift, kop, x, range(9), 0, EXT)
-    acc[...] = dot_rows(stacked(pad, 0, PLANE, slice(None)), x[0])
+    acc[...] = dot_rows(stacked(pad, 0, 0, EXT), x[0])
+    acc[...] += dot_rows(stacked(pad, 1, 0, EARLY), x[1, pl.ds(0, EARLY * PLANE), :])
 
 
 def second_kernel(pad, x, before, acc):
-    acc[...] = before[...] + dot_rows(stacked(pad, 1, PLANE, slice(None)), x[1])
-
-
-def tilt_kernel(sub, own, got, got2, fs, bands, acc, keep, send, zs, z, more):
+    late = EXT - EARLY
+    acc[...] = before[...] + dot_rows(stacked(pad, 1, EARLY, late), x[1, pl.ds(EARLY * PLANE, late * PLANE), :])
+
+
+def encode(ref, at, v):
+    top = jnp.maximum(jnp.max(jnp.abs(v), axis=0, keepdims=True), 1e-33)
+    e = jnp.floor(jnp.log2(top)) - 14
+    q = jnp.clip(jnp.round(v * jnp.exp2(-e)), -32767, 32767)
+    if v.shape[0] < CUT:
+        q = jnp.concatenate([q, jnp.zeros((CUT - v.shape[0], C), F32)], axis=0)
+    ref[(*at, pl.ds(0, CUT), slice(None))] = q.astype(jnp.int32).astype(jnp.int16)
+    e = jnp.broadcast_to(e, (C - CUT, C))
+    ref[(*at, pl.ds(CUT, C - CUT), slice(None))] = e.astype(jnp.int32).astype(jnp.int16)
+
+
+def decoded(ref, at, rows):
+    e = ref[(*at, pl.ds(CUT, C - CUT), slice(None))].astype(jnp.int32).astype(F32)[:1]
+    q = ref[(*at, pl.ds(0, CUT), slice(None))].astype(jnp.int32).astype(F32)
+    return (q * jnp.exp2(e))[:rows]
+
+
+def tilt_kernel(own, got, got2, fs, bands, acc, keep, code, zs, z, more, send):
+    sub = lax.axis_index("sub")
     for parity in range(2):
 
-        @pl.when(sub[0] == parity)
+        @pl.when(sub == parity)
         def _(parity=parity):
             vertical_operands(own, (got2, got) if parity else (got, got2), z)
 
@@ -254,7 +287,7 @@
     size = keep.shape[1]
     for parity in range(2):
 
-        @pl.when(sub[0] == parity)
+        @pl.when(sub == parity)
         def _(parity=parity):
             for t in range(27):
                 da, k = divmod(t, 9)
@@ -270,6 +303,12 @@
                     ref[block // 2, pl.ds(row - block * size, end - row), :] = v * (1.0 / VOX)
                     row = end
 
+    if code is send:
+        return
+    for n in range(keep.shape[0]):
+        encode(code, (n, 0), send[n, pl.ds(0, CUT), :])
+        encode(code, (n, 1), send[n, pl.ds(CUT, size - CUT), :])
+
 
 def columns(w, ks):
     return jnp.concatenate([jnp.concatenate([w[d * 9 + k] for k in ks], axis=1) for d in range(3)], axis=0)
@@ -281,69 +320,89 @@
     return total + y[pl.ds(p * rows, rows), pl.ds(2 * C, C)]
 
 
-def dgrad_kernel(j, mask, w, x, zs, before, out, y, yz, plane, res, sem):
+def dgrad_kernel(j, first, count, mask, w, x, zs, before, out, y, yz, plane, res, sem):
     del before
-    y[...] = dot_t(x[j], columns(w, range(9)))
+    y[...] = dot_t(x[j, pl.ds(first * PLANE, (count + 2) * PLANE), :], columns(w, range(9)))
     for n in range(2):
-        yz[n] = dot_t(zs[n, j], columns(w, (2, 5, 8) if n == 0 else (0, 3, 6)))
-    for p in range(BSIDE):
+        yz[n] = dot_t(zs[n, j, pl.ds(first * 16, (count + 2) * 16), :], columns(w, (2, 5, 8) if n == 0 else (0, 3, 6)))
+    for p in range(count):
         plane[pl.ds(0, PLANE), :] = joined(y, p, PLANE)
         for n in range(2):
             at = pl.ds(11 * n, BSIDE, stride=BSIDE)
             plane[at, :] = plane[at, :] + joined(yz.at[n], p, 16)[:BSIDE]
-        m = mask[pl.ds(p * PLANE, PLANE), pl.ds(j * C, C)].astype(F32)
+        m = mask[pl.ds((first + p) * PLANE, PLANE), pl.ds(j * C, C)].astype(F32)
         res[pl.ds(p * PLANE, PLANE), :] = (plane[pl.ds(0, PLANE), :] * m).astype(BF)
-    store = pltpu.make_async_copy(res, out.at[j], sem)
+    store = pltpu.make_async_copy(res, out.at[j, pl.ds(first * PLANE, count * PLANE)], sem)
     store.start()
     store.wait()
 
 
-def blocks_kernel(bits, keep, got, send1, keep1, send2, keep2):
-    b0, b1 = bits[0], bits[1]
-    cut = send1.shape[2]
+def place():
+    s = lax.axis_index("space")
+    return s % 2, s // 2 % 2, s // 4
+
+
+def blocks_kernel(keep, got, send1, keep1, send2, keep2):
+    b0, b1, _ = place()
+    rows = keep.shape[1]
+
+    def first(i):
+        return keep[i, pl.ds(0, CUT), :] + decoded(got, (i, 0), CUT)
+
+    def second(i):
+        return keep[i, pl.ds(CUT, rows - CUT), :] + decoded(got, (i, 1), rows - CUT)
+
     for z1 in range(2):
         for n in range(2):
-            for flip, ref1, ref2 in ((0, keep1, keep2), (1, send1, send2)):
-                i = z1 * 4 + n * 2 + jnp.bitwise_xor(b0, flip)
-                ref1[z1, n] = keep[i, pl.ds(0, cut), :] + got[i, pl.ds(0, cut), :]
-                i = z1 * 4 + jnp.bitwise_xor(b1, flip) * 2 + n
-                rest = pl.ds(cut, keep.shape[1] - cut)
-                ref2[z1, n] = keep[i, rest, :] + got[i, rest, :]
-
-
-def halves_kernel(bits, one, got1, two, got2, send1, keep1, send2, keep2):
-    b0, b1 = bits[0], bits[1]
+            i, k = z1 * 4 + n * 2, z1 * 4 + n
+            encode(send1, (z1, n), first(i + 1 - b0))
+            encode(send2, (z1, n), second(k + 2 - 2 * b1))
+            keep1[z1, n] = first(i + b0)
+            keep2[z1, n] = second(k + 2 * b1)
+
+
+def halves_kernel(one, got1, two, got2, send1, keep1, send2, keep2):
+    b0, b1, _ = place()
+    rest = two.shape[2]
     for z1 in range(2):
-        for flip, ref1, ref2 in ((0, keep1, keep2), (1, send1, send2)):
-            i, k = jnp.bitwise_xor(b1, flip), jnp.bitwise_xor(b0, flip)
-            ref1[z1] = one[z1, i] + got1[z1, i]
-            ref2[z1] = two[z1, k] + got2[z1, k]
-
-
-def last_kernel(bits, one, got1, two, got2, send, keep):
-    cut = one.shape[1]
-    for flip, ref in ((0, keep), (1, send)):
-        i = jnp.bitwise_xor(bits[2], flip)
-        ref[pl.ds(0, cut), :] = one[i] + got1[i]
-        ref[pl.ds(cut, two.shape[1]), :] = two[i] + got2[i]
+        encode(send1, (z1,), one[z1, 1 - b1] + decoded(got1, (z1, 1 - b1), CUT))
+        encode(send2, (z1,), two[z1, 1 - b0] + decoded(got2, (z1, 1 - b0), rest))
+        keep1[z1] = one[z1, b1] + decoded(got1, (z1, b1), CUT)
+        keep2[z1] = two[z1, b0] + decoded(got2, (z1, b0), rest)
+
+
+def last_kernel(one, got1, two, got2, send, keep):
+    b2 = place()[2]
+    rest = two.shape[1]
+    encode(send, (0,), one[1 - b2] + decoded(got1, (1 - b2,), CUT))
+    encode(send, (1,), two[1 - b2] + decoded(got2, (1 - b2,), rest))
+    keep[pl.ds(0, CUT), :] = one[b2] + decoded(got1, (b2,), CUT)
+    keep[pl.ds(CUT, rest), :] = two[b2] + decoded(got2, (b2,), rest)
+
+
+def sum_kernel(keep, got, out):
+    rest = keep.shape[0] - CUT
+    out[pl.ds(0, CUT), :] = keep[pl.ds(0, CUT), :] + decoded(got, (0,), CUT)
+    out[pl.ds(CUT, rest), :] = keep[pl.ds(CUT, rest), :] + decoded(got, (1,), rest)
 
 
 VMEM = pl.BlockSpec(memory_space=pltpu.MemorySpace.VMEM)
 SMEM = pl.BlockSpec(memory_space=pltpu.MemorySpace.SMEM)
 ANY = pl.BlockSpec(memory_space=pl.ANY)
 HBM = pl.BlockSpec(memory_space=pltpu.MemorySpace.HBM)
-
-
-def call(kernel, name, ins, outs, scratch=(), aliases=None, flops=0, size=0):
+FIXED = None
+
+
+def call(kernel, name, ins, outs, scratch=(), aliases=None, flops=0, size=0, limit=4):
     return pl.pallas_call(
         kernel,
         name=name,
-        out_shape=[jax.ShapeDtypeStruct(s, d) for s, d, _ in outs],
+        out_shape=[pltpu.VMEM(s, d) if o is FIXED else jax.ShapeDtypeStruct(s, d) for s, d, o in outs],
         in_specs=ins,
-        out_specs=[o for _, _, o in outs],
+        out_specs=[VMEM if o is FIXED else o for _, _, o in outs],
         scratch_shapes=list(scratch),
         input_output_aliases=aliases or {},
-        compiler_params=pltpu.CompilerParams(vmem_limit_bytes=LIMIT),
+        compiler_params=pltpu.CompilerParams(vmem_limit_bytes=limit * 2**20),
         cost_estimate=pl.CostEstimate(flops=flops, transcendentals=0, bytes_accessed=size),
     )
 
@@ -353,64 +412,68 @@
     return lax.ppermute(value, axis, pairs)
 
 
+def in_hbm(value):
+    return pltpu.with_memory_space_constraint(value, pltpu.MemorySpace.HBM)
+
+
 def tied(*values):
     return lax.optimization_barrier(values)
 
 
 def reduce_blocks(keep, got, fillers):
-    s = lax.axis_index("space").astype(jnp.int32)
-    bits = jnp.stack([s & 1, (s >> 1) & 1, (s >> 2) & 1])
-    rows = keep.shape[1]
-    cut = rows // 16 * 8
+    rest = keep.shape[1] - CUT
 
     def sums(kernel, name, lead, *values):
-        shapes = [((*lead, cut, C), F32, VMEM)] * 2 + [((*lead, rows - cut, C), F32, VMEM)] * 2
-        return call(kernel, name, [SMEM] + [VMEM] * len(values), shapes)(bits, *values)
+        code = ((*lead, C, C), jnp.int16, VMEM)
+        shapes = [code, ((*lead, CUT, C), F32, VMEM), code, ((*lead, rest, C), F32, VMEM)]
+        return call(kernel, name, [VMEM] * len(values), shapes)(*values)
 
     send1, keep1, send2, keep2 = sums(blocks_kernel, "blocks", (2, 2), keep, got)
     got1, got2 = exchange(send1, "space", 1), exchange(send2, "space", 2)
     got1, got2, fill = tied(got1, got2, fillers[0](None))
     send1, keep1, send2, keep2 = sums(halves_kernel, "halves", (2,), keep1, got1, keep2, got2)
     got1, got2 = exchange(send1, "space", 2), exchange(send2, "space", 1)
-    send, keep = call(last_kernel, "last", [SMEM] + [VMEM] * 4, [((rows, C), F32, VMEM)] * 2)(
-        bits, keep1, got1, keep2, got2
-    )
-    got, fill = tied(exchange(send, "space", 4), fillers[1](fill))
-    return keep + got, fill
+    got1, got2, fill = tied(got1, got2, fillers[1](fill))
+    send, keep = call(
+        last_kernel, "last", [VMEM] * 4, [((2, C, C), jnp.int16, VMEM), ((CUT + rest, C), F32, VMEM)]
+    )(keep1, got1, keep2, got2)
+    got, fill = tied(exchange(send, "space", 4), fillers[2](fill))
+    return call(sum_kernel, "sum", [VMEM] * 2, [((CUT + rest, C), F32, VMEM)])(keep, got)[0], fill
 
 
 def on_device(features, out_grad, weight, neighbours, active):
     layers = lax.axis_size("space")
-    sub = lax.axis_index("sub").astype(jnp.int32).reshape(1)
     strips, shift, bands = jnp.asarray(strip_matrix()), jnp.asarray(shift_matrix()), jnp.asarray(band_matrix())
 
-    gm, own, mine, mask = call(
+    gm, own, mine, mask, strips = call(
         prep_kernel,
         "prep",
-        [SMEM] * 2 + [HBM] * 3,
+        [HBM] * 4,
         [
             ((BSIDE, PLANE, 2 * C), BF, VMEM),
             ((MINE + 208, 2 * C), BF, VMEM),
             ((208, 2 * C), BF, VMEM),
             ((14 * C, 2 * C), BF, VMEM),
+            ((64, PLANE), BF, VMEM),
         ],
         [
+            pltpu.SMEM((2, 6), jnp.int32),
             pltpu.VMEM((2, VOX), jnp.int32),
-            pltpu.VMEM((64, PLANE), BF),
             pltpu.VMEM((2, VOX, C), BF),
-            pltpu.SemaphoreType.DMA((3,)),
+            pltpu.SemaphoreType.DMA((7,)),
         ],
-    )(sub, neighbours, active, strips, out_grad)
+    )(in_hbm(neighbours), in_hbm(active), in_hbm(strips), in_hbm(out_grad))
 
     other = exchange(own, "sub", 1)
     pad, fs = call(
         features_kernel,
         "features",
-        [VMEM] * 3,
+        [VMEM] * 2 + [HBM],
         [((2, (EXT + 2) * PLANE, C), BF, VMEM), ((2, (EXT + 2) * 16, 2 * C), BF, VMEM)],
+        [pltpu.VMEM((2, VOX, C), BF), pltpu.SemaphoreType.DMA],
         flops=10**7,
         size=10**6,
-    )(mask, strips, features)
+    )(mask, strips, in_hbm(features))
 
     ways = [(2 * i, 2 * i + 2) for i in range(layers - 1)] + [(2 * i + 3, 2 * i + 1) for i in range(layers - 1)]
     got = lax.ppermute(jnp.concatenate([mine, other[MINE:]], axis=0), ("space", "sub"), ways)
@@ -421,10 +484,11 @@
         first_kernel,
         "first",
         [VMEM] * 5,
-        [((2, EXT * PLANE, 9 * C), BF, VMEM), ((3 * C, 9 * C), F32, VMEM)],
+        [((2, EXT * PLANE, 9 * C), BF, FIXED), ((3 * C, 9 * C), F32, VMEM)],
         [pltpu.VMEM(kop_shape, BF)],
         flops=2 * work,
         size=8 * 2**20,
+        limit=6,
     )(shift, gm, own, other, pad)
     got, acc = tied(got, acc)
     got2 = exchange(got, "sub", 1)
@@ -440,36 +504,44 @@
     size = 27 * C // (2 * layers)
     custom = layers == 8
     rows = (layers, size, C) if custom else (8, 216, C)
+    exact = (rows, F32, VMEM)
+    tilt_ins = (own, got, got2, fs, bands, acc)
+    tilt_scratch = [pltpu.VMEM((2, EXT * 16, 2 * C), BF), pltpu.VMEM((2, 3 * C, 3 * C), F32)]
     keep, send, zs = call(
-        tilt_kernel,
+        tilt_kernel if custom else (lambda *refs: tilt_kernel(*refs, refs[7])),
         "tilt",
-        [SMEM] + [VMEM] * 6,
-        [(rows, F32, VMEM), (rows, F32, VMEM), ((2, 2, EXT * 16, 3 * C), BF, VMEM)],
-        [pltpu.VMEM((2, EXT * 16, 2 * C), BF), pltpu.VMEM((2, 3 * C, 3 * C), F32)],
+        [VMEM] * 6,
+        [
+            exact,
+            ((layers, 2, C, C), jnp.int16, VMEM) if custom else exact,
+            ((2, 2, EXT * 16, 3 * C), BF, VMEM),
+        ],
+        tilt_scratch + ([pltpu.VMEM(rows, F32)] if custom else []),
         flops=work // 4,
         size=4 * 2**20,
-    )(sub, own, got, got2, fs, bands, acc)
-
-    def dgrad(j):
+    )(*tilt_ins)
+
+    def dgrad(j, first, count):
         def run(before):
             fresh = before is None
             return call(
-                (lambda m, w, x_, z, *refs: dgrad_kernel(j, m, w, x_, z, None, *refs))
+                (lambda m, w, x_, z, *refs: dgrad_kernel(j, first, count, m, w, x_, z, None, *refs))
                 if fresh
-                else (lambda *refs: dgrad_kernel(j, *refs)),
+                else (lambda *refs: dgrad_kernel(j, first, count, *refs)),
                 "dgrad",
                 [VMEM] * 4 + ([] if fresh else [ANY]),
                 [((2, VOX, C), BF, ANY)],
                 [
-                    pltpu.VMEM((EXT * PLANE, 3 * C), F32),
-                    pltpu.VMEM((2, EXT * 16, 3 * C), F32),
+                    pltpu.VMEM(((count + 2) * PLANE, 3 * C), F32),
+                    pltpu.VMEM((2, (count + 2) * 16, 3 * C), F32),
                     pltpu.VMEM((PLANE + 16, C), F32),
-                    pltpu.VMEM((VOX, C), BF),
+                    pltpu.VMEM((count * PLANE, C), BF),
                     pltpu.SemaphoreType.DMA,
                 ],
                 aliases={} if fresh else {4: 0},
-                flops=work,
+                flops=work * count // 12,
                 size=4 * 2**20,
+                limit=10,
             )(mask, weight, x, zs, *(() if fresh else (before,)))[0]
 
         return run
@@ -477,13 +549,14 @@
     if custom:
         got = exchange(send, "sub", 1)
         got, zs = tied(got, zs)
-        weight_grad, input_grad = reduce_blocks(keep, got, [dgrad(0), dgrad(1)])
+        weight_grad, input_grad = reduce_blocks(keep, got, [dgrad(0, 0, 12), dgrad(1, 0, 6), dgrad(1, 6, 6)])
     else:
-        even = jnp.where(sub[0] == 0, keep, send)
-        odd = jnp.where(sub[0] == 0, send, keep)
+        first = lax.axis_index("sub") == 0
+        even = jnp.where(first, keep, send)
+        odd = jnp.where(first, send, keep)
         kernel_term = jnp.stack([even, odd], axis=1).reshape(27 * C, C)
         weight_grad = lax.psum_scatter(kernel_term, ("space", "sub"), scatter_dimension=0, tiled=True)
-        input_grad = dgrad(1)(dgrad(0)(None))
+        input_grad = dgrad(1, 0, 12)(dgrad(0, 0, 12)(None))
     return input_grad, weight_grad
 
 

time: 52.8 us -> 41.2 us (0.78)
  local copies, waits for them, and re-layouts: 8.55 us -> 0.03 us
  waiting for transfers between devices: 8.73 us -> 5.14 us
  Pallas kernels: 21.7 us -> 22.5 us
  other arithmetic: 0.75 us -> 0.02 us
  starting transfers between devices: 11.9 us -> 12.5 us
    unnamed x22 -> x6, local copies, waits for them, and re-layouts: 8.54 us -> 0.02 us
    ppermute x8, waiting for transfers between devices: 7.83 us -> 5.14 us  [exchange(): return lax.ppermute(value, axis, pairs)]
    pallas_call x9 -> x11, Pallas kernels: 19.5 us -> 21.5 us  [the longest x3 9 us: run(): call((lambda m, w, x_, z, *refs: dgrad_kernel(j, first, count, m, w, x_,...]
    pallas_call x1, Pallas kernels: 2.26 us -> 1.02 us  [on_device(): call(second_kernel, 'second', [VMEM, VMEM, VMEM], [((3 * C, 9 * C), F32,...]
    ppermute x1, waiting for transfers between devices: 0.91 us -> 0.01 us  [on_device(): lax.ppermute(jnp.concatenate([mine, other[MINE:]], axis=0), ('space', 'su...]
    add x1 -> x0, other arithmetic: 0.66 us -> none  [reduce_blocks(): return (keep + got, fill)]
    ppermute x8, starting transfers between devices: 7.44 us -> 8.03 us  [exchange(): return lax.ppermute(value, axis, pairs)]
  transfers between devices with their start and end apart: 9 -> 9, of which waited for: 5 -> 4; matrix products, arithmetic and copies ran while one was open for 0% -> 0% of each run, Pallas kernels for 29% -> 43%
where the time goes in v3:
time: 41.2 us; the launch traced here: 41 us
  Pallas kernels  22.5 us (55%)
  starting transfers between devices  12.5 us (30%)
  waiting for transfers between devices  5.14 us (12%)
  between operations  0.8 us (2%)
    pallas_call x3, Pallas kernels, run(): call((lambda m, w, x_, z, *refs: dgrad_kernel(j, first, count, m, w, x_,...  9 us
    ppermute x8, starting transfers between devices, exchange(): return lax.ppermute(value, axis, pairs)  8.03 us
    pallas_call x1, Pallas kernels, on_device(): call(first_kernel, 'first', [VMEM] * 5, [((2, EXT * PLANE, 9 * C), BF, FI...  5.95 us
    ppermute x8, waiting for transfers between devices, exchange(): return lax.ppermute(value, axis, pairs)  5.14 us
    ppermute x1, starting transfers between devices, on_device(): lax.ppermute(jnp.concatenate([mine, other[MINE:]], axis=0), ('space', 'su...  4.45 us
    pallas_call x1, Pallas kernels, on_device(): call(prep_kernel, 'prep', [HBM] * 4, [((BSIDE, PLANE, 2 * C), BF, VMEM),...  2.03 us
    pallas_call x1, Pallas kernels, on_device(): call(tilt_kernel if custom else lambda *refs: tilt_kernel(*refs, refs[7])...  1.75 us
    pallas_call x1, Pallas kernels, on_device(): call(features_kernel, 'features', [VMEM] * 2 + [HBM], [((2, (EXT + 2) * P...  1.64 us
  transfers between devices with their start and end apart: 9, of which 4 were waited for; matrix products, arithmetic and copies ran while one was open for 0% of the time, Pallas kernels for 43%

profile of v3, /device:TPU:0, one launch (start us, length us, event | category | flops | bytes accessed | tf_op | source)
XLA Modules:
  0.0 41.0 jit_solution(18156181909606491222)
XLA Ops:
  0.6 0.0 copy-start.2
  0.6 2.0 %prep.1 = (bf16[12,144,256]{2,1,0:T(8,128)(2,1)S(1)}, bf16[560,256]{1,0:T(8,128)(2,1)S(1)}, bf16[208,256]{1,0:T(8,128)(2,1)S(1)}, bf16[1792,256]{1,0:T(8,128)(2,1)S(1)}, bf16[64,144]{1,0:T(8,128)(2,1)S(1)}) custom-call(s32[2,6]{1,0:T(2,128)} %nb_hbm.1, s32[2,1728]{1,0:T(2,128)} %act_hbm.1, bf16[64,144]{1,0:T(8,128)(2,1)} %constant.6.clone.strips_hbm, ...), custom_call_target="tpu_custom_call" | custom-call | tf_op jit(solution)/shard_map/prep/pallas_call | solution.py:448
  2.7 0.5 %collective-permute-start = (bf16[560,256]{1,0:T(8,128)(2,1)S(1)}, bf16[560,256]{1,0:T(8,128)(2,1)S(1)}, u32[]{:S(2)}, u32[]{:S(2)}) collective-permute-start(bf16[560,256]{1,0:T(8,128)(2,1)S(1)} %get-tuple-element.36.own), channel_id=1, source_target_pairs={{0,1},{1,0},{2,3},{3,2},{4,5},{5,4},{6,7},{7,6},{8,9},{9,8},{10,11... | collective-permute-start | bytes 860168 | tf_op jit(solution)/shard_map/ppermute | solution.py:412
  3.2 1.6 %features.1 = (bf16[2,2304,128]{2,1,0:T(8,128)(2,1)S(1)}, bf16[2,256,256]{2,1,0:T(8,128)(2,1)S(1)}) custom-call(bf16[1792,256]{1,0:T(8,128)(2,1)S(1)} %get-tuple-element.39.mask.m.refs_0_, bf16[64,144]{1,0:T(8,128)(2,1)S(1)} %get-tuple-element.40.strips, bf16[2,1728,128]{2,1,0:T(8,128)(2,1)} %f_hbm.1), custom_call_target="tpu_custom_call" | custom-call | flops 10000000 | bytes 1000000 | tf_op jit(solution)/shard_map/features/pallas_call | solution.py:468
  4.8 0.0 collective-permute-done.other
  4.9 4.5 %collective-permute-start.1 = (bf16[416,256]{1,0:T(8,128)(2,1)S(1)}, bf16[416,256]{1,0:T(8,128)(2,1)S(1)}, u32[]{:S(2)}, u32[]{:S(2)}) collective-permute-start(bf16[416,256]{1,0:T(8,128)(2,1)S(1)} %pad_maximum_fusion), channel_id=1, source_target_pairs={{0,2},{2,4},{4,6},{6,8},{8,10},{10,12},{12,14},{3,1},{5,3},{7,5},{... | collective-permute-start | bytes 638984 | tf_op jit(solution)/shard_map/ppermute | solution.py:479
  9.4 0.0 copy-done.2
  9.4 5.9 %first.1 = (bf16[2,2016,1152]{2,1,0:T(8,128)(2,1)S(1)}, f32[384,1152]{1,0:T(8,128)S(1)}) custom-call(bf16[1296,256]{1,0:T(8,128)(2,1)S(1)} %copy-done.2, bf16[12,144,256]{2,1,0:T(8,128)(2,1)S(1)} %get-tuple-element.38.gm, bf16[560,256]{1,0:T(8,128)(2,1)S(1)} %get-tuple-element.36.own, bf16[560,256]{1,0:T(8,128)(2,1)S(1)} %collective-permute-done.other, ...), custom_call_target="tpu_custom_call" | custom-call | flops 3567255552 | bytes 8388608 | tf_op jit(solution)/shard_map/first/pallas_call | solution.py:483
  15.3 0.0 collective-permute-done.1.got
  15.3 0.1 collective-permute-start.2
  15.4 0.0 copy-start.1
  15.4 1.0 %second.1.acc = f32[384,1152]{1,0:T(8,128)S(1)} custom-call(bf16[2,2304,128]{2,1,0:T(8,128)(2,1)S(1)} %get-tuple-element.41.pad, bf16[2,2016,1152]{2,1,0:T(8,128)(2,1)S(1)} %get-tuple-element.45.x.x_.refs_2_, f32[384,1152]{1,0:T(8,128)S(1)} %get-tuple-element.46.before), custom_call_target="tpu_custom_call" | custom-call | flops 1783627776 | bytes 4194304 | tf_op jit(solution)/shard_map/second/pallas_call | solution.py:495
  16.4 0.4 %collective-permute-done.2.got2 = bf16[416,256]{1,0:T(8,128)(2,1)S(1)} collective-permute-done((bf16[416,256]{1,0:T(8,128)(2,1)S(1)}, bf16[416,256]{1,0:T(8,128)(2,1)S(1)}, u32[]{:S(2)}, u32[]{:S(2)}) %collective-permute-start.2) | collective-permute-done | bytes 213024 | tf_op jit(solution)/shard_map/ppermute | solution.py:412
  16.9 0.0 copy-done.1
  16.9 0.0 copy-start
  16.9 1.8 %tilt.1 = (f32[8,216,128]{2,1,0:T(8,128)S(1)}, s16[8,2,128,128]{3,2,1,0:T(8,128)(2,1)S(1)}, bf16[2,2,224,384]{3,2,1,0:T(8,128)(2,1)S(1)}) custom-call(bf16[560,256]{1,0:T(8,128)(2,1)S(1)} %get-tuple-element.36.own, bf16[416,256]{1,0:T(8,128)(2,1)S(1)} %collective-permute-done.1.got, bf16[416,256]{1,0:T(8,128)(2,1)S(1)} %collective-permute-done.2.got2, ...), custom_call_target="tpu_custom_call" | custom-call | flops 445906944 | bytes 4194304 | tf_op jit(solution)/shard_map/tilt/pallas_call | solution.py:510
  18.6 0.2 collective-permute-start.3
  18.9 1.7 %collective-permute-done.3.got = s16[8,2,128,128]{3,2,1,0:T(8,128)(2,1)S(1)} collective-permute-done((s16[8,2,128,128]{3,2,1,0:T(8,128)(2,1)S(1)}, s16[8,2,128,128]{3,2,1,0:T(8,128)(2,1)S(1)}, u32[]{:S(2)}, u32[]{:S(2)}) %collective-permute-start.3) | collective-permute-done | bytes 524320 | tf_op jit(solution)/shard_map/ppermute | solution.py:412
  20.6 0.2 blocks.1
  20.8 2.1 %collective-permute-start.4 = (s16[2,2,128,128]{3,2,1,0:T(8,128)(2,1)S(1)}, s16[2,2,128,128]{3,2,1,0:T(8,128)(2,1)S(1)}, u32[]{:S(2)}, u32[]{:S(2)}) collective-permute-start(s16[2,2,128,128]{3,2,1,0:T(8,128)(2,1)S(1)} %get-tuple-element.52), channel_id=1, source_target_pairs={{0,2},{2,0},{4,6},{6,4},{8,10},{10,8},{12,14},{14,12},{1,3},{3,1},... | collective-permute-start | bytes 393224 | tf_op jit(solution)/shard_map/ppermute | solution.py:412
  23.0 1.6 %collective-permute-start.5 = (s16[2,2,128,128]{3,2,1,0:T(8,128)(2,1)S(1)}, s16[2,2,128,128]{3,2,1,0:T(8,128)(2,1)S(1)}, u32[]{:S(2)}, u32[]{:S(2)}) collective-permute-start(s16[2,2,128,128]{3,2,1,0:T(8,128)(2,1)S(1)} %get-tuple-element.53), channel_id=1, source_target_pairs={{0,4},{2,6},{4,0},{6,2},{8,12},{10,14},{12,8},{14,10},{1,5},{3,7},... | collective-permute-start | bytes 393224 | tf_op jit(solution)/shard_map/ppermute | solution.py:412
  24.5 0.0 copy-done
  24.5 3.9 %dgrad.3.refs_4_ = bf16[2,1728,128]{2,1,0:T(8,128)(2,1)} custom-call(bf16[1792,256]{1,0:T(8,128)(2,1)S(1)} %get-tuple-element.39.mask.m.refs_0_, bf16[27,128,128]{2,1,0:T(8,128)(2,1)S(1)} %copy-done, bf16[2,2016,1152]{2,1,0:T(8,128)(2,1)S(1)} %get-tuple-element.45.x.x_.refs_2_, bf16[2,2,224,384]{3,2,1,0:T(8,128)(2,1)S(1)} %get-tuple-element.54.z.refs_3_), custom_call_target="tpu_custom_call" | custom-call | flops 1783627776 | bytes 4194304 | tf_op jit(solution)/shard_map/dgrad/pallas_call | solution.py:527
  28.5 0.0 collective-permute-done.4.got1
  28.5 0.0 collective-permute-done.5.got2
  28.5 0.1 halves.1
  28.6 1.4 %collective-permute-start.6 = (s16[2,128,128]{2,1,0:T(8,128)(2,1)S(1)}, s16[2,128,128]{2,1,0:T(8,128)(2,1)S(1)}, u32[]{:S(2)}, u32[]{:S(2)}) collective-permute-start(s16[2,128,128]{2,1,0:T(8,128)(2,1)S(1)} %get-tuple-element.59), channel_id=1, source_target_pairs={{0,4},{2,6},{4,0},{6,2},{8,12},{10,14},{12,8},{14,10},{1,5},{3,7},... | collective-permute-start | bytes 196616 | tf_op jit(solution)/shard_map/ppermute | solution.py:412
  30.0 0.4 collective-permute-start.7
  30.4 2.5 %dgrad.4.refs_4_ = bf16[2,1728,128]{2,1,0:T(8,128)(2,1)} custom-call(bf16[1792,256]{1,0:T(8,128)(2,1)S(1)} %get-tuple-element.39.mask.m.refs_0_, bf16[27,128,128]{2,1,0:T(8,128)(2,1)S(1)} %copy-done, bf16[2,2016,1152]{2,1,0:T(8,128)(2,1)S(1)} %get-tuple-element.45.x.x_.refs_2_, ...), custom_call_target="tpu_custom_call", output_to_operand_aliasing={{}: (4, {})} | custom-call | flops 891813888 | bytes 4194304 | tf_op jit(solution)/shard_map/dgrad/pallas_call | solution.py:527
  32.9 0.0 collective-permute-done.6.got1
  33.0 1.3 %collective-permute-done.7.got2 = s16[2,128,128]{2,1,0:T(8,128)(2,1)S(1)} collective-permute-done((s16[2,128,128]{2,1,0:T(8,128)(2,1)S(1)}, s16[2,128,128]{2,1,0:T(8,128)(2,1)S(1)}, u32[]{:S(2)}, u32[]{:S(2)}) %collective-permute-start.7) | collective-permute-done | bytes 65568 | tf_op jit(solution)/shard_map/ppermute | solution.py:412
  34.3 0.1 last.1
  34.4 1.8 %collective-permute-start.8 = (s16[2,128,128]{2,1,0:T(8,128)(2,1)S(1)}, s16[2,128,128]{2,1,0:T(8,128)(2,1)S(1)}, u32[]{:S(2)}, u32[]{:S(2)}) collective-permute-start(s16[2,128,128]{2,1,0:T(8,128)(2,1)S(1)} %get-tuple-element.65), channel_id=1, source_target_pairs={{0,8},{2,10},{4,12},{6,14},{8,0},{10,2},{12,4},{14,6},{1,9},{3,11}... | collective-permute-start | bytes 196616 | tf_op jit(solution)/shard_map/ppermute | solution.py:412
  36.1 2.6 %dgrad.5 = bf16[2,1728,128]{2,1,0:T(8,128)(2,1)} custom-call(bf16[1792,256]{1,0:T(8,128)(2,1)S(1)} %get-tuple-element.39.mask.m.refs_0_, bf16[27,128,128]{2,1,0:T(8,128)(2,1)S(1)} %copy-done, bf16[2,2016,1152]{2,1,0:T(8,128)(2,1)S(1)} %get-tuple-element.45.x.x_.refs_2_, ...), custom_call_target="tpu_custom_call", output_to_operand_aliasing={{}: (4, {})} | custom-call | flops 891813888 | bytes 4194304 | tf_op jit(solution)/shard_map/dgrad/pallas_call | solution.py:527
  38.7 1.6 %collective-permute-done.8.got = s16[2,128,128]{2,1,0:T(8,128)(2,1)S(1)} collective-permute-done((s16[2,128,128]{2,1,0:T(8,128)(2,1)S(1)}, s16[2,128,128]{2,1,0:T(8,128)(2,1)S(1)}, u32[]{:S(2)}, u32[]{:S(2)}) %collective-permute-start.8) | collective-permute-done | bytes 65568 | tf_op jit(solution)/shard_map/ppermute | solution.py:412
  40.3 0.7 %sum.1 = f32[216,128]{1,0:T(8,128)} custom-call(f32[216,128]{1,0:T(8,128)S(1)} %get-tuple-element.68.keep, s16[2,128,128]{2,1,0:T(8,128)(2,1)S(1)} %collective-permute-done.8.got), custom_call_target="tpu_custom_call" | custom-call | tf_op jit(solution)/shard_map/sum/pallas_call | solution.py:441
  (2 shorter events, 0.0 us)
Async XLA Ops:
  0.6 8.7 %copy-start.2 = (bf16[1296,256]{1,0:T(8,128)(2,1)S(1)}, bf16[1296,256]{1,0:T(8,128)(2,1)}, u32[]{:S(2)}) copy-start(bf16[1296,256]{1,0:T(8,128)(2,1)} %constant.7.clone.shift) | copy-start | bytes 1990660
  2.7 2.2 %collective-permute-start = (bf16[560,256]{1,0:T(8,128)(2,1)S(1)}, bf16[560,256]{1,0:T(8,128)(2,1)S(1)}, u32[]{:S(2)}, u32[]{:S(2)}) collective-permute-start(bf16[560,256]{1,0:T(8,128)(2,1)S(1)} %get-tuple-element.36.own), channel_id=1, source_target_pairs={{0,1},{1,0},{2,3},{3,2},{4,5},{5,4},{6,7},{7,6},{8,9},{9,8},{10,11... | collective-permute-start | bytes 860168 | tf_op jit(solution)/shard_map/ppermute | solution.py:412
  4.9 10.4 %collective-permute-start.1 = (bf16[416,256]{1,0:T(8,128)(2,1)S(1)}, bf16[416,256]{1,0:T(8,128)(2,1)S(1)}, u32[]{:S(2)}, u32[]{:S(2)}) collective-permute-start(bf16[416,256]{1,0:T(8,128)(2,1)S(1)} %pad_maximum_fusion), channel_id=1, source_target_pairs={{0,2},{2,4},{4,6},{6,8},{8,10},{10,12},{12,14},{3,1},{5,3},{7,5},{... | collective-permute-start | bytes 638984 | tf_op jit(solution)/shard_map/ppermute | solution.py:479
  15.3 1.5 %collective-permute-start.2 = (bf16[416,256]{1,0:T(8,128)(2,1)S(1)}, bf16[416,256]{1,0:T(8,128)(2,1)S(1)}, u32[]{:S(2)}, u32[]{:S(2)}) collective-permute-start(bf16[416,256]{1,0:T(8,128)(2,1)S(1)} %collective-permute-done.1.got), channel_id=1, source_target_pairs={{0,1},{1,0},{2,3},{3,2},{4,5},{5,4},{6,7},{7,6},{8,9},{9,8},{10,11... | collective-permute-start | bytes 638984 | tf_op jit(solution)/shard_map/ppermute | solution.py:412
  15.4 1.5 %copy-start.1 = (bf16[672,224]{1,0:T(8,128)(2,1)S(1)}, bf16[672,224]{1,0:T(8,128)(2,1)}, u32[]{:S(2)}) copy-start(bf16[672,224]{1,0:T(8,128)(2,1)} %constant.8.clone.bands) | copy-start | bytes 903172
  16.9 7.7 %copy-start = (bf16[27,128,128]{2,1,0:T(8,128)(2,1)S(1)}, bf16[27,128,128]{2,1,0:T(8,128)(2,1)}, u32[]{:S(2)}) copy-start(bf16[27,128,128]{2,1,0:T(8,128)(2,1)} %refs_1_.3) | copy-start | bytes 2654212
  18.6 2.0 %collective-permute-start.3 = (s16[8,2,128,128]{3,2,1,0:T(8,128)(2,1)S(1)}, s16[8,2,128,128]{3,2,1,0:T(8,128)(2,1)S(1)}, u32[]{:S(2)}, u32[]{:S(2)}) collective-permute-start(s16[8,2,128,128]{3,2,1,0:T(8,128)(2,1)S(1)} %get-tuple-element.48), channel_id=1, source_target_pairs={{0,1},{1,0},{2,3},{3,2},{4,5},{5,4},{6,7},{7,6},{8,9},{9,8},{10,11... | collective-permute-start | bytes 1572872 | tf_op jit(solution)/shard_map/ppermute | solution.py:412
  20.8 7.6 %collective-permute-start.4 = (s16[2,2,128,128]{3,2,1,0:T(8,128)(2,1)S(1)}, s16[2,2,128,128]{3,2,1,0:T(8,128)(2,1)S(1)}, u32[]{:S(2)}, u32[]{:S(2)}) collective-permute-start(s16[2,2,128,128]{3,2,1,0:T(8,128)(2,1)S(1)} %get-tuple-element.52), channel_id=1, source_target_pairs={{0,2},{2,0},{4,6},{6,4},{8,10},{10,8},{12,14},{14,12},{1,3},{3,1},... | collective-permute-start | bytes 393224 | tf_op jit(solution)/shard_map/ppermute | solution.py:412
  23.0 5.5 %collective-permute-start.5 = (s16[2,2,128,128]{3,2,1,0:T(8,128)(2,1)S(1)}, s16[2,2,128,128]{3,2,1,0:T(8,128)(2,1)S(1)}, u32[]{:S(2)}, u32[]{:S(2)}) collective-permute-start(s16[2,2,128,128]{3,2,1,0:T(8,128)(2,1)S(1)} %get-tuple-element.53), channel_id=1, source_target_pairs={{0,4},{2,6},{4,0},{6,2},{8,12},{10,14},{12,8},{14,10},{1,5},{3,7},... | collective-permute-start | bytes 393224 | tf_op jit(solution)/shard_map/ppermute | solution.py:412
  28.6 4.3 %collective-permute-start.6 = (s16[2,128,128]{2,1,0:T(8,128)(2,1)S(1)}, s16[2,128,128]{2,1,0:T(8,128)(2,1)S(1)}, u32[]{:S(2)}, u32[]{:S(2)}) collective-permute-start(s16[2,128,128]{2,1,0:T(8,128)(2,1)S(1)} %get-tuple-element.59), channel_id=1, source_target_pairs={{0,4},{2,6},{4,0},{6,2},{8,12},{10,14},{12,8},{14,10},{1,5},{3,7},... | collective-permute-start | bytes 196616 | tf_op jit(solution)/shard_map/ppermute | solution.py:412
  30.0 4.3 %collective-permute-start.7 = (s16[2,128,128]{2,1,0:T(8,128)(2,1)S(1)}, s16[2,128,128]{2,1,0:T(8,128)(2,1)S(1)}, u32[]{:S(2)}, u32[]{:S(2)}) collective-permute-start(s16[2,128,128]{2,1,0:T(8,128)(2,1)S(1)} %get-tuple-element.60), channel_id=1, source_target_pairs={{0,2},{2,0},{4,6},{6,4},{8,10},{10,8},{12,14},{14,12},{1,3},{3,1},... | collective-permute-start | bytes 196616 | tf_op jit(solution)/shard_map/ppermute | solution.py:412
  34.4 5.9 %collective-permute-start.8 = (s16[2,128,128]{2,1,0:T(8,128)(2,1)S(1)}, s16[2,128,128]{2,1,0:T(8,128)(2,1)S(1)}, u32[]{:S(2)}, u32[]{:S(2)}) collective-permute-start(s16[2,128,128]{2,1,0:T(8,128)(2,1)S(1)} %get-tuple-element.65), channel_id=1, source_target_pairs={{0,8},{2,10},{4,12},{6,14},{8,0},{10,2},{12,4},{14,6},{1,9},{3,11}... | collective-permute-start | bytes 196616 | tf_op jit(solution)/shard_map/ppermute | solution.py:412

commit v4 on v3

--- a/solution.py
+++ b/solution.py
@@ -13,7 +13,6 @@
 C = 128
 KROWS = 256
 EARLY = 9
-CUT = 112
 MINE = PLANE + 208
 BF = jnp.bfloat16
 F32 = jnp.float32
@@ -252,17 +251,13 @@
     top = jnp.maximum(jnp.max(jnp.abs(v), axis=0, keepdims=True), 1e-33)
     e = jnp.floor(jnp.log2(top)) - 14
     q = jnp.clip(jnp.round(v * jnp.exp2(-e)), -32767, 32767)
-    if v.shape[0] < CUT:
-        q = jnp.concatenate([q, jnp.zeros((CUT - v.shape[0], C), F32)], axis=0)
-    ref[(*at, pl.ds(0, CUT), slice(None))] = q.astype(jnp.int32).astype(jnp.int16)
-    e = jnp.broadcast_to(e, (C - CUT, C))
-    ref[(*at, pl.ds(CUT, C - CUT), slice(None))] = e.astype(jnp.int32).astype(jnp.int16)
-
-
-def decoded(ref, at, rows):
-    e = ref[(*at, pl.ds(CUT, C - CUT), slice(None))].astype(jnp.int32).astype(F32)[:1]
-    q = ref[(*at, pl.ds(0, CUT), slice(None))].astype(jnp.int32).astype(F32)
-    return (q * jnp.exp2(e))[:rows]
+    ref[at] = jnp.concatenate([q, jnp.broadcast_to(e, (8, C))], axis=0).astype(jnp.int32).astype(jnp.int16)
+
+
+def decoded(ref, at):
+    v = ref[at].astype(jnp.int32).astype(F32)
+    rows = v.shape[0] - 8
+    return v[:rows] * jnp.exp2(v[rows : rows + 1])
 
 
 def tilt_kernel(own, got, got2, fs, bands, acc, keep, code, zs, z, more, send):
@@ -306,8 +301,7 @@
     if code is send:
         return
     for n in range(keep.shape[0]):
-        encode(code, (n, 0), send[n, pl.ds(0, CUT), :])
-        encode(code, (n, 1), send[n, pl.ds(CUT, size - CUT), :])
+        encode(code, n, send[n])
 
 
 def columns(w, ks):
@@ -320,21 +314,29 @@
     return total + y[pl.ds(p * rows, rows), pl.ds(2 * C, C)]
 
 
-def dgrad_kernel(j, first, count, mask, w, x, zs, before, out, y, yz, plane, res, sem):
+def dgrad_kernel(pieces, mask, w, x, zs, before, out, y, yz, plane, res, sem):
     del before
-    y[...] = dot_t(x[j, pl.ds(first * PLANE, (count + 2) * PLANE), :], columns(w, range(9)))
-    for n in range(2):
-        yz[n] = dot_t(zs[n, j, pl.ds(first * 16, (count + 2) * 16), :], columns(w, (2, 5, 8) if n == 0 else (0, 3, 6)))
-    for p in range(count):
-        plane[pl.ds(0, PLANE), :] = joined(y, p, PLANE)
+    stores = []
+    for j, first, count in pieces:
+        rows = pl.ds(0, (count + 2) * PLANE)
+        y[rows, :] = dot_t(x[j, pl.ds(first * PLANE, (count + 2) * PLANE), :], columns(w, range(9)))
         for n in range(2):
-            at = pl.ds(11 * n, BSIDE, stride=BSIDE)
-            plane[at, :] = plane[at, :] + joined(yz.at[n], p, 16)[:BSIDE]
-        m = mask[pl.ds((first + p) * PLANE, PLANE), pl.ds(j * C, C)].astype(F32)
-        res[pl.ds(p * PLANE, PLANE), :] = (plane[pl.ds(0, PLANE), :] * m).astype(BF)
-    store = pltpu.make_async_copy(res, out.at[j, pl.ds(first * PLANE, count * PLANE)], sem)
-    store.start()
-    store.wait()
+            faces = dot_t(zs[n, j, pl.ds(first * 16, (count + 2) * 16), :], columns(w, (2, 5, 8) if n == 0 else (0, 3, 6)))
+            yz[n, pl.ds(0, (count + 2) * 16), :] = faces
+        for p in range(count):
+            plane[pl.ds(0, PLANE), :] = joined(y, p, PLANE)
+            for n in range(2):
+                at = pl.ds(11 * n, BSIDE, stride=BSIDE)
+                plane[at, :] = plane[at, :] + joined(yz.at[n], p, 16)[:BSIDE]
+            m = mask[pl.ds((first + p) * PLANE, PLANE), pl.ds(j * C, C)].astype(F32)
+            at = pl.ds((first + p) * PLANE, PLANE)
+            res[j, at, :] = (plane[pl.ds(0, PLANE), :] * m).astype(BF)
+            if p % 2 == 1:
+                at = pl.ds((first + p - 1) * PLANE, 2 * PLANE)
+                stores.append(pltpu.make_async_copy(res.at[j, at], out.at[j, at], sem.at[len(stores)]))
+                stores[-1].start()
+    for store in stores:
+        store.wait()
 
 
 def place():
@@ -342,48 +344,28 @@
     return s % 2, s // 2 % 2, s // 4
 
 
-def blocks_kernel(keep, got, send1, keep1, send2, keep2):
-    b0, b1, _ = place()
-    rows = keep.shape[1]
-
-    def first(i):
-        return keep[i, pl.ds(0, CUT), :] + decoded(got, (i, 0), CUT)
-
-    def second(i):
-        return keep[i, pl.ds(CUT, rows - CUT), :] + decoded(got, (i, 1), rows - CUT)
-
-    for z1 in range(2):
-        for n in range(2):
-            i, k = z1 * 4 + n * 2, z1 * 4 + n
-            encode(send1, (z1, n), first(i + 1 - b0))
-            encode(send2, (z1, n), second(k + 2 - 2 * b1))
-            keep1[z1, n] = first(i + b0)
-            keep2[z1, n] = second(k + 2 * b1)
-
-
-def halves_kernel(one, got1, two, got2, send1, keep1, send2, keep2):
-    b0, b1, _ = place()
-    rest = two.shape[2]
-    for z1 in range(2):
-        encode(send1, (z1,), one[z1, 1 - b1] + decoded(got1, (z1, 1 - b1), CUT))
-        encode(send2, (z1,), two[z1, 1 - b0] + decoded(got2, (z1, 1 - b0), rest))
-        keep1[z1] = one[z1, b1] + decoded(got1, (z1, b1), CUT)
-        keep2[z1] = two[z1, b0] + decoded(got2, (z1, b0), rest)
-
-
-def last_kernel(one, got1, two, got2, send, keep):
-    b2 = place()[2]
-    rest = two.shape[1]
-    encode(send, (0,), one[1 - b2] + decoded(got1, (1 - b2,), CUT))
-    encode(send, (1,), two[1 - b2] + decoded(got2, (1 - b2,), rest))
-    keep[pl.ds(0, CUT), :] = one[b2] + decoded(got1, (b2,), CUT)
-    keep[pl.ds(CUT, rest), :] = two[b2] + decoded(got2, (b2,), rest)
+def blocks_kernel(keep, got, send_y, send_z, send_yz, own):
+    y, z, _ = place()
+    for high in range(2):
+        for ref, to_y, to_z in ((send_y, 1 - y, z), (send_z, y, 1 - z), (send_yz, 1 - y, 1 - z)):
+            n = high * 4 + to_z * 2 + to_y
+            encode(ref, high, keep[n] + decoded(got, n))
+        n = high * 4 + z * 2 + y
+        own[high] = keep[n] + decoded(got, n)
+
+
+def last_kernel(own, got_y, got_z, got_yz, send, keep):
+    high = place()[2]
+
+    def total(n):
+        return own[n] + decoded(got_y, n) + decoded(got_z, n) + decoded(got_yz, n)
+
+    encode(send, Ellipsis, total(1 - high))
+    keep[...] = total(high)
 
 
 def sum_kernel(keep, got, out):
-    rest = keep.shape[0] - CUT
-    out[pl.ds(0, CUT), :] = keep[pl.ds(0, CUT), :] + decoded(got, (0,), CUT)
-    out[pl.ds(CUT, rest), :] = keep[pl.ds(CUT, rest), :] + decoded(got, (1,), rest)
+    out[...] = keep[...] + decoded(got, Ellipsis)
 
 
 VMEM = pl.BlockSpec(memory_space=pltpu.MemorySpace.VMEM)
@@ -421,24 +403,14 @@
 
 
 def reduce_blocks(keep, got, fillers):
-    rest = keep.shape[1] - CUT
-
-    def sums(kernel, name, lead, *values):
-        code = ((*lead, C, C), jnp.int16, VMEM)
-        shapes = [code, ((*lead, CUT, C), F32, VMEM), code, ((*lead, rest, C), F32, VMEM)]
-        return call(kernel, name, [VMEM] * len(values), shapes)(*values)
-
-    send1, keep1, send2, keep2 = sums(blocks_kernel, "blocks", (2, 2), keep, got)
-    got1, got2 = exchange(send1, "space", 1), exchange(send2, "space", 2)
-    got1, got2, fill = tied(got1, got2, fillers[0](None))
-    send1, keep1, send2, keep2 = sums(halves_kernel, "halves", (2,), keep1, got1, keep2, got2)
-    got1, got2 = exchange(send1, "space", 2), exchange(send2, "space", 1)
-    got1, got2, fill = tied(got1, got2, fillers[1](fill))
-    send, keep = call(
-        last_kernel, "last", [VMEM] * 4, [((2, C, C), jnp.int16, VMEM), ((CUT + rest, C), F32, VMEM)]
-    )(keep1, got1, keep2, got2)
-    got, fill = tied(exchange(send, "space", 4), fillers[2](fill))
-    return call(sum_kernel, "sum", [VMEM] * 2, [((CUT + rest, C), F32, VMEM)])(keep, got)[0], fill
+    rows = keep.shape[1]
+    code = (rows + 8, C)
+    *sends, own = call(blocks_kernel, "blocks", [VMEM] * 2, [((2, *code), jnp.int16, VMEM)] * 3 + [((2, rows, C), F32, VMEM)])(keep, got)
+    gots = [exchange(send, "space", bit) for bit, send in enumerate(sends, 1)]
+    *gots, fill = tied(*gots, fillers[0](None))
+    send, keep = call(last_kernel, "last", [VMEM] * 4, [(code, jnp.int16, VMEM), ((rows, C), F32, VMEM)])(own, *gots)
+    got, fill = tied(exchange(send, "space", 4), fillers[1](fill))
+    return call(sum_kernel, "sum", [VMEM] * 2, [((rows, C), F32, VMEM)])(keep, got)[0], fill
 
 
 def on_device(features, out_grad, weight, neighbours, active):
@@ -513,7 +485,7 @@
         [VMEM] * 6,
         [
             exact,
-            ((layers, 2, C, C), jnp.int16, VMEM) if custom else exact,
+            ((layers, size + 8, C), jnp.int16, VMEM) if custom else exact,
             ((2, 2, EXT * 16, 3 * C), BF, VMEM),
         ],
         tilt_scratch + ([pltpu.VMEM(rows, F32)] if custom else []),
@@ -521,27 +493,29 @@
         size=4 * 2**20,
     )(*tilt_ins)
 
-    def dgrad(j, first, count):
+    def dgrad(*pieces):
+        most = max(count for _, _, count in pieces) + 2
+
         def run(before):
             fresh = before is None
             return call(
-                (lambda m, w, x_, z, *refs: dgrad_kernel(j, first, count, m, w, x_, z, None, *refs))
+                (lambda m, w, x_, z, *refs: dgrad_kernel(pieces, m, w, x_, z, None, *refs))
                 if fresh
-                else (lambda *refs: dgrad_kernel(j, first, count, *refs)),
+                else (lambda *refs: dgrad_kernel(pieces, *refs)),
                 "dgrad",
                 [VMEM] * 4 + ([] if fresh else [ANY]),
                 [((2, VOX, C), BF, ANY)],
                 [
-                    pltpu.VMEM(((count + 2) * PLANE, 3 * C), F32),
-                    pltpu.VMEM((2, (count + 2) * 16, 3 * C), F32),
+                    pltpu.VMEM((most * PLANE, 3 * C), F32),
+                    pltpu.VMEM((2, most * 16, 3 * C), F32),
                     pltpu.VMEM((PLANE + 16, C), F32),
-                    pltpu.VMEM((count * PLANE, C), BF),
-                    pltpu.SemaphoreType.DMA,
+                    pltpu.VMEM((2, VOX, C), BF),
+                    pltpu.SemaphoreType.DMA((12,)),
                 ],
                 aliases={} if fresh else {4: 0},
-                flops=work * count // 12,
+                flops=work * sum(count for _, _, count in pieces) // 12,
                 size=4 * 2**20,
-                limit=10,
+                limit=12,
             )(mask, weight, x, zs, *(() if fresh else (before,)))[0]
 
         return run
@@ -549,14 +523,14 @@
     if custom:
         got = exchange(send, "sub", 1)
         got, zs = tied(got, zs)
-        weight_grad, input_grad = reduce_blocks(keep, got, [dgrad(0, 0, 12), dgrad(1, 0, 6), dgrad(1, 6, 6)])
+        weight_grad, input_grad = reduce_blocks(keep, got, [dgrad((0, 0, 12), (1, 0, 4)), dgrad((1, 4, 8))])
     else:
         first = lax.axis_index("sub") == 0
         even = jnp.where(first, keep, send)
         odd = jnp.where(first, send, keep)
         kernel_term = jnp.stack([even, odd], axis=1).reshape(27 * C, C)
         weight_grad = lax.psum_scatter(kernel_term, ("space", "sub"), scatter_dimension=0, tiled=True)
-        input_grad = dgrad(1, 0, 12)(dgrad(0, 0, 12)(None))
+        input_grad = dgrad((0, 0, 12), (1, 0, 12))(None)
     return input_grad, weight_grad
 
 

time: 41.2 us -> 36.8 us (0.89)
  waiting for transfers between devices: 5.14 us -> 2.65 us
  starting transfers between devices: 12.5 us -> 11.6 us
  Pallas kernels: 22.5 us -> 21.6 us
    ppermute x8 -> x7, waiting for transfers between devices: 5.14 us -> 2.64 us  [exchange(): return lax.ppermute(value, axis, pairs)]
    pallas_call x7 -> x5, Pallas kernels: 10.1 us -> 9.15 us  [the longest x2 8.1 us: run(): call((lambda m, w, x_, z, *refs: dgrad_kernel(pieces, m, w, x_, z, None,...]
    ppermute x8 -> x7, starting transfers between devices: 8.03 us -> 7.12 us  [exchange(): return lax.ppermute(value, axis, pairs)]
  transfers between devices with their start and end apart: 9 -> 8, of which waited for: 4 -> 3; matrix products, arithmetic and copies ran while one was open for 0% -> 0% of each run, Pallas kernels for 43% -> 46%
where the time goes in v4:
time: 36.8 us; the launch traced here: 36.7 us
  Pallas kernels  21.6 us (59%)
  starting transfers between devices  11.6 us (32%)
  waiting for transfers between devices  2.65 us (7%)
  between operations  0.79 us (2%)
    pallas_call x2, Pallas kernels, run(): call((lambda m, w, x_, z, *refs: dgrad_kernel(pieces, m, w, x_, z, None,...  8.1 us
    ppermute x7, starting transfers between devices, exchange(): return lax.ppermute(value, axis, pairs)  7.12 us
    pallas_call x1, Pallas kernels, on_device(): call(first_kernel, 'first', [VMEM] * 5, [((2, EXT * PLANE, 9 * C), BF, FI...  5.95 us
    ppermute x1, starting transfers between devices, on_device(): lax.ppermute(jnp.concatenate([mine, other[MINE:]], axis=0), ('space', 'su...  4.45 us
    ppermute x7, waiting for transfers between devices, exchange(): return lax.ppermute(value, axis, pairs)  2.64 us
    pallas_call x1, Pallas kernels, on_device(): call(prep_kernel, 'prep', [HBM] * 4, [((BSIDE, PLANE, 2 * C), BF, VMEM),...  2.02 us
    pallas_call x1, Pallas kernels, on_device(): call(tilt_kernel if custom else lambda *refs: tilt_kernel(*refs, refs[7])...  1.82 us
    pallas_call x1, Pallas kernels, on_device(): call(features_kernel, 'features', [VMEM] * 2 + [HBM], [((2, (EXT + 2) * P...  1.64 us
  transfers between devices with their start and end apart: 8, of which 3 were waited for; matrix products, arithmetic and copies ran while one was open for 0% of the time, Pallas kernels for 46%

profile of v4, /device:TPU:0, one launch (start us, length us, event | category | flops | bytes accessed | tf_op | source)
XLA Modules:
  0.0 36.7 jit_solution(14779679001801933679)
XLA Ops:
  0.6 0.0 copy-start.2
  0.6 2.0 %prep.1 = (bf16[12,144,256]{2,1,0:T(8,128)(2,1)S(1)}, bf16[560,256]{1,0:T(8,128)(2,1)S(1)}, bf16[208,256]{1,0:T(8,128)(2,1)S(1)}, bf16[1792,256]{1,0:T(8,128)(2,1)S(1)}, bf16[64,144]{1,0:T(8,128)(2,1)S(1)}) custom-call(s32[2,6]{1,0:T(2,128)} %nb_hbm.1, s32[2,1728]{1,0:T(2,128)} %act_hbm.1, bf16[64,144]{1,0:T(8,128)(2,1)} %constant.6.clone.strips_hbm, ...), custom_call_target="tpu_custom_call" | custom-call | tf_op jit(solution)/shard_map/prep/pallas_call | solution.py:420
  2.7 0.5 %collective-permute-start = (bf16[560,256]{1,0:T(8,128)(2,1)S(1)}, bf16[560,256]{1,0:T(8,128)(2,1)S(1)}, u32[]{:S(2)}, u32[]{:S(2)}) collective-permute-start(bf16[560,256]{1,0:T(8,128)(2,1)S(1)} %get-tuple-element.30.own), channel_id=1, source_target_pairs={{0,1},{1,0},{2,3},{3,2},{4,5},{5,4},{6,7},{7,6},{8,9},{9,8},{10,11... | collective-permute-start | bytes 860168 | tf_op jit(solution)/shard_map/ppermute | solution.py:394
  3.2 1.6 %features.1 = (bf16[2,2304,128]{2,1,0:T(8,128)(2,1)S(1)}, bf16[2,256,256]{2,1,0:T(8,128)(2,1)S(1)}) custom-call(bf16[1792,256]{1,0:T(8,128)(2,1)S(1)} %get-tuple-element.33.mask.m.refs_0_, bf16[64,144]{1,0:T(8,128)(2,1)S(1)} %get-tuple-element.34.strips, bf16[2,1728,128]{2,1,0:T(8,128)(2,1)} %f_hbm.1), custom_call_target="tpu_custom_call" | custom-call | flops 10000000 | bytes 1000000 | tf_op jit(solution)/shard_map/features/pallas_call | solution.py:440
  4.8 0.0 collective-permute-done.other
  4.9 4.5 %collective-permute-start.1 = (bf16[416,256]{1,0:T(8,128)(2,1)S(1)}, bf16[416,256]{1,0:T(8,128)(2,1)S(1)}, u32[]{:S(2)}, u32[]{:S(2)}) collective-permute-start(bf16[416,256]{1,0:T(8,128)(2,1)S(1)} %pad_maximum_fusion), channel_id=1, source_target_pairs={{0,2},{2,4},{4,6},{6,8},{8,10},{10,12},{12,14},{3,1},{5,3},{7,5},{... | collective-permute-start | bytes 638984 | tf_op jit(solution)/shard_map/ppermute | solution.py:451
  9.3 0.0 copy-done.2
  9.4 5.9 %first.1 = (bf16[2,2016,1152]{2,1,0:T(8,128)(2,1)S(1)}, f32[384,1152]{1,0:T(8,128)S(1)}) custom-call(bf16[1296,256]{1,0:T(8,128)(2,1)S(1)} %copy-done.2, bf16[12,144,256]{2,1,0:T(8,128)(2,1)S(1)} %get-tuple-element.32.gm, bf16[560,256]{1,0:T(8,128)(2,1)S(1)} %get-tuple-element.30.own, bf16[560,256]{1,0:T(8,128)(2,1)S(1)} %collective-permute-done.other, ...), custom_call_target="tpu_custom_call" | custom-call | flops 3567255552 | bytes 8388608 | tf_op jit(solution)/shard_map/first/pallas_call | solution.py:455
  15.3 0.0 collective-permute-done.1.got
  15.3 0.1 collective-permute-start.2
  15.4 0.0 copy-start.1
  15.4 1.0 %second.1.acc = f32[384,1152]{1,0:T(8,128)S(1)} custom-call(bf16[2,2304,128]{2,1,0:T(8,128)(2,1)S(1)} %get-tuple-element.35.pad, bf16[2,2016,1152]{2,1,0:T(8,128)(2,1)S(1)} %get-tuple-element.39.x.x_.refs_2_, f32[384,1152]{1,0:T(8,128)S(1)} %get-tuple-element.40.before), custom_call_target="tpu_custom_call" | custom-call | flops 1783627776 | bytes 4194304 | tf_op jit(solution)/shard_map/second/pallas_call | solution.py:467
  16.4 0.4 %collective-permute-done.2.got2 = bf16[416,256]{1,0:T(8,128)(2,1)S(1)} collective-permute-done((bf16[416,256]{1,0:T(8,128)(2,1)S(1)}, bf16[416,256]{1,0:T(8,128)(2,1)S(1)}, u32[]{:S(2)}, u32[]{:S(2)}) %collective-permute-start.2) | collective-permute-done | bytes 213024 | tf_op jit(solution)/shard_map/ppermute | solution.py:394
  16.9 0.0 copy-done.1
  16.9 0.0 copy-start
  16.9 1.8 %tilt.1 = (f32[8,216,128]{2,1,0:T(8,128)S(1)}, s16[8,224,128]{2,1,0:T(8,128)(2,1)S(1)}, bf16[2,2,224,384]{3,2,1,0:T(8,128)(2,1)S(1)}) custom-call(bf16[560,256]{1,0:T(8,128)(2,1)S(1)} %get-tuple-element.30.own, bf16[416,256]{1,0:T(8,128)(2,1)S(1)} %collective-permute-done.1.got, bf16[416,256]{1,0:T(8,128)(2,1)S(1)} %collective-permute-done.2.got2, ...), custom_call_target="tpu_custom_call" | custom-call | flops 445906944 | bytes 4194304 | tf_op jit(solution)/shard_map/tilt/pallas_call | solution.py:482
  18.7 0.2 collective-permute-start.3
  18.9 1.6 %collective-permute-done.3.got = s16[8,224,128]{2,1,0:T(8,128)(2,1)S(1)} collective-permute-done((s16[8,224,128]{2,1,0:T(8,128)(2,1)S(1)}, s16[8,224,128]{2,1,0:T(8,128)(2,1)S(1)}, u32[]{:S(2)}, u32[]{:S(2)}) %collective-permute-start.3) | collective-permute-done | bytes 458784 | tf_op jit(solution)/shard_map/ppermute | solution.py:394
  20.6 0.3 blocks.1
  20.8 2.1 %collective-permute-start.4 = (s16[2,224,128]{2,1,0:T(8,128)(2,1)S(1)}, s16[2,224,128]{2,1,0:T(8,128)(2,1)S(1)}, u32[]{:S(2)}, u32[]{:S(2)}) collective-permute-start(s16[2,224,128]{2,1,0:T(8,128)(2,1)S(1)} %get-tuple-element.46), channel_id=1, source_target_pairs={{0,2},{2,0},{4,6},{6,4},{8,10},{10,8},{12,14},{14,12},{1,3},{3,1},... | collective-permute-start | bytes 344072 | tf_op jit(solution)/shard_map/ppermute | solution.py:394
  23.0 1.6 %collective-permute-start.5 = (s16[2,224,128]{2,1,0:T(8,128)(2,1)S(1)}, s16[2,224,128]{2,1,0:T(8,128)(2,1)S(1)}, u32[]{:S(2)}, u32[]{:S(2)}) collective-permute-start(s16[2,224,128]{2,1,0:T(8,128)(2,1)S(1)} %get-tuple-element.47), channel_id=1, source_target_pairs={{0,4},{2,6},{4,0},{6,2},{8,12},{10,14},{12,8},{14,10},{1,5},{3,7},... | collective-permute-start | bytes 344072 | tf_op jit(solution)/shard_map/ppermute | solution.py:394
  24.5 0.0 collective-permute-start.6
  24.5 0.0 copy-done
  24.5 5.1 %dgrad.2.refs_4_ = bf16[2,1728,128]{2,1,0:T(8,128)(2,1)} custom-call(bf16[1792,256]{1,0:T(8,128)(2,1)S(1)} %get-tuple-element.33.mask.m.refs_0_, bf16[27,128,128]{2,1,0:T(8,128)(2,1)S(1)} %copy-done, bf16[2,2016,1152]{2,1,0:T(8,128)(2,1)S(1)} %get-tuple-element.39.x.x_.refs_2_, bf16[2,2,224,384]{3,2,1,0:T(8,128)(2,1)S(1)} %get-tuple-element.49.z.refs_3_), custom_call_target="tpu_custom_call" | custom-call | flops 2378170368 | bytes 4194304 | tf_op jit(solution)/shard_map/dgrad/pallas_call | solution.py:501
  29.6 0.0 collective-permute-done.4.got_y
  29.6 0.0 collective-permute-done.5.got_z
  29.7 0.6 %collective-permute-done.6.got_yz = s16[2,224,128]{2,1,0:T(8,128)(2,1)S(1)} collective-permute-done((s16[2,224,128]{2,1,0:T(8,128)(2,1)S(1)}, s16[2,224,128]{2,1,0:T(8,128)(2,1)S(1)}, u32[]{:S(2)}, u32[]{:S(2)}) %collective-permute-start.6) | collective-permute-done | bytes 114720 | tf_op jit(solution)/shard_map/ppermute | solution.py:394
  30.2 0.1 last.1
  30.4 2.6 %collective-permute-start.7 = (s16[224,128]{1,0:T(8,128)(2,1)S(1)}, s16[224,128]{1,0:T(8,128)(2,1)S(1)}, u32[]{:S(2)}, u32[]{:S(2)}) collective-permute-start(s16[224,128]{1,0:T(8,128)(2,1)S(1)} %get-tuple-element.53), channel_id=1, source_target_pairs={{0,8},{2,10},{4,12},{6,14},{8,0},{10,2},{12,4},{14,6},{1,9},{3,11}... | collective-permute-start | bytes 172040 | tf_op jit(solution)/shard_map/ppermute | solution.py:394
  32.9 3.0 %dgrad.3 = bf16[2,1728,128]{2,1,0:T(8,128)(2,1)} custom-call(bf16[1792,256]{1,0:T(8,128)(2,1)S(1)} %get-tuple-element.33.mask.m.refs_0_, bf16[27,128,128]{2,1,0:T(8,128)(2,1)S(1)} %copy-done, bf16[2,2016,1152]{2,1,0:T(8,128)(2,1)S(1)} %get-tuple-element.39.x.x_.refs_2_, ...), custom_call_target="tpu_custom_call", output_to_operand_aliasing={{}: (4, {})} | custom-call | flops 1189085184 | bytes 4194304 | tf_op jit(solution)/shard_map/dgrad/pallas_call | solution.py:501
  36.0 0.0 collective-permute-done.7.got
  36.0 0.7 %sum.1 = f32[216,128]{1,0:T(8,128)} custom-call(f32[216,128]{1,0:T(8,128)S(1)} %get-tuple-element.56.keep, s16[224,128]{1,0:T(8,128)(2,1)S(1)} %collective-permute-done.7.got), custom_call_target="tpu_custom_call" | custom-call | tf_op jit(solution)/shard_map/sum/pallas_call | solution.py:413
  (2 shorter events, 0.0 us)
Async XLA Ops:
  0.6 8.7 %copy-start.2 = (bf16[1296,256]{1,0:T(8,128)(2,1)S(1)}, bf16[1296,256]{1,0:T(8,128)(2,1)}, u32[]{:S(2)}) copy-start(bf16[1296,256]{1,0:T(8,128)(2,1)} %constant.7.clone.shift) | copy-start | bytes 1990660
  2.7 2.2 %collective-permute-start = (bf16[560,256]{1,0:T(8,128)(2,1)S(1)}, bf16[560,256]{1,0:T(8,128)(2,1)S(1)}, u32[]{:S(2)}, u32[]{:S(2)}) collective-permute-start(bf16[560,256]{1,0:T(8,128)(2,1)S(1)} %get-tuple-element.30.own), channel_id=1, source_target_pairs={{0,1},{1,0},{2,3},{3,2},{4,5},{5,4},{6,7},{7,6},{8,9},{9,8},{10,11... | collective-permute-start | bytes 860168 | tf_op jit(solution)/shard_map/ppermute | solution.py:394
  4.9 10.4 %collective-permute-start.1 = (bf16[416,256]{1,0:T(8,128)(2,1)S(1)}, bf16[416,256]{1,0:T(8,128)(2,1)S(1)}, u32[]{:S(2)}, u32[]{:S(2)}) collective-permute-start(bf16[416,256]{1,0:T(8,128)(2,1)S(1)} %pad_maximum_fusion), channel_id=1, source_target_pairs={{0,2},{2,4},{4,6},{6,8},{8,10},{10,12},{12,14},{3,1},{5,3},{7,5},{... | collective-permute-start | bytes 638984 | tf_op jit(solution)/shard_map/ppermute | solution.py:451
  15.3 1.5 %collective-permute-start.2 = (bf16[416,256]{1,0:T(8,128)(2,1)S(1)}, bf16[416,256]{1,0:T(8,128)(2,1)S(1)}, u32[]{:S(2)}, u32[]{:S(2)}) collective-permute-start(bf16[416,256]{1,0:T(8,128)(2,1)S(1)} %collective-permute-done.1.got), channel_id=1, source_target_pairs={{0,1},{1,0},{2,3},{3,2},{4,5},{5,4},{6,7},{7,6},{8,9},{9,8},{10,11... | collective-permute-start | bytes 638984 | tf_op jit(solution)/shard_map/ppermute | solution.py:394
  15.4 1.5 %copy-start.1 = (bf16[672,224]{1,0:T(8,128)(2,1)S(1)}, bf16[672,224]{1,0:T(8,128)(2,1)}, u32[]{:S(2)}) copy-start(bf16[672,224]{1,0:T(8,128)(2,1)} %constant.8.clone.bands) | copy-start | bytes 903172
  16.9 7.7 %copy-start = (bf16[27,128,128]{2,1,0:T(8,128)(2,1)S(1)}, bf16[27,128,128]{2,1,0:T(8,128)(2,1)}, u32[]{:S(2)}) copy-start(bf16[27,128,128]{2,1,0:T(8,128)(2,1)} %refs_1_.1) | copy-start | bytes 2654212
  18.7 1.9 %collective-permute-start.3 = (s16[8,224,128]{2,1,0:T(8,128)(2,1)S(1)}, s16[8,224,128]{2,1,0:T(8,128)(2,1)S(1)}, u32[]{:S(2)}, u32[]{:S(2)}) collective-permute-start(s16[8,224,128]{2,1,0:T(8,128)(2,1)S(1)} %get-tuple-element.42), channel_id=1, source_target_pairs={{0,1},{1,0},{2,3},{3,2},{4,5},{5,4},{6,7},{7,6},{8,9},{9,8},{10,11... | collective-permute-start | bytes 1376264 | tf_op jit(solution)/shard_map/ppermute | solution.py:394
  20.8 8.8 %collective-permute-start.4 = (s16[2,224,128]{2,1,0:T(8,128)(2,1)S(1)}, s16[2,224,128]{2,1,0:T(8,128)(2,1)S(1)}, u32[]{:S(2)}, u32[]{:S(2)}) collective-permute-start(s16[2,224,128]{2,1,0:T(8,128)(2,1)S(1)} %get-tuple-element.46), channel_id=1, source_target_pairs={{0,2},{2,0},{4,6},{6,4},{8,10},{10,8},{12,14},{14,12},{1,3},{3,1},... | collective-permute-start | bytes 344072 | tf_op jit(solution)/shard_map/ppermute | solution.py:394
  23.0 6.7 %collective-permute-start.5 = (s16[2,224,128]{2,1,0:T(8,128)(2,1)S(1)}, s16[2,224,128]{2,1,0:T(8,128)(2,1)S(1)}, u32[]{:S(2)}, u32[]{:S(2)}) collective-permute-start(s16[2,224,128]{2,1,0:T(8,128)(2,1)S(1)} %get-tuple-element.47), channel_id=1, source_target_pairs={{0,4},{2,6},{4,0},{6,2},{8,12},{10,14},{12,8},{14,10},{1,5},{3,7},... | collective-permute-start | bytes 344072 | tf_op jit(solution)/shard_map/ppermute | solution.py:394
  24.5 5.7 %collective-permute-start.6 = (s16[2,224,128]{2,1,0:T(8,128)(2,1)S(1)}, s16[2,224,128]{2,1,0:T(8,128)(2,1)S(1)}, u32[]{:S(2)}, u32[]{:S(2)}) collective-permute-start(s16[2,224,128]{2,1,0:T(8,128)(2,1)S(1)} %get-tuple-element.48), channel_id=1, source_target_pairs={{0,6},{2,4},{4,2},{6,0},{8,14},{10,12},{12,10},{14,8},{1,7},{3,5},... | collective-permute-start | bytes 344072 | tf_op jit(solution)/shard_map/ppermute | solution.py:394
  30.4 5.6 %collective-permute-start.7 = (s16[224,128]{1,0:T(8,128)(2,1)S(1)}, s16[224,128]{1,0:T(8,128)(2,1)S(1)}, u32[]{:S(2)}, u32[]{:S(2)}) collective-permute-start(s16[224,128]{1,0:T(8,128)(2,1)S(1)} %get-tuple-element.53), channel_id=1, source_target_pairs={{0,8},{2,10},{4,12},{6,14},{8,0},{10,2},{12,4},{14,6},{1,9},{3,11}... | collective-permute-start | bytes 172040 | tf_op jit(solution)/shard_map/ppermute | solution.py:394

commit v5 on v4

--- a/solution.py
+++ b/solution.py
@@ -12,7 +12,6 @@
 EXT = BSIDE + 2
 C = 128
 KROWS = 256
-EARLY = 9
 MINE = PLANE + 208
 BF = jnp.bfloat16
 F32 = jnp.float32
@@ -107,6 +106,7 @@
     code = (2 * a0 + b0).astype(BF)
     a0, b0 = a0.astype(BF), b0.astype(BF)
     second = jnp.full((16, 2 * C), lax.axis_index("sub").astype(F32), F32).astype(BF)
+    row14 = jnp.where(lax.broadcasted_iota(jnp.int32, (16, 2 * C), 0) == 14, 1.0, 0.0).astype(BF)
     loads[1].wait()
     for p in range(BSIDE):
         if p % 3 == 0:
@@ -115,35 +115,37 @@
         plane = jnp.concatenate([g[0, rows, :], g[1, rows, :]], axis=1) * mask[rows, :]
         gm[p] = plane
         s = dot(strips[...], plane).astype(BF)
-        mine[pl.ds(p * 16, 16), :] = s[0:16] * second + s[16:32] * (1 - second)
-        message[pl.ds(MINE + p * 16, 16), :] = s[16:32] * second + s[0:16] * (1 - second)
+        here, there = s[0:16] * second + s[16:32] * (1 - second), s[16:32] * second + s[0:16] * (1 - second)
+        if p == 0:
+            here, there = here + code * row14, there + code * row14
+        mine[pl.ds(p * 16, 16), :] = here
+        message[pl.ds(MINE + p * 16, 16), :] = there
         message[pl.ds(PLANE + p * 16, 16), :] = s[32:48] * b0 + s[48:64] * (1 - b0)
     for r in range(0, PLANE, 16):
         message[pl.ds(r, 16), :] = gm[0, pl.ds(r, 16), :] * a0 + gm[11, pl.ds(r, 16), :] * (1 - a0)
     message[pl.ds(PLANE + 192, 16), :] = code
-    message[pl.ds(MINE + 192, 16), :] = code
-    mine[pl.ds(192, 16), :] = code
-
-
-def features_kernel(mask, strips, f_hbm, pad, fs, f, sem):
+
+
+def features_kernel(mask, strips, f_hbm, pad, strip, strip_send, f, sem):
     load = pltpu.make_async_copy(f_hbm, f, sem)
     load.start()
     zero = jnp.zeros((2 * PLANE, C), BF)
     edge = jnp.zeros((32, 2 * C), BF)
+    second = jnp.full((16, 2 * C), lax.axis_index("sub").astype(F32), F32).astype(BF)
     for j in range(2):
         pad[j, pl.ds(0, 2 * PLANE), :] = zero
         pad[j, pl.ds(EXT * PLANE, 2 * PLANE), :] = zero
+    for ref in (strip, strip_send):
+        ref[pl.ds(0, 32), :] = edge
+        ref[pl.ds(EXT * 16, 32), :] = edge
     load.wait()
     for j in range(2):
         pad[j, pl.ds(2 * PLANE, VOX), :] = f[j] * mask[pl.ds(0, VOX), pl.ds(j * C, C)]
-    for n in range(2):
-        fs[n, pl.ds(0, 32), :] = edge
-        fs[n, pl.ds(EXT * 16, 32), :] = edge
     for p in range(BSIDE):
         rows = pl.ds((p + 2) * PLANE, PLANE)
         s = dot(strips[pl.ds(0, 32), :], jnp.concatenate([pad[0, rows, :], pad[1, rows, :]], axis=1)).astype(BF)
-        for n in range(2):
-            fs[n, pl.ds((p + 2) * 16, 16), :] = s[16 * n : 16 * n + 16]
+        strip[pl.ds((p + 2) * 16, 16), :] = s[0:16] * (1 - second) + s[16:32] * second
+        strip_send[pl.ds((p + 2) * 16, 16), :] = s[0:16] * second + s[16:32] * (1 - second)
 
 
 def position(own):
@@ -156,7 +158,8 @@
 def candidates(refs, at):
     tiles = []
     for ref, base, swapped in refs:
-        t = ref[pl.ds(base + at, 16), :].astype(F32)
+        t = ref[pl.ds(base + at // 16 * 16, 16), :].astype(F32)
+        t = jnp.broadcast_to(t[at % 16 : at % 16 + 1], (16, 2 * C))
         tiles.append(((ref, base, swapped), halves(t) if swapped else t))
     return tiles
 
@@ -189,46 +192,47 @@
         kop[p + 1, pl.ds(144, 16), :] = side * b0h
         kop[p + 1, pl.ds(160, 16), :] = side * b1h
         kop[p + 1, pl.ds(176, KROWS - 176), :] = rest
-    for at, plane, w in ((0, 11, a0h), (EXT - 1, 0, a1h)):
-        for r in range(0, PLANE, 16):
-            kop[at, pl.ds(r, 16), :] = gather(pick_a, r) * w
-        side = gather(pick_d, PLANE + plane * 16) * w
-        kop[at, pl.ds(144, 16), :] = side * b0h
-        kop[at, pl.ds(160, 16), :] = side * b1h
-        kop[at, pl.ds(176, KROWS - 176), :] = rest
-
-
-def vertical_operands(own, zs, z):
-    code, a0, b0 = position(own)
+    for r in range(0, PLANE, 16):
+        kop[0, pl.ds(r, 16), :] = gather(pick_a, r)
+    side = gather(pick_d, PLANE + 176) * a0h + gather(pick_d, PLANE) * a1h
+    kop[0, pl.ds(144, 16), :] = side * b0h
+    kop[0, pl.ds(160, 16), :] = side * b1h
+    kop[0, pl.ds(176, KROWS - 176), :] = rest
+    return a0h, a1h
+
+
+def facing_plane(message, got, z):
+    code, a0, b0 = position(message)
     row16 = lax.broadcasted_iota(jnp.int32, (16, 2 * C), 0)
     inner = jnp.where(row16 < 12, 1.0, 0.0).astype(BF)
     edge = jnp.where(row16 == 12, 1 - b0, jnp.where(row16 == 13, b0, 0.0)).astype(BF)
     a0h = a0.astype(BF)
-    for n, ref in enumerate(zs):
-        cands = candidates([(ref, base, swapped) for base in (0, 208) for swapped in (False, True)], 192)
-        near = [(*q, w * inner) for *q, w in hits(cands, code)]
-        near += [(*q, w * edge) for *q, w in hits(cands, code + 1 - 2 * b0)]
-        far = [(*q, w * inner) for *q, w in hits(cands, code + 2 - 4 * a0)]
-        far += [(*q, w * edge) for *q, w in hits(cands, 3 - code)]
-        for p in range(BSIDE):
-            z[n, pl.ds((p + 1) * 16, 16), :] = gather(near, p * 16)
-        z[n, pl.ds(0, 16), :] = gather(far, 11 * 16) * a0h
-        z[n, pl.ds((EXT - 1) * 16, 16), :] = gather(far, 0) * (1 - a0h)
-
-
-def shifted(shift, kop, x, ks, first, count):
-    for p in range(count):
-        for n, k in enumerate(ks):
+    cands = candidates([(got, base, swapped) for base in (0, 192) for swapped in (False, True)], 14)
+    near = [(*q, w * inner) for *q, w in hits(cands, code)]
+    near += [(*q, w * edge) for *q, w in hits(cands, code + 1 - 2 * b0)]
+    far = [(*q, w * inner) for *q, w in hits(cands, code + 2 - 4 * a0)]
+    far += [(*q, w * edge) for *q, w in hits(cands, 3 - code)]
+    for p in range(BSIDE):
+        z[pl.ds((p + 1) * 16, 16), :] = gather(near, p * 16)
+    z[pl.ds(0, 16), :] = gather(far, 11 * 16) * a0h
+    z[pl.ds((EXT - 1) * 16, 16), :] = gather(far, 0) * (1 - a0h)
+
+
+def shifted(shift, kop, x, ends):
+    for p in range(EXT - 1):
+        for k in range(9):
             if k == 4:
-                y = kop[first + p, pl.ds(0, PLANE), :]
+                y = kop[p, pl.ds(0, PLANE), :]
             else:
-                y = dot(shift[pl.ds(k * PLANE, PLANE), :], kop[first + p]).astype(BF)
-            for j in range(2):
-                x[j, pl.ds(p * PLANE, PLANE), pl.ds(n * C, C)] = y[:, j * C : j * C + C]
-
-
-def stacked(ref, j, first, count):
-    return jnp.concatenate([ref[j, pl.ds((d + first) * PLANE, count * PLANE), :] for d in range(3)], axis=1)
+                y = dot(shift[pl.ds(k * PLANE, PLANE), :], kop[p]).astype(BF)
+            for at in (p,) if p else (0, EXT - 1):
+                v = y if p else y * ends[1 if at else 0]
+                for j in range(2):
+                    x[j, pl.ds(at * PLANE, PLANE), pl.ds(k * C, C)] = v[:, j * C : j * C + C]
+
+
+def stacked(ref, j):
+    return jnp.concatenate([ref[j, pl.ds(d * PLANE, EXT * PLANE), :] for d in range(3)], axis=1)
 
 
 def dot_rows(a, b):
@@ -236,15 +240,10 @@
 
 
 def first_kernel(shift, gm, own, other, pad, x, acc, kop):
-    layer_operands(gm, own, other, kop)
-    shifted(shift, kop, x, range(9), 0, EXT)
-    acc[...] = dot_rows(stacked(pad, 0, 0, EXT), x[0])
-    acc[...] += dot_rows(stacked(pad, 1, 0, EARLY), x[1, pl.ds(0, EARLY * PLANE), :])
-
-
-def second_kernel(pad, x, before, acc):
-    late = EXT - EARLY
-    acc[...] = before[...] + dot_rows(stacked(pad, 1, EARLY, late), x[1, pl.ds(EARLY * PLANE, late * PLANE), :])
+    ends = [jnp.concatenate([w] * (PLANE // 16), axis=0) for w in layer_operands(gm, own, other, kop)]
+    shifted(shift, kop, x, ends)
+    acc[...] = dot_rows(stacked(pad, 0), x[0])
+    acc[...] += dot_rows(stacked(pad, 1), x[1])
 
 
 def encode(ref, at, v):
@@ -260,25 +259,20 @@
     return v[:rows] * jnp.exp2(v[rows : rows + 1])
 
 
-def tilt_kernel(own, got, got2, fs, bands, acc, keep, code, zs, z, more, send):
+def tilt_kernel(own, other, got, strip, strip_other, bands, acc, keep, code, zs, zs_send, z, more, send):
     sub = lax.axis_index("sub")
-    for parity in range(2):
-
-        @pl.when(sub == parity)
-        def _(parity=parity):
-            vertical_operands(own, (got2, got) if parity else (got, got2), z)
-
-    for n in range(2):
+    rows = EXT * 16
+    total = None
+    for n, (message, features, out) in enumerate(((own, strip, zs), (other, strip_other, zs_send))):
+        facing_plane(message, got, z.at[n])
         v = dot(bands[...], z[n]).astype(BF)
-        rows = EXT * 16
-        total = None
         for j in range(2):
             lanes = slice(j * C, j * C + C)
-            zs[n, j] = jnp.concatenate([v[q * rows : q * rows + rows, lanes] for q in range(3)], axis=1)
-            f3 = jnp.concatenate([fs[n, pl.ds(d * 16, rows), lanes] for d in range(3)], axis=1)
-            part_ = dot_rows(f3, zs[n, j])
-            total = part_ if total is None else total + part_
-        more[n] = total
+            out[j] = jnp.concatenate([v[q * rows : q * rows + rows, lanes] for q in range(3)], axis=1)
+            f3 = jnp.concatenate([features[pl.ds(d * 16, rows), lanes] for d in range(3)], axis=1)
+            term = dot_rows(f3, out[j])
+            total = term if total is None else total + term
+    more[...] = total
     size = keep.shape[1]
     for parity in range(2):
 
@@ -292,8 +286,8 @@
                     end = min((block + 1) * size, (t + 1) * C)
                     at = pl.ds(da * C + row - t * C, end - row)
                     v = acc[at, pl.ds(k * C, C)]
-                    if k % 3 != 1:
-                        v = v + more[0 if k % 3 == 2 else 1, at, pl.ds(k // 3 * C, C)]
+                    if k % 3 == 2 - 2 * parity:
+                        v = v + more[at, pl.ds(k // 3 * C, C)]
                     ref = keep if block % 2 == parity else send
                     ref[block // 2, pl.ds(row - block * size, end - row), :] = v * (1.0 / VOX)
                     row = end
@@ -314,15 +308,17 @@
     return total + y[pl.ds(p * rows, rows), pl.ds(2 * C, C)]
 
 
-def dgrad_kernel(pieces, mask, w, x, zs, before, out, y, yz, plane, res, sem):
+def dgrad_kernel(pieces, mask, w, x, zs, zs_got, before, out, y, yz, plane, res, sem):
     del before
+    core = lax.axis_index("sub")
     stores = []
     for j, first, count in pieces:
         rows = pl.ds(0, (count + 2) * PLANE)
         y[rows, :] = dot_t(x[j, pl.ds(first * PLANE, (count + 2) * PLANE), :], columns(w, range(9)))
+        at = pl.ds(first * 16, (count + 2) * 16)
         for n in range(2):
-            faces = dot_t(zs[n, j, pl.ds(first * 16, (count + 2) * 16), :], columns(w, (2, 5, 8) if n == 0 else (0, 3, 6)))
-            yz[n, pl.ds(0, (count + 2) * 16), :] = faces
+            faces = jnp.where(core == n, zs[j, at, :], zs_got[j, at, :])
+            yz[n, pl.ds(0, (count + 2) * 16), :] = dot_t(faces, columns(w, (2, 5, 8) if n == 0 else (0, 3, 6)))
         for p in range(count):
             plane[pl.ds(0, PLANE), :] = joined(y, p, PLANE)
             for n in range(2):
@@ -423,8 +419,8 @@
         [HBM] * 4,
         [
             ((BSIDE, PLANE, 2 * C), BF, VMEM),
-            ((MINE + 208, 2 * C), BF, VMEM),
-            ((208, 2 * C), BF, VMEM),
+            ((MINE + 192, 2 * C), BF, VMEM),
+            ((192, 2 * C), BF, VMEM),
             ((14 * C, 2 * C), BF, VMEM),
             ((64, PLANE), BF, VMEM),
         ],
@@ -437,11 +433,11 @@
     )(in_hbm(neighbours), in_hbm(active), in_hbm(strips), in_hbm(out_grad))
 
     other = exchange(own, "sub", 1)
-    pad, fs = call(
+    pad, strip, strip_send = call(
         features_kernel,
         "features",
         [VMEM] * 2 + [HBM],
-        [((2, (EXT + 2) * PLANE, C), BF, VMEM), ((2, (EXT + 2) * 16, 2 * C), BF, VMEM)],
+        [((2, (EXT + 2) * PLANE, C), BF, VMEM)] + [(((EXT + 2) * 16, 2 * C), BF, VMEM)] * 2,
         [pltpu.VMEM((2, VOX, C), BF), pltpu.SemaphoreType.DMA],
         flops=10**7,
         size=10**6,
@@ -450,7 +446,9 @@
     ways = [(2 * i, 2 * i + 2) for i in range(layers - 1)] + [(2 * i + 3, 2 * i + 1) for i in range(layers - 1)]
     got = lax.ppermute(jnp.concatenate([mine, other[MINE:]], axis=0), ("space", "sub"), ways)
 
-    kop_shape = (EXT, KROWS, 2 * C)
+    strip_other = exchange(strip_send, "sub", 1)
+
+    kop_shape = (EXT - 1, KROWS, 2 * C)
     work = 2 * 3 * C * 9 * C * EXT * PLANE
     x, acc = call(
         first_kernel,
@@ -462,48 +460,41 @@
         size=8 * 2**20,
         limit=6,
     )(shift, gm, own, other, pad)
-    got, acc = tied(got, acc)
-    got2 = exchange(got, "sub", 1)
-    (acc,) = call(
-        second_kernel,
-        "second",
-        [VMEM, VMEM, VMEM],
-        [((3 * C, 9 * C), F32, VMEM)],
-        flops=work,
-        size=4 * 2**20,
-    )(pad, x, acc)
-
     size = 27 * C // (2 * layers)
     custom = layers == 8
     rows = (layers, size, C) if custom else (8, 216, C)
     exact = (rows, F32, VMEM)
-    tilt_ins = (own, got, got2, fs, bands, acc)
-    tilt_scratch = [pltpu.VMEM((2, EXT * 16, 2 * C), BF), pltpu.VMEM((2, 3 * C, 3 * C), F32)]
-    keep, send, zs = call(
-        tilt_kernel if custom else (lambda *refs: tilt_kernel(*refs, refs[7])),
+    tilt_ins = (own, other, got, strip, strip_other, bands, acc)
+    tilt_scratch = [pltpu.VMEM((2, EXT * 16, 2 * C), BF), pltpu.VMEM((3 * C, 3 * C), F32)]
+    keep, send, zs, zs_send = call(
+        tilt_kernel if custom else (lambda *refs: tilt_kernel(*refs, refs[8])),
         "tilt",
-        [VMEM] * 6,
+        [VMEM] * 7,
         [
             exact,
             ((layers, size + 8, C), jnp.int16, VMEM) if custom else exact,
-            ((2, 2, EXT * 16, 3 * C), BF, VMEM),
+            ((2, EXT * 16, 3 * C), BF, VMEM),
+            ((2, EXT * 16, 3 * C), BF, VMEM),
         ],
         tilt_scratch + ([pltpu.VMEM(rows, F32)] if custom else []),
         flops=work // 4,
         size=4 * 2**20,
     )(*tilt_ins)
 
+    got = exchange(send, "sub", 1) if custom else None
+    zs_got = exchange(zs_send, "sub", 1)
+
     def dgrad(*pieces):
         most = max(count for _, _, count in pieces) + 2
 
         def run(before):
             fresh = before is None
             return call(
-                (lambda m, w, x_, z, *refs: dgrad_kernel(pieces, m, w, x_, z, None, *refs))
+                (lambda *refs: dgrad_kernel(pieces, *refs[:5], None, *refs[5:]))
                 if fresh
                 else (lambda *refs: dgrad_kernel(pieces, *refs)),
                 "dgrad",
-                [VMEM] * 4 + ([] if fresh else [ANY]),
+                [VMEM] * 5 + ([] if fresh else [ANY]),
                 [((2, VOX, C), BF, ANY)],
                 [
                     pltpu.VMEM((most * PLANE, 3 * C), F32),
@@ -512,16 +503,15 @@
                     pltpu.VMEM((2, VOX, C), BF),
                     pltpu.SemaphoreType.DMA((12,)),
                 ],
-                aliases={} if fresh else {4: 0},
+                aliases={} if fresh else {5: 0},
                 flops=work * sum(count for _, _, count in pieces) // 12,
                 size=4 * 2**20,
                 limit=12,
-            )(mask, weight, x, zs, *(() if fresh else (before,)))[0]
+            )(mask, weight, x, zs, zs_got, *(() if fresh else (before,)))[0]
 
         return run
 
     if custom:
-        got = exchange(send, "sub", 1)
         got, zs = tied(got, zs)
         weight_grad, input_grad = reduce_blocks(keep, got, [dgrad((0, 0, 12), (1, 0, 4)), dgrad((1, 4, 8))])
     else:

time: 36.8 us -> 36 us (0.978)
  waiting for transfers between devices: 2.65 us -> 1.46 us
  starting transfers between devices: 11.6 us -> 12.3 us
    ppermute x7 -> x8, waiting for transfers between devices: 2.64 us -> 1.46 us  [exchange(): return lax.ppermute(value, axis, pairs)]
    pallas_call x4 -> x3, Pallas kernels: 10.9 us -> 10.2 us  [the longest x2 8.24 us: run(): call((lambda *refs: dgrad_kernel(pieces, *refs[:5], None, *refs[5:])) if...]
    ppermute x1, starting transfers between devices: 4.45 us -> 4.88 us  [on_device(): lax.ppermute(jnp.concatenate([mine, other[MINE:]], axis=0), ('space', 'su...]
    ppermute x7 -> x8, starting transfers between devices: 7.12 us -> 7.42 us  [exchange(): return lax.ppermute(value, axis, pairs)]
  transfers between devices with their start and end apart: 8 -> 9, of which waited for: 3 -> 2; matrix products, arithmetic and copies ran while one was open for 0% -> 0% of each run, Pallas kernels for 46% -> 46%
where the time goes in v5:
time: 36 us; the launch traced here: 35.9 us
  Pallas kernels  21.3 us (59%)
  starting transfers between devices  12.3 us (34%)
  waiting for transfers between devices  1.46 us (4%)
  between operations  0.8 us (2%)
    pallas_call x2, Pallas kernels, run(): call((lambda *refs: dgrad_kernel(pieces, *refs[:5], None, *refs[5:])) if...  8.24 us
    ppermute x8, starting transfers between devices, exchange(): return lax.ppermute(value, axis, pairs)  7.42 us
    pallas_call x1, Pallas kernels, on_device(): call(first_kernel, 'first', [VMEM] * 5, [((2, EXT * PLANE, 9 * C), BF, FI...  6.3 us
    ppermute x1, starting transfers between devices, on_device(): lax.ppermute(jnp.concatenate([mine, other[MINE:]], axis=0), ('space', 'su...  4.88 us
    pallas_call x1, Pallas kernels, on_device(): call(prep_kernel, 'prep', [HBM] * 4, [((BSIDE, PLANE, 2 * C), BF, VMEM),...  2.05 us
    pallas_call x1, Pallas kernels, on_device(): call(tilt_kernel if custom else lambda *refs: tilt_kernel(*refs, refs[8])...  1.94 us
    pallas_call x1, Pallas kernels, on_device(): call(features_kernel, 'features', [VMEM] * 2 + [HBM], [((2, (EXT + 2) * P...  1.68 us
    ppermute x8, waiting for transfers between devices, exchange(): return lax.ppermute(value, axis, pairs)  1.46 us
  transfers between devices with their start and end apart: 9, of which 2 were waited for; matrix products, arithmetic and copies ran while one was open for 0% of the time, Pallas kernels for 46%

profile of v5, /device:TPU:0, one launch (start us, length us, event | category | flops | bytes accessed | tf_op | source)
XLA Modules:
  0.0 35.9 jit_solution(8384803712332156904)
XLA Ops:
  0.6 0.0 copy-start.2
  0.6 2.1 %prep.1 = (bf16[12,144,256]{2,1,0:T(8,128)(2,1)S(1)}, bf16[544,256]{1,0:T(8,128)(2,1)S(1)}, bf16[192,256]{1,0:T(8,128)(2,1)S(1)}, bf16[1792,256]{1,0:T(8,128)(2,1)S(1)}, bf16[64,144]{1,0:T(8,128)(2,1)S(1)}) custom-call(s32[2,6]{1,0:T(2,128)} %nb_hbm.1, s32[2,1728]{1,0:T(2,128)} %act_hbm.1, bf16[64,144]{1,0:T(8,128)(2,1)} %constant.6.clone.strips_hbm, ...), custom_call_target="tpu_custom_call" | custom-call | tf_op jit(solution)/shard_map/prep/pallas_call | solution.py:416
  2.7 0.5 %collective-permute-start = (bf16[544,256]{1,0:T(8,128)(2,1)S(1)}, bf16[544,256]{1,0:T(8,128)(2,1)S(1)}, u32[]{:S(2)}, u32[]{:S(2)}) collective-permute-start(bf16[544,256]{1,0:T(8,128)(2,1)S(1)} %get-tuple-element.30.own), channel_id=1, source_target_pairs={{0,1},{1,0},{2,3},{3,2},{4,5},{5,4},{6,7},{7,6},{8,9},{9,8},{10,11... | collective-permute-start | bytes 835592 | tf_op jit(solution)/shard_map/ppermute | solution.py:390
  3.2 1.7 %features.1 = (bf16[2,2304,128]{2,1,0:T(8,128)(2,1)S(1)}, bf16[256,256]{1,0:T(8,128)(2,1)S(1)}, bf16[256,256]{1,0:T(8,128)(2,1)S(1)}) custom-call(bf16[1792,256]{1,0:T(8,128)(2,1)S(1)} %get-tuple-element.32.mask.refs_0_, bf16[64,144]{1,0:T(8,128)(2,1)S(1)} %get-tuple-element.33.strips, bf16[2,1728,128]{2,1,0:T(8,128)(2,1)} %f_hbm.1), custom_call_target="tpu_custom_call" | custom-call | flops 10000000 | bytes 1000000 | tf_op jit(solution)/shard_map/features/pallas_call | solution.py:436
  4.9 0.1 collective-permute-start.2
  5.0 0.0 collective-permute-done.other
  5.1 4.9 %collective-permute-start.1 = (bf16[384,256]{1,0:T(8,128)(2,1)S(1)}, bf16[384,256]{1,0:T(8,128)(2,1)S(1)}, u32[]{:S(2)}, u32[]{:S(2)}) collective-permute-start(bf16[384,256]{1,0:T(8,128)(2,1)S(1)} %pad_maximum_fusion), channel_id=1, source_target_pairs={{0,2},{2,4},{4,6},{6,8},{8,10},{10,12},{12,14},{3,1},{5,3},{7,5},{... | collective-permute-start | bytes 589832 | tf_op jit(solution)/shard_map/ppermute | solution.py:447
  10.0 0.0 copy-done.2
  10.0 0.0 copy-start.1
  10.0 6.3 %first.1 = (bf16[2,2016,1152]{2,1,0:T(8,128)(2,1)S(1)}, f32[384,1152]{1,0:T(8,128)S(1)}) custom-call(bf16[1296,256]{1,0:T(8,128)(2,1)S(1)} %copy-done.2, bf16[12,144,256]{2,1,0:T(8,128)(2,1)S(1)} %get-tuple-element.36.gm, bf16[544,256]{1,0:T(8,128)(2,1)S(1)} %get-tuple-element.30.own, bf16[544,256]{1,0:T(8,128)(2,1)S(1)} %collective-permute-done.other, ...), custom_call_target="tpu_custom_call" | custom-call | flops 3567255552 | bytes 8388608 | tf_op jit(solution)/shard_map/first/pallas_call | solution.py:453
  16.3 0.0 collective-permute-done.2.strip_other
  16.3 0.0 collective-permute-done.1.got
  16.3 0.0 copy-done.1
  16.3 0.0 copy-start
  16.3 1.9 %tilt.1 = (f32[8,216,128]{2,1,0:T(8,128)S(1)}, s16[8,224,128]{2,1,0:T(8,128)(2,1)S(1)}, bf16[2,224,384]{2,1,0:T(8,128)(2,1)S(1)}, bf16[2,224,384]{2,1,0:T(8,128)(2,1)S(1)}) custom-call(bf16[544,256]{1,0:T(8,128)(2,1)S(1)} %get-tuple-element.30.own, bf16[544,256]{1,0:T(8,128)(2,1)S(1)} %collective-permute-done.other, ...), custom_call_target="tpu_custom_call" | custom-call | flops 445906944 | bytes 4194304 | tf_op jit(solution)/shard_map/tilt/pallas_call | solution.py:469
  18.3 0.1 collective-permute-start.3
  18.4 0.5 %collective-permute-start.7 = (bf16[2,224,384]{2,1,0:T(8,128)(2,1)S(1)}, bf16[2,224,384]{2,1,0:T(8,128)(2,1)S(1)}, u32[]{:S(2)}, u32[]{:S(2)}) collective-permute-start(bf16[2,224,384]{2,1,0:T(8,128)(2,1)S(1)} %get-tuple-element.49), channel_id=1, source_target_pairs={{0,1},{1,0},{2,3},{3,2},{4,5},{5,4},{6,7},{7,6},{8,9},{9,8},{10,11... | collective-permute-start | bytes 1032200 | tf_op jit(solution)/shard_map/ppermute | solution.py:390
  18.9 1.3 %collective-permute-done.3.got = s16[8,224,128]{2,1,0:T(8,128)(2,1)S(1)} collective-permute-done((s16[8,224,128]{2,1,0:T(8,128)(2,1)S(1)}, s16[8,224,128]{2,1,0:T(8,128)(2,1)S(1)}, u32[]{:S(2)}, u32[]{:S(2)}) %collective-permute-start.3) | collective-permute-done | bytes 458784 | tf_op jit(solution)/shard_map/ppermute | solution.py:390
  20.2 0.3 blocks.1
  20.4 1.6 %collective-permute-start.4 = (s16[2,224,128]{2,1,0:T(8,128)(2,1)S(1)}, s16[2,224,128]{2,1,0:T(8,128)(2,1)S(1)}, u32[]{:S(2)}, u32[]{:S(2)}) collective-permute-start(s16[2,224,128]{2,1,0:T(8,128)(2,1)S(1)} %get-tuple-element.44), channel_id=1, source_target_pairs={{0,2},{2,0},{4,6},{6,4},{8,10},{10,8},{12,14},{14,12},{1,3},{3,1},... | collective-permute-start | bytes 344072 | tf_op jit(solution)/shard_map/ppermute | solution.py:390
  22.0 1.6 %collective-permute-start.5 = (s16[2,224,128]{2,1,0:T(8,128)(2,1)S(1)}, s16[2,224,128]{2,1,0:T(8,128)(2,1)S(1)}, u32[]{:S(2)}, u32[]{:S(2)}) collective-permute-start(s16[2,224,128]{2,1,0:T(8,128)(2,1)S(1)} %get-tuple-element.45), channel_id=1, source_target_pairs={{0,4},{2,6},{4,0},{6,2},{8,12},{10,14},{12,8},{14,10},{1,5},{3,7},... | collective-permute-start | bytes 344072 | tf_op jit(solution)/shard_map/ppermute | solution.py:390
  23.6 0.4 %collective-permute-start.6 = (s16[2,224,128]{2,1,0:T(8,128)(2,1)S(1)}, s16[2,224,128]{2,1,0:T(8,128)(2,1)S(1)}, u32[]{:S(2)}, u32[]{:S(2)}) collective-permute-start(s16[2,224,128]{2,1,0:T(8,128)(2,1)S(1)} %get-tuple-element.46), channel_id=1, source_target_pairs={{0,6},{2,4},{4,2},{6,0},{8,14},{10,12},{12,10},{14,8},{1,7},{3,5},... | collective-permute-start | bytes 344072 | tf_op jit(solution)/shard_map/ppermute | solution.py:390
  24.0 0.0 collective-permute-done.7.refs_4_
  24.0 0.0 copy-done
  24.0 5.2 %dgrad.2.refs_5_ = bf16[2,1728,128]{2,1,0:T(8,128)(2,1)} custom-call(bf16[1792,256]{1,0:T(8,128)(2,1)S(1)} %get-tuple-element.32.mask.refs_0_, bf16[27,128,128]{2,1,0:T(8,128)(2,1)S(1)} %copy-done, bf16[2,2016,1152]{2,1,0:T(8,128)(2,1)S(1)} %get-tuple-element.47.refs_2_, bf16[2,224,384]{2,1,0:T(8,128)(2,1)S(1)} %get-tuple-element.48.refs_3_, ...), custom_call_target="tpu_custom_call" | custom-call | flops 2378170368 | bytes 4194304 | tf_op jit(solution)/shard_map/dgrad/pallas_call | solution.py:492
  29.2 0.0 collective-permute-done.4.got_y
  29.2 0.0 collective-permute-done.5.got_z
  29.2 0.1 collective-permute-done.6.got_yz
  29.3 0.1 last.1
  29.5 2.7 %collective-permute-start.8 = (s16[224,128]{1,0:T(8,128)(2,1)S(1)}, s16[224,128]{1,0:T(8,128)(2,1)S(1)}, u32[]{:S(2)}, u32[]{:S(2)}) collective-permute-start(s16[224,128]{1,0:T(8,128)(2,1)S(1)} %get-tuple-element.53), channel_id=1, source_target_pairs={{0,8},{2,10},{4,12},{6,14},{8,0},{10,2},{12,4},{14,6},{1,9},{3,11}... | collective-permute-start | bytes 172040 | tf_op jit(solution)/shard_map/ppermute | solution.py:390
  32.1 3.1 %dgrad.3 = bf16[2,1728,128]{2,1,0:T(8,128)(2,1)} custom-call(bf16[1792,256]{1,0:T(8,128)(2,1)S(1)} %get-tuple-element.32.mask.refs_0_, bf16[27,128,128]{2,1,0:T(8,128)(2,1)S(1)} %copy-done, bf16[2,2016,1152]{2,1,0:T(8,128)(2,1)S(1)} %get-tuple-element.47.refs_2_, bf16[2,224,384]{2,1,0:T(8,128)(2,1)S(1)} %get-tuple-element.48.refs_3_, ...), custom_call_target="tpu_custom_call", output_to_operand_aliasing={{}: (5, {})} | custom-call | flops 1189085184 | bytes 4194304 | tf_op jit(solution)/shard_map/dgrad/pallas_call | solution.py:492
  35.2 0.0 collective-permute-done.8.got
  35.2 0.7 %sum.1 = f32[216,128]{1,0:T(8,128)} custom-call(f32[216,128]{1,0:T(8,128)S(1)} %get-tuple-element.56.keep, s16[224,128]{1,0:T(8,128)(2,1)S(1)} %collective-permute-done.8.got), custom_call_target="tpu_custom_call" | custom-call | tf_op jit(solution)/shard_map/sum/pallas_call | solution.py:409
  (2 shorter events, 0.0 us)
Async XLA Ops:
  0.6 9.3 %copy-start.2 = (bf16[1296,256]{1,0:T(8,128)(2,1)S(1)}, bf16[1296,256]{1,0:T(8,128)(2,1)}, u32[]{:S(2)}) copy-start(bf16[1296,256]{1,0:T(8,128)(2,1)} %constant.7.clone.shift) | copy-start | bytes 1990660
  2.7 2.3 %collective-permute-start = (bf16[544,256]{1,0:T(8,128)(2,1)S(1)}, bf16[544,256]{1,0:T(8,128)(2,1)S(1)}, u32[]{:S(2)}, u32[]{:S(2)}) collective-permute-start(bf16[544,256]{1,0:T(8,128)(2,1)S(1)} %get-tuple-element.30.own), channel_id=1, source_target_pairs={{0,1},{1,0},{2,3},{3,2},{4,5},{5,4},{6,7},{7,6},{8,9},{9,8},{10,11... | collective-permute-start | bytes 835592 | tf_op jit(solution)/shard_map/ppermute | solution.py:390
  4.9 11.4 %collective-permute-start.2 = (bf16[256,256]{1,0:T(8,128)(2,1)S(1)}, bf16[256,256]{1,0:T(8,128)(2,1)S(1)}, u32[]{:S(2)}, u32[]{:S(2)}) collective-permute-start(bf16[256,256]{1,0:T(8,128)(2,1)S(1)} %get-tuple-element.35), channel_id=1, source_target_pairs={{0,1},{1,0},{2,3},{3,2},{4,5},{5,4},{6,7},{7,6},{8,9},{9,8},{10,11... | collective-permute-start | bytes 393224 | tf_op jit(solution)/shard_map/ppermute | solution.py:390
  5.1 11.2 %collective-permute-start.1 = (bf16[384,256]{1,0:T(8,128)(2,1)S(1)}, bf16[384,256]{1,0:T(8,128)(2,1)S(1)}, u32[]{:S(2)}, u32[]{:S(2)}) collective-permute-start(bf16[384,256]{1,0:T(8,128)(2,1)S(1)} %pad_maximum_fusion), channel_id=1, source_target_pairs={{0,2},{2,4},{4,6},{6,8},{8,10},{10,12},{12,14},{3,1},{5,3},{7,5},{... | collective-permute-start | bytes 589832 | tf_op jit(solution)/shard_map/ppermute | solution.py:447
  10.0 6.3 %copy-start.1 = (bf16[672,224]{1,0:T(8,128)(2,1)S(1)}, bf16[672,224]{1,0:T(8,128)(2,1)}, u32[]{:S(2)}) copy-start(bf16[672,224]{1,0:T(8,128)(2,1)} %constant.8.clone.bands) | copy-start | bytes 903172
  16.3 7.7 %copy-start = (bf16[27,128,128]{2,1,0:T(8,128)(2,1)S(1)}, bf16[27,128,128]{2,1,0:T(8,128)(2,1)}, u32[]{:S(2)}) copy-start(bf16[27,128,128]{2,1,0:T(8,128)(2,1)} %refs_1_.3) | copy-start | bytes 2654212
  18.3 1.9 %collective-permute-start.3 = (s16[8,224,128]{2,1,0:T(8,128)(2,1)S(1)}, s16[8,224,128]{2,1,0:T(8,128)(2,1)S(1)}, u32[]{:S(2)}, u32[]{:S(2)}) collective-permute-start(s16[8,224,128]{2,1,0:T(8,128)(2,1)S(1)} %get-tuple-element.40), channel_id=1, source_target_pairs={{0,1},{1,0},{2,3},{3,2},{4,5},{5,4},{6,7},{7,6},{8,9},{9,8},{10,11... | collective-permute-start | bytes 1376264 | tf_op jit(solution)/shard_map/ppermute | solution.py:390
  18.4 5.6 %collective-permute-start.7 = (bf16[2,224,384]{2,1,0:T(8,128)(2,1)S(1)}, bf16[2,224,384]{2,1,0:T(8,128)(2,1)S(1)}, u32[]{:S(2)}, u32[]{:S(2)}) collective-permute-start(bf16[2,224,384]{2,1,0:T(8,128)(2,1)S(1)} %get-tuple-element.49), channel_id=1, source_target_pairs={{0,1},{1,0},{2,3},{3,2},{4,5},{5,4},{6,7},{7,6},{8,9},{9,8},{10,11... | collective-permute-start | bytes 1032200 | tf_op jit(solution)/shard_map/ppermute | solution.py:390
  20.4 8.7 %collective-permute-start.4 = (s16[2,224,128]{2,1,0:T(8,128)(2,1)S(1)}, s16[2,224,128]{2,1,0:T(8,128)(2,1)S(1)}, u32[]{:S(2)}, u32[]{:S(2)}) collective-permute-start(s16[2,224,128]{2,1,0:T(8,128)(2,1)S(1)} %get-tuple-element.44), channel_id=1, source_target_pairs={{0,2},{2,0},{4,6},{6,4},{8,10},{10,8},{12,14},{14,12},{1,3},{3,1},... | collective-permute-start | bytes 344072 | tf_op jit(solution)/shard_map/ppermute | solution.py:390
  22.0 7.2 %collective-permute-start.5 = (s16[2,224,128]{2,1,0:T(8,128)(2,1)S(1)}, s16[2,224,128]{2,1,0:T(8,128)(2,1)S(1)}, u32[]{:S(2)}, u32[]{:S(2)}) collective-permute-start(s16[2,224,128]{2,1,0:T(8,128)(2,1)S(1)} %get-tuple-element.45), channel_id=1, source_target_pairs={{0,4},{2,6},{4,0},{6,2},{8,12},{10,14},{12,8},{14,10},{1,5},{3,7},... | collective-permute-start | bytes 344072 | tf_op jit(solution)/shard_map/ppermute | solution.py:390
  23.6 5.7 %collective-permute-start.6 = (s16[2,224,128]{2,1,0:T(8,128)(2,1)S(1)}, s16[2,224,128]{2,1,0:T(8,128)(2,1)S(1)}, u32[]{:S(2)}, u32[]{:S(2)}) collective-permute-start(s16[2,224,128]{2,1,0:T(8,128)(2,1)S(1)} %get-tuple-element.46), channel_id=1, source_target_pairs={{0,6},{2,4},{4,2},{6,0},{8,14},{10,12},{12,10},{14,8},{1,7},{3,5},... | collective-permute-start | bytes 344072 | tf_op jit(solution)/shard_map/ppermute | solution.py:390
  29.5 5.7 %collective-permute-start.8 = (s16[224,128]{1,0:T(8,128)(2,1)S(1)}, s16[224,128]{1,0:T(8,128)(2,1)S(1)}, u32[]{:S(2)}, u32[]{:S(2)}) collective-permute-start(s16[224,128]{1,0:T(8,128)(2,1)S(1)} %get-tuple-element.53), channel_id=1, source_target_pairs={{0,8},{2,10},{4,12},{6,14},{8,0},{10,2},{12,4},{14,6},{1,9},{3,11}... | collective-permute-start | bytes 172040 | tf_op jit(solution)/shard_map/ppermute | solution.py:390

commit v6 on v5

--- a/solution.py
+++ b/solution.py
@@ -23,7 +23,7 @@
         m[i, i * BSIDE] = 1
         m[16 + i, i * BSIDE + 11] = 1
         m[32 + i, i] = 1
-        m[48 + i, 11 * BSIDE + i] = 1
+        m[52 + i, 11 * BSIDE + i] = 1
     m[12, 0] = m[28, 11] = 1
     m[13, 11 * BSIDE] = m[29, 11 * BSIDE + 11] = 1
     return m.astype(jnp.bfloat16)
@@ -35,13 +35,8 @@
         for b in range(BSIDE):
             for c in range(BSIDE):
                 sb, sc = b - (k // 3 - 1), c - (k % 3 - 1)
-                if sc in (-1, 12):
-                    row = {-1: 13, 12: 12}.get(sb, sb) + (176 if sc < 0 else 192)
-                elif sb in (-1, 12):
-                    row = sc + (144 if sb < 0 else 160)
-                else:
-                    row = sb * BSIDE + sc
-                m[k, b, c, row] = 1
+                if 0 <= sc < BSIDE:
+                    m[k, b, c, 16 + sb * BSIDE + sc] = 1
     return m.reshape(9 * PLANE, KROWS).astype(jnp.bfloat16)
 
 
@@ -187,15 +182,15 @@
     a1h, b1h = 1 - a0h, 1 - b0h
     rest = jnp.zeros((KROWS - 176, 2 * C), BF)
     for p in range(BSIDE):
-        kop[p + 1, pl.ds(0, PLANE), :] = gm[p]
+        kop[p + 1, pl.ds(16, PLANE), :] = gm[p]
         side = gather(pick_b, PLANE + p * 16)
-        kop[p + 1, pl.ds(144, 16), :] = side * b0h
+        kop[p + 1, pl.ds(0, 16), :] = side * b0h
         kop[p + 1, pl.ds(160, 16), :] = side * b1h
         kop[p + 1, pl.ds(176, KROWS - 176), :] = rest
     for r in range(0, PLANE, 16):
-        kop[0, pl.ds(r, 16), :] = gather(pick_a, r)
+        kop[0, pl.ds(16 + r, 16), :] = gather(pick_a, r)
     side = gather(pick_d, PLANE + 176) * a0h + gather(pick_d, PLANE) * a1h
-    kop[0, pl.ds(144, 16), :] = side * b0h
+    kop[0, pl.ds(0, 16), :] = side * b0h
     kop[0, pl.ds(160, 16), :] = side * b1h
     kop[0, pl.ds(176, KROWS - 176), :] = rest
     return a0h, a1h
@@ -221,8 +216,8 @@
 def shifted(shift, kop, x, ends):
     for p in range(EXT - 1):
         for k in range(9):
-            if k == 4:
-                y = kop[p, pl.ds(0, PLANE), :]
+            if k % 3 == 1:
+                y = kop[p, pl.ds(16 - BSIDE * (k // 3 - 1), PLANE), :]
             else:
                 y = dot(shift[pl.ds(k * PLANE, PLANE), :], kop[p]).astype(BF)
             for at in (p,) if p else (0, EXT - 1):
@@ -308,19 +303,25 @@
     return total + y[pl.ds(p * rows, rows), pl.ds(2 * C, C)]
 
 
-def dgrad_kernel(pieces, mask, w, x, zs, zs_got, before, out, y, yz, plane, res, sem):
+def products_kernel(w, x, out):
+    out[...] = dot_t(x[1, pl.ds(0, out.shape[0]), :], columns(w, range(9)))
+
+
+def dgrad_kernel(pieces, mask, w, x, zs, zs_got, ready, before, out, y, yz, plane, res, sem):
     del before
     core = lax.axis_index("sub")
     stores = []
-    for j, first, count in pieces:
-        rows = pl.ds(0, (count + 2) * PLANE)
-        y[rows, :] = dot_t(x[j, pl.ds(first * PLANE, (count + 2) * PLANE), :], columns(w, range(9)))
+    for j, first, count, done in pieces:
+        source = ready if done else y
+        if not done:
+            rows = pl.ds(0, (count + 2) * PLANE)
+            y[rows, :] = dot_t(x[j, pl.ds(first * PLANE, (count + 2) * PLANE), :], columns(w, range(9)))
         at = pl.ds(first * 16, (count + 2) * 16)
         for n in range(2):
             faces = jnp.where(core == n, zs[j, at, :], zs_got[j, at, :])
             yz[n, pl.ds(0, (count + 2) * 16), :] = dot_t(faces, columns(w, (2, 5, 8) if n == 0 else (0, 3, 6)))
         for p in range(count):
-            plane[pl.ds(0, PLANE), :] = joined(y, p, PLANE)
+            plane[pl.ds(0, PLANE), :] = joined(source, p, PLANE)
             for n in range(2):
                 at = pl.ds(11 * n, BSIDE, stride=BSIDE)
                 plane[at, :] = plane[at, :] + joined(yz.at[n], p, 16)[:BSIDE]
@@ -481,20 +482,29 @@
         size=4 * 2**20,
     )(*tilt_ins)
 
+    send, x = tied(send, x)
     got = exchange(send, "sub", 1) if custom else None
+    (ready,) = call(
+        products_kernel,
+        "products",
+        [VMEM] * 2,
+        [((6 * PLANE, 3 * C), F32, VMEM)],
+        flops=work * 6 // EXT,
+        size=4 * 2**20,
+    )(weight, x)
     zs_got = exchange(zs_send, "sub", 1)
 
     def dgrad(*pieces):
-        most = max(count for _, _, count in pieces) + 2
+        most = max(count for _, _, count, _ in pieces) + 2
 
         def run(before):
             fresh = before is None
             return call(
-                (lambda *refs: dgrad_kernel(pieces, *refs[:5], None, *refs[5:]))
+                (lambda *refs: dgrad_kernel(pieces, *refs[:6], None, *refs[6:]))
                 if fresh
                 else (lambda *refs: dgrad_kernel(pieces, *refs)),
                 "dgrad",
-                [VMEM] * 5 + ([] if fresh else [ANY]),
+                [VMEM] * 6 + ([] if fresh else [ANY]),
                 [((2, VOX, C), BF, ANY)],
                 [
                     pltpu.VMEM((most * PLANE, 3 * C), F32),
@@ -503,24 +513,24 @@
                     pltpu.VMEM((2, VOX, C), BF),
                     pltpu.SemaphoreType.DMA((12,)),
                 ],
-                aliases={} if fresh else {5: 0},
-                flops=work * sum(count for _, _, count in pieces) // 12,
+                aliases={} if fresh else {6: 0},
+                flops=work * sum(count for _, _, count, _ in pieces) // 12,
                 size=4 * 2**20,
                 limit=12,
-            )(mask, weight, x, zs, zs_got, *(() if fresh else (before,)))[0]
+            )(mask, weight, x, zs, zs_got, ready, *(() if fresh else (before,)))[0]
 
         return run
 
     if custom:
-        got, zs = tied(got, zs)
-        weight_grad, input_grad = reduce_blocks(keep, got, [dgrad((0, 0, 12), (1, 0, 4)), dgrad((1, 4, 8))])
+        got, zs, ready = tied(got, zs, ready)
+        weight_grad, input_grad = reduce_blocks(keep, got, [dgrad((0, 0, 12, False), (1, 0, 4, True), (1, 4, 2, False)), dgrad((1, 6, 6, False))])
     else:
         first = lax.axis_index("sub") == 0
         even = jnp.where(first, keep, send)
         odd = jnp.where(first, send, keep)
         kernel_term = jnp.stack([even, odd], axis=1).reshape(27 * C, C)
         weight_grad = lax.psum_scatter(kernel_term, ("space", "sub"), scatter_dimension=0, tiled=True)
-        input_grad = dgrad((0, 0, 12), (1, 0, 12))(None)
+        input_grad = dgrad((0, 0, 12, False), (1, 0, 12, False))(None)
     return input_grad, weight_grad
 
 

time: 36 us -> 35.2 us (0.978)
  waiting for transfers between devices: 1.46 us -> 0.52 us
    ppermute x8, waiting for transfers between devices: 1.46 us -> 0.52 us  [exchange(): return lax.ppermute(value, axis, pairs)]
    pallas_call x2 -> x3, Pallas kernels: 8.24 us -> 8.76 us  [the longest x2 7.5 us: run(): call((lambda *refs: dgrad_kernel(pieces, *refs[:6], None, *refs[6:])) if...]
  transfers between devices with their start and end apart: 9 -> 9, of which waited for: 2 -> 1; matrix products, arithmetic and copies ran while one was open for 0% -> 0% of each run, Pallas kernels for 46% -> 48%
where the time goes in v6:
time: 35.2 us; the launch traced here: 35 us
  Pallas kernels  21.4 us (61%)
  starting transfers between devices  12.2 us (35%)
  between operations  0.81 us (2%)
  waiting for transfers between devices  0.52 us (1%)
    pallas_call x2, Pallas kernels, run(): call((lambda *refs: dgrad_kernel(pieces, *refs[:6], None, *refs[6:])) if...  7.5 us
    ppermute x8, starting transfers between devices, exchange(): return lax.ppermute(value, axis, pairs)  7.35 us
    pallas_call x1, Pallas kernels, on_device(): call(first_kernel, 'first', [VMEM] * 5, [((2, EXT * PLANE, 9 * C), BF, FI...  6.03 us
    ppermute x1, starting transfers between devices, on_device(): lax.ppermute(jnp.concatenate([mine, other[MINE:]], axis=0), ('space', 'su...  4.88 us
    pallas_call x1, Pallas kernels, on_device(): call(prep_kernel, 'prep', [HBM] * 4, [((BSIDE, PLANE, 2 * C), BF, VMEM),...  2.01 us
    pallas_call x1, Pallas kernels, on_device(): call(tilt_kernel if custom else lambda *refs: tilt_kernel(*refs, refs[8])...  1.94 us
    pallas_call x1, Pallas kernels, on_device(): call(features_kernel, 'features', [VMEM] * 2 + [HBM], [((2, (EXT + 2) * P...  1.67 us
    pallas_call x1, Pallas kernels, on_device(): call(products_kernel, 'products', [VMEM] * 2, [((6 * PLANE, 3 * C), F32,...  1.26 us
  transfers between devices with their start and end apart: 9, of which 1 were waited for; matrix products, arithmetic and copies ran while one was open for 0% of the time, Pallas kernels for 48%

profile of v6, /device:TPU:0, one launch (start us, length us, event | category | flops | bytes accessed | tf_op | source)
XLA Modules:
  0.0 35.0 jit_solution(14845816320364881799)
XLA Ops:
  0.6 0.0 copy-start.2
  0.6 2.0 %prep.1 = (bf16[12,144,256]{2,1,0:T(8,128)(2,1)S(1)}, bf16[544,256]{1,0:T(8,128)(2,1)S(1)}, bf16[192,256]{1,0:T(8,128)(2,1)S(1)}, bf16[1792,256]{1,0:T(8,128)(2,1)S(1)}, bf16[64,144]{1,0:T(8,128)(2,1)S(1)}) custom-call(s32[2,6]{1,0:T(2,128)} %nb_hbm.1, s32[2,1728]{1,0:T(2,128)} %act_hbm.1, bf16[64,144]{1,0:T(8,128)(2,1)} %constant.6.clone.strips_hbm, ...), custom_call_target="tpu_custom_call" | custom-call | tf_op jit(solution)/shard_map/prep/pallas_call | solution.py:417
  2.7 0.5 %collective-permute-start = (bf16[544,256]{1,0:T(8,128)(2,1)S(1)}, bf16[544,256]{1,0:T(8,128)(2,1)S(1)}, u32[]{:S(2)}, u32[]{:S(2)}) collective-permute-start(bf16[544,256]{1,0:T(8,128)(2,1)S(1)} %get-tuple-element.33.own), channel_id=1, source_target_pairs={{0,1},{1,0},{2,3},{3,2},{4,5},{5,4},{6,7},{7,6},{8,9},{9,8},{10,11... | collective-permute-start | bytes 835592 | tf_op jit(solution)/shard_map/ppermute | solution.py:391
  3.2 1.7 %features.1 = (bf16[2,2304,128]{2,1,0:T(8,128)(2,1)S(1)}, bf16[256,256]{1,0:T(8,128)(2,1)S(1)}, bf16[256,256]{1,0:T(8,128)(2,1)S(1)}) custom-call(bf16[1792,256]{1,0:T(8,128)(2,1)S(1)} %get-tuple-element.35.mask.refs_0_, bf16[64,144]{1,0:T(8,128)(2,1)S(1)} %get-tuple-element.36.strips, bf16[2,1728,128]{2,1,0:T(8,128)(2,1)} %f_hbm.1), custom_call_target="tpu_custom_call" | custom-call | flops 10000000 | bytes 1000000 | tf_op jit(solution)/shard_map/features/pallas_call | solution.py:437
  4.9 0.1 collective-permute-start.2
  5.0 0.0 collective-permute-done.other
  5.0 4.9 %collective-permute-start.1 = (bf16[384,256]{1,0:T(8,128)(2,1)S(1)}, bf16[384,256]{1,0:T(8,128)(2,1)S(1)}, u32[]{:S(2)}, u32[]{:S(2)}) collective-permute-start(bf16[384,256]{1,0:T(8,128)(2,1)S(1)} %pad_maximum_fusion), channel_id=1, source_target_pairs={{0,2},{2,4},{4,6},{6,8},{8,10},{10,12},{12,14},{3,1},{5,3},{7,5},{... | collective-permute-start | bytes 589832 | tf_op jit(solution)/shard_map/ppermute | solution.py:448
  9.9 0.0 copy-done.2
  9.9 0.0 copy-start.1
  9.9 6.0 %first.1 = (bf16[2,2016,1152]{2,1,0:T(8,128)(2,1)S(1)}, f32[384,1152]{1,0:T(8,128)S(1)}) custom-call(bf16[1296,256]{1,0:T(8,128)(2,1)S(1)} %copy-done.2, bf16[12,144,256]{2,1,0:T(8,128)(2,1)S(1)} %get-tuple-element.39.gm, bf16[544,256]{1,0:T(8,128)(2,1)S(1)} %get-tuple-element.33.own, bf16[544,256]{1,0:T(8,128)(2,1)S(1)} %collective-permute-done.other, ...), custom_call_target="tpu_custom_call" | custom-call | flops 3567255552 | bytes 8388608 | tf_op jit(solution)/shard_map/first/pallas_call | solution.py:454
  16.0 0.0 copy-start
  16.0 0.0 collective-permute-done.2.strip_other
  16.0 0.0 collective-permute-done.1.got
  16.0 0.0 copy-done.1
  16.0 1.9 %tilt.1 = (f32[8,216,128]{2,1,0:T(8,128)S(1)}, s16[8,224,128]{2,1,0:T(8,128)(2,1)S(1)}, bf16[2,224,384]{2,1,0:T(8,128)(2,1)S(1)}, bf16[2,224,384]{2,1,0:T(8,128)(2,1)S(1)}) custom-call(bf16[544,256]{1,0:T(8,128)(2,1)S(1)} %get-tuple-element.33.own, bf16[544,256]{1,0:T(8,128)(2,1)S(1)} %collective-permute-done.other, ...), custom_call_target="tpu_custom_call" | custom-call | flops 445906944 | bytes 4194304 | tf_op jit(solution)/shard_map/tilt/pallas_call | solution.py:470
  18.0 0.1 collective-permute-start.3
  18.0 0.5 %collective-permute-start.7 = (bf16[2,224,384]{2,1,0:T(8,128)(2,1)S(1)}, bf16[2,224,384]{2,1,0:T(8,128)(2,1)S(1)}, u32[]{:S(2)}, u32[]{:S(2)}) collective-permute-start(bf16[2,224,384]{2,1,0:T(8,128)(2,1)S(1)} %get-tuple-element.54), channel_id=1, source_target_pairs={{0,1},{1,0},{2,3},{3,2},{4,5},{5,4},{6,7},{7,6},{8,9},{9,8},{10,11... | collective-permute-start | bytes 1032200 | tf_op jit(solution)/shard_map/ppermute | solution.py:391
  18.5 0.0 copy-done
  18.5 1.3 %products.1.refs_5_ = f32[864,384]{1,0:T(8,128)S(1)} custom-call(bf16[27,128,128]{2,1,0:T(8,128)(2,1)S(1)} %copy-done, bf16[2,2016,1152]{2,1,0:T(8,128)(2,1)S(1)} %get-tuple-element.47.x.refs_2_), custom_call_target="tpu_custom_call" | custom-call | flops 764411904 | bytes 4194304 | tf_op jit(solution)/shard_map/products/pallas_call | solution.py:487
  19.8 0.0 collective-permute-done.3.got
  19.8 0.3 blocks.1
  20.1 1.7 %collective-permute-start.4 = (s16[2,224,128]{2,1,0:T(8,128)(2,1)S(1)}, s16[2,224,128]{2,1,0:T(8,128)(2,1)S(1)}, u32[]{:S(2)}, u32[]{:S(2)}) collective-permute-start(s16[2,224,128]{2,1,0:T(8,128)(2,1)S(1)} %get-tuple-element.50), channel_id=1, source_target_pairs={{0,2},{2,0},{4,6},{6,4},{8,10},{10,8},{12,14},{14,12},{1,3},{3,1},... | collective-permute-start | bytes 344072 | tf_op jit(solution)/shard_map/ppermute | solution.py:391
  21.8 1.6 %collective-permute-start.5 = (s16[2,224,128]{2,1,0:T(8,128)(2,1)S(1)}, s16[2,224,128]{2,1,0:T(8,128)(2,1)S(1)}, u32[]{:S(2)}, u32[]{:S(2)}) collective-permute-start(s16[2,224,128]{2,1,0:T(8,128)(2,1)S(1)} %get-tuple-element.51), channel_id=1, source_target_pairs={{0,4},{2,6},{4,0},{6,2},{8,12},{10,14},{12,8},{14,10},{1,5},{3,7},... | collective-permute-start | bytes 344072 | tf_op jit(solution)/shard_map/ppermute | solution.py:391
  23.4 0.3 collective-permute-start.6
  23.7 0.0 collective-permute-done.7.refs_4_
  23.7 4.9 %dgrad.2.refs_6_ = bf16[2,1728,128]{2,1,0:T(8,128)(2,1)} custom-call(bf16[1792,256]{1,0:T(8,128)(2,1)S(1)} %get-tuple-element.35.mask.refs_0_, bf16[27,128,128]{2,1,0:T(8,128)(2,1)S(1)} %copy-done, bf16[2,2016,1152]{2,1,0:T(8,128)(2,1)S(1)} %get-tuple-element.47.x.refs_2_, bf16[2,224,384]{2,1,0:T(8,128)(2,1)S(1)} %get-tuple-element.53.refs_3_, ...), custom_call_target="tpu_custom_call" | custom-call | flops 2675441664 | bytes 4194304 | tf_op jit(solution)/shard_map/dgrad/pallas_call | solution.py:502
  28.6 0.0 collective-permute-done.4.got_y
  28.6 0.0 collective-permute-done.5.got_z
  28.6 0.5 %collective-permute-done.6.got_yz = s16[2,224,128]{2,1,0:T(8,128)(2,1)S(1)} collective-permute-done((s16[2,224,128]{2,1,0:T(8,128)(2,1)S(1)}, s16[2,224,128]{2,1,0:T(8,128)(2,1)S(1)}, u32[]{:S(2)}, u32[]{:S(2)}) %collective-permute-start.6) | collective-permute-done | bytes 114720 | tf_op jit(solution)/shard_map/ppermute | solution.py:391
  29.1 0.1 last.1
  29.2 2.6 %collective-permute-start.8 = (s16[224,128]{1,0:T(8,128)(2,1)S(1)}, s16[224,128]{1,0:T(8,128)(2,1)S(1)}, u32[]{:S(2)}, u32[]{:S(2)}) collective-permute-start(s16[224,128]{1,0:T(8,128)(2,1)S(1)} %get-tuple-element.59), channel_id=1, source_target_pairs={{0,8},{2,10},{4,12},{6,14},{8,0},{10,2},{12,4},{14,6},{1,9},{3,11}... | collective-permute-start | bytes 172040 | tf_op jit(solution)/shard_map/ppermute | solution.py:391
  31.8 2.6 %dgrad.3 = bf16[2,1728,128]{2,1,0:T(8,128)(2,1)} custom-call(bf16[1792,256]{1,0:T(8,128)(2,1)S(1)} %get-tuple-element.35.mask.refs_0_, bf16[27,128,128]{2,1,0:T(8,128)(2,1)S(1)} %copy-done, bf16[2,2016,1152]{2,1,0:T(8,128)(2,1)S(1)} %get-tuple-element.47.x.refs_2_, ...), custom_call_target="tpu_custom_call", output_to_operand_aliasing={{}: (6, {})} | custom-call | flops 891813888 | bytes 4194304 | tf_op jit(solution)/shard_map/dgrad/pallas_call | solution.py:502
  34.4 0.0 collective-permute-done.8.got
  34.4 0.7 %sum.1 = f32[216,128]{1,0:T(8,128)} custom-call(f32[216,128]{1,0:T(8,128)S(1)} %get-tuple-element.62.keep, s16[224,128]{1,0:T(8,128)(2,1)S(1)} %collective-permute-done.8.got), custom_call_target="tpu_custom_call" | custom-call | tf_op jit(solution)/shard_map/sum/pallas_call | solution.py:410
  (2 shorter events, 0.0 us)
Async XLA Ops:
  0.6 9.3 %copy-start.2 = (bf16[1296,256]{1,0:T(8,128)(2,1)S(1)}, bf16[1296,256]{1,0:T(8,128)(2,1)}, u32[]{:S(2)}) copy-start(bf16[1296,256]{1,0:T(8,128)(2,1)} %constant.7.clone.shift) | copy-start | bytes 1990660
  2.7 2.3 %collective-permute-start = (bf16[544,256]{1,0:T(8,128)(2,1)S(1)}, bf16[544,256]{1,0:T(8,128)(2,1)S(1)}, u32[]{:S(2)}, u32[]{:S(2)}) collective-permute-start(bf16[544,256]{1,0:T(8,128)(2,1)S(1)} %get-tuple-element.33.own), channel_id=1, source_target_pairs={{0,1},{1,0},{2,3},{3,2},{4,5},{5,4},{6,7},{7,6},{8,9},{9,8},{10,11... | collective-permute-start | bytes 835592 | tf_op jit(solution)/shard_map/ppermute | solution.py:391
  4.9 11.1 %collective-permute-start.2 = (bf16[256,256]{1,0:T(8,128)(2,1)S(1)}, bf16[256,256]{1,0:T(8,128)(2,1)S(1)}, u32[]{:S(2)}, u32[]{:S(2)}) collective-permute-start(bf16[256,256]{1,0:T(8,128)(2,1)S(1)} %get-tuple-element.38), channel_id=1, source_target_pairs={{0,1},{1,0},{2,3},{3,2},{4,5},{5,4},{6,7},{7,6},{8,9},{9,8},{10,11... | collective-permute-start | bytes 393224 | tf_op jit(solution)/shard_map/ppermute | solution.py:391
  5.0 11.0 %collective-permute-start.1 = (bf16[384,256]{1,0:T(8,128)(2,1)S(1)}, bf16[384,256]{1,0:T(8,128)(2,1)S(1)}, u32[]{:S(2)}, u32[]{:S(2)}) collective-permute-start(bf16[384,256]{1,0:T(8,128)(2,1)S(1)} %pad_maximum_fusion), channel_id=1, source_target_pairs={{0,2},{2,4},{4,6},{6,8},{8,10},{10,12},{12,14},{3,1},{5,3},{7,5},{... | collective-permute-start | bytes 589832 | tf_op jit(solution)/shard_map/ppermute | solution.py:448
  9.9 6.1 %copy-start.1 = (bf16[672,224]{1,0:T(8,128)(2,1)S(1)}, bf16[672,224]{1,0:T(8,128)(2,1)}, u32[]{:S(2)}) copy-start(bf16[672,224]{1,0:T(8,128)(2,1)} %constant.8.clone.bands) | copy-start | bytes 903172
  16.0 2.6 %copy-start = (bf16[27,128,128]{2,1,0:T(8,128)(2,1)S(1)}, bf16[27,128,128]{2,1,0:T(8,128)(2,1)}, u32[]{:S(2)}) copy-start(bf16[27,128,128]{2,1,0:T(8,128)(2,1)} %refs_1_.3) | copy-start | bytes 2654212
  18.0 1.9 %collective-permute-start.3 = (s16[8,224,128]{2,1,0:T(8,128)(2,1)S(1)}, s16[8,224,128]{2,1,0:T(8,128)(2,1)S(1)}, u32[]{:S(2)}, u32[]{:S(2)}) collective-permute-start(s16[8,224,128]{2,1,0:T(8,128)(2,1)S(1)} %get-tuple-element.45), channel_id=1, source_target_pairs={{0,1},{1,0},{2,3},{3,2},{4,5},{5,4},{6,7},{7,6},{8,9},{9,8},{10,11... | collective-permute-start | bytes 1376264 | tf_op jit(solution)/shard_map/ppermute | solution.py:391
  18.0 5.6 %collective-permute-start.7 = (bf16[2,224,384]{2,1,0:T(8,128)(2,1)S(1)}, bf16[2,224,384]{2,1,0:T(8,128)(2,1)S(1)}, u32[]{:S(2)}, u32[]{:S(2)}) collective-permute-start(bf16[2,224,384]{2,1,0:T(8,128)(2,1)S(1)} %get-tuple-element.54), channel_id=1, source_target_pairs={{0,1},{1,0},{2,3},{3,2},{4,5},{5,4},{6,7},{7,6},{8,9},{9,8},{10,11... | collective-permute-start | bytes 1032200 | tf_op jit(solution)/shard_map/ppermute | solution.py:391
  20.1 8.5 %collective-permute-start.4 = (s16[2,224,128]{2,1,0:T(8,128)(2,1)S(1)}, s16[2,224,128]{2,1,0:T(8,128)(2,1)S(1)}, u32[]{:S(2)}, u32[]{:S(2)}) collective-permute-start(s16[2,224,128]{2,1,0:T(8,128)(2,1)S(1)} %get-tuple-element.50), channel_id=1, source_target_pairs={{0,2},{2,0},{4,6},{6,4},{8,10},{10,8},{12,14},{14,12},{1,3},{3,1},... | collective-permute-start | bytes 344072 | tf_op jit(solution)/shard_map/ppermute | solution.py:391
  21.8 6.8 %collective-permute-start.5 = (s16[2,224,128]{2,1,0:T(8,128)(2,1)S(1)}, s16[2,224,128]{2,1,0:T(8,128)(2,1)S(1)}, u32[]{:S(2)}, u32[]{:S(2)}) collective-permute-start(s16[2,224,128]{2,1,0:T(8,128)(2,1)S(1)} %get-tuple-element.51), channel_id=1, source_target_pairs={{0,4},{2,6},{4,0},{6,2},{8,12},{10,14},{12,8},{14,10},{1,5},{3,7},... | collective-permute-start | bytes 344072 | tf_op jit(solution)/shard_map/ppermute | solution.py:391
  23.4 5.7 %collective-permute-start.6 = (s16[2,224,128]{2,1,0:T(8,128)(2,1)S(1)}, s16[2,224,128]{2,1,0:T(8,128)(2,1)S(1)}, u32[]{:S(2)}, u32[]{:S(2)}) collective-permute-start(s16[2,224,128]{2,1,0:T(8,128)(2,1)S(1)} %get-tuple-element.52), channel_id=1, source_target_pairs={{0,6},{2,4},{4,2},{6,0},{8,14},{10,12},{12,10},{14,8},{1,7},{3,5},... | collective-permute-start | bytes 344072 | tf_op jit(solution)/shard_map/ppermute | solution.py:391
  29.2 5.2 %collective-permute-start.8 = (s16[224,128]{1,0:T(8,128)(2,1)S(1)}, s16[224,128]{1,0:T(8,128)(2,1)S(1)}, u32[]{:S(2)}, u32[]{:S(2)}) collective-permute-start(s16[224,128]{1,0:T(8,128)(2,1)S(1)} %get-tuple-element.59), channel_id=1, source_target_pairs={{0,8},{2,10},{4,12},{6,14},{8,0},{10,2},{12,4},{14,6},{1,9},{3,11}... | collective-permute-start | bytes 172040 | tf_op jit(solution)/shard_map/ppermute | solution.py:391

commit v7 on v6

--- a/solution.py
+++ b/solution.py
@@ -12,6 +12,7 @@
 EXT = BSIDE + 2
 C = 128
 KROWS = 256
+SPAN = 176
 MINE = PLANE + 208
 BF = jnp.bfloat16
 F32 = jnp.float32
@@ -30,14 +31,14 @@
 
 
 def shift_matrix():
-    m = np.zeros((9, BSIDE, BSIDE, KROWS), np.float32)
-    for k in range(9):
-        for b in range(BSIDE):
+    m = np.zeros((2, SPAN, KROWS), np.float32)
+    for n in range(2):
+        for b in range(EXT):
             for c in range(BSIDE):
-                sb, sc = b - (k // 3 - 1), c - (k % 3 - 1)
-                if 0 <= sc < BSIDE:
-                    m[k, b, c, 16 + sb * BSIDE + sc] = 1
-    return m.reshape(9 * PLANE, KROWS).astype(jnp.bfloat16)
+                source = c - (2 * n - 1)
+                if 0 <= source < BSIDE:
+                    m[n, 4 + b * BSIDE + c, 4 + b * BSIDE + source] = 1
+    return m.reshape(2 * SPAN, KROWS).astype(jnp.bfloat16)
 
 
 def band_matrix():
@@ -213,13 +214,13 @@
     z[pl.ds((EXT - 1) * 16, 16), :] = gather(far, 0) * (1 - a0h)
 
 
-def shifted(shift, kop, x, ends):
+def shifted(shift, kop, sides, x, ends):
     for p in range(EXT - 1):
+        for n in range(2):
+            sides[p % 4, n] = dot(shift[pl.ds(n * SPAN, SPAN), :], kop[p]).astype(BF)
         for k in range(9):
-            if k % 3 == 1:
-                y = kop[p, pl.ds(16 - BSIDE * (k // 3 - 1), PLANE), :]
-            else:
-                y = dot(shift[pl.ds(k * PLANE, PLANE), :], kop[p]).astype(BF)
+            rows = pl.ds(16 - BSIDE * (k // 3 - 1), PLANE)
+            y = kop[p, rows, :] if k % 3 == 1 else sides[p % 4, k % 3 // 2, rows, :]
             for at in (p,) if p else (0, EXT - 1):
                 v = y if p else y * ends[1 if at else 0]
                 for j in range(2):
@@ -234,11 +235,11 @@
     return lax.dot_general(a, b, (((0,), (0,)), ((), ())), preferred_element_type=F32)
 
 
-def first_kernel(shift, gm, own, other, pad, x, acc, kop):
+def first_kernel(shift, gm, own, other, pad, x, acc, kop, sides):
     ends = [jnp.concatenate([w] * (PLANE // 16), axis=0) for w in layer_operands(gm, own, other, kop)]
-    shifted(shift, kop, x, ends)
-    acc[...] = dot_rows(stacked(pad, 0), x[0])
-    acc[...] += dot_rows(stacked(pad, 1), x[1])
+    shifted(shift, kop, sides, x, ends)
+    both = jnp.concatenate([stacked(pad, 0), stacked(pad, 1)], axis=0)
+    acc[...] = dot_rows(both, x[...].reshape(both.shape[0], 9 * C))
 
 
 def encode(ref, at, v):
@@ -257,16 +258,17 @@
 def tilt_kernel(own, other, got, strip, strip_other, bands, acc, keep, code, zs, zs_send, z, more, send):
     sub = lax.axis_index("sub")
     rows = EXT * 16
-    total = None
-    for n, (message, features, out) in enumerate(((own, strip, zs), (other, strip_other, zs_send))):
+    for n, message in enumerate((own, other)):
         facing_plane(message, got, z.at[n])
+    left, right = [], []
+    for n, (features, out) in enumerate(((strip, zs), (strip_other, zs_send))):
         v = dot(bands[...], z[n]).astype(BF)
         for j in range(2):
             lanes = slice(j * C, j * C + C)
-            out[j] = jnp.concatenate([v[q * rows : q * rows + rows, lanes] for q in range(3)], axis=1)
-            f3 = jnp.concatenate([features[pl.ds(d * 16, rows), lanes] for d in range(3)], axis=1)
-            term = dot_rows(f3, out[j])
-            total = term if total is None else total + term
+            right.append(jnp.concatenate([v[q * rows : q * rows + rows, lanes] for q in range(3)], axis=1))
+            left.append(jnp.concatenate([features[pl.ds(d * 16, rows), lanes] for d in range(3)], axis=1))
+            out[j] = right[-1]
+    total = dot_rows(jnp.concatenate(left, axis=0), jnp.concatenate(right, axis=0))
     more[...] = total
     size = keep.shape[1]
     for parity in range(2):
@@ -372,7 +374,7 @@
 FIXED = None
 
 
-def call(kernel, name, ins, outs, scratch=(), aliases=None, flops=0, size=0, limit=4):
+def call(kernel, name, ins, outs, scratch=(), aliases=None, flops=0, size=0, limit=6):
     return pl.pallas_call(
         kernel,
         name=name,
@@ -456,10 +458,10 @@
         "first",
         [VMEM] * 5,
         [((2, EXT * PLANE, 9 * C), BF, FIXED), ((3 * C, 9 * C), F32, VMEM)],
-        [pltpu.VMEM(kop_shape, BF)],
+        [pltpu.VMEM(kop_shape, BF), pltpu.VMEM((4, 2, SPAN, 2 * C), BF)],
         flops=2 * work,
         size=8 * 2**20,
-        limit=6,
+        limit=12,
     )(shift, gm, own, other, pad)
     size = 27 * C // (2 * layers)
     custom = layers == 8

time: 35.2 us -> 34.6 us (0.983)
  Pallas kernels: 21.4 us -> 20.5 us
    pallas_call x1, Pallas kernels: 1.94 us -> 1.44 us  [on_device(): call(tilt_kernel if custom else lambda *refs: tilt_kernel(*refs, refs[8])...]
    pallas_call x1, Pallas kernels: 6.03 us -> 5.6 us  [on_device(): call(first_kernel, 'first', [VMEM] * 5, [((2, EXT * PLANE, 9 * C), BF, FI...]
  transfers between devices with their start and end apart: 9 -> 9, of which waited for: 1 -> 1; matrix products, arithmetic and copies ran while one was open for 0% -> 0% of each run, Pallas kernels for 48% -> 47%
where the time goes in v7:
time: 34.6 us; the launch traced here: 34.5 us
  Pallas kernels  20.5 us (59%)
  starting transfers between devices  12.3 us (36%)
  waiting for transfers between devices  0.81 us (2%)
  between operations  0.81 us (2%)
    pallas_call x2, Pallas kernels, run(): call((lambda *refs: dgrad_kernel(pieces, *refs[:6], None, *refs[6:])) if...  7.5 us
    ppermute x8, starting transfers between devices, exchange(): return lax.ppermute(value, axis, pairs)  7.42 us
    pallas_call x1, Pallas kernels, on_device(): call(first_kernel, 'first', [VMEM] * 5, [((2, EXT * PLANE, 9 * C), BF, FI...  5.6 us
    ppermute x1, starting transfers between devices, on_device(): lax.ppermute(jnp.concatenate([mine, other[MINE:]], axis=0), ('space', 'su...  4.88 us
    pallas_call x1, Pallas kernels, on_device(): call(prep_kernel, 'prep', [HBM] * 4, [((BSIDE, PLANE, 2 * C), BF, VMEM),...  1.99 us
    pallas_call x1, Pallas kernels, on_device(): call(features_kernel, 'features', [VMEM] * 2 + [HBM], [((2, (EXT + 2) * P...  1.66 us
    pallas_call x1, Pallas kernels, on_device(): call(tilt_kernel if custom else lambda *refs: tilt_kernel(*refs, refs[8])...  1.44 us
    pallas_call x1, Pallas kernels, on_device(): call(products_kernel, 'products', [VMEM] * 2, [((6 * PLANE, 3 * C), F32,...  1.26 us
  transfers between devices with their start and end apart: 9, of which 1 were waited for; matrix products, arithmetic and copies ran while one was open for 0% of the time, Pallas kernels for 47%

profile of v7, /device:TPU:0, one launch (start us, length us, event | category | flops | bytes accessed | tf_op | source)
XLA Modules:
  0.0 34.5 jit_solution(16375668496589050830)
XLA Ops:
  0.6 0.0 copy-start.2
  0.6 2.0 %prep.1 = (bf16[12,144,256]{2,1,0:T(8,128)(2,1)S(1)}, bf16[544,256]{1,0:T(8,128)(2,1)S(1)}, bf16[192,256]{1,0:T(8,128)(2,1)S(1)}, bf16[1792,256]{1,0:T(8,128)(2,1)S(1)}, bf16[64,144]{1,0:T(8,128)(2,1)S(1)}) custom-call(s32[2,6]{1,0:T(2,128)} %nb_hbm.1, s32[2,1728]{1,0:T(2,128)} %act_hbm.1, bf16[64,144]{1,0:T(8,128)(2,1)} %constant.6.clone.strips_hbm, ...), custom_call_target="tpu_custom_call" | custom-call | tf_op jit(solution)/shard_map/prep/pallas_call | solution.py:419
  2.6 0.5 %collective-permute-start = (bf16[544,256]{1,0:T(8,128)(2,1)S(1)}, bf16[544,256]{1,0:T(8,128)(2,1)S(1)}, u32[]{:S(2)}, u32[]{:S(2)}) collective-permute-start(bf16[544,256]{1,0:T(8,128)(2,1)S(1)} %get-tuple-element.33.own), channel_id=1, source_target_pairs={{0,1},{1,0},{2,3},{3,2},{4,5},{5,4},{6,7},{7,6},{8,9},{9,8},{10,11... | collective-permute-start | bytes 835592 | tf_op jit(solution)/shard_map/ppermute | solution.py:393
  3.1 1.7 %features.1 = (bf16[2,2304,128]{2,1,0:T(8,128)(2,1)S(1)}, bf16[256,256]{1,0:T(8,128)(2,1)S(1)}, bf16[256,256]{1,0:T(8,128)(2,1)S(1)}) custom-call(bf16[1792,256]{1,0:T(8,128)(2,1)S(1)} %get-tuple-element.35.mask.refs_0_, bf16[64,144]{1,0:T(8,128)(2,1)S(1)} %get-tuple-element.36.strips, bf16[2,1728,128]{2,1,0:T(8,128)(2,1)} %f_hbm.1), custom_call_target="tpu_custom_call" | custom-call | flops 10000000 | bytes 1000000 | tf_op jit(solution)/shard_map/features/pallas_call | solution.py:439
  4.8 0.1 collective-permute-start.2
  5.0 0.0 collective-permute-done.other
  5.0 4.9 %collective-permute-start.1 = (bf16[384,256]{1,0:T(8,128)(2,1)S(1)}, bf16[384,256]{1,0:T(8,128)(2,1)S(1)}, u32[]{:S(2)}, u32[]{:S(2)}) collective-permute-start(bf16[384,256]{1,0:T(8,128)(2,1)S(1)} %pad_maximum_fusion), channel_id=1, source_target_pairs={{0,2},{2,4},{4,6},{6,8},{8,10},{10,12},{12,14},{3,1},{5,3},{7,5},{... | collective-permute-start | bytes 589832 | tf_op jit(solution)/shard_map/ppermute | solution.py:450
  9.9 0.0 copy-done.2
  9.9 0.0 copy-start.1
  9.9 5.6 %first.1 = (bf16[2,2016,1152]{2,1,0:T(8,128)(2,1)S(1)}, f32[384,1152]{1,0:T(8,128)S(1)}) custom-call(bf16[352,256]{1,0:T(8,128)(2,1)S(1)} %copy-done.2, bf16[12,144,256]{2,1,0:T(8,128)(2,1)S(1)} %get-tuple-element.39.gm, bf16[544,256]{1,0:T(8,128)(2,1)S(1)} %get-tuple-element.33.own, bf16[544,256]{1,0:T(8,128)(2,1)S(1)} %collective-permute-done.other, ...), custom_call_target="tpu_custom_call" | custom-call | flops 3567255552 | bytes 8388608 | tf_op jit(solution)/shard_map/first/pallas_call | solution.py:456
  15.5 0.0 copy-start
  15.5 0.0 collective-permute-done.2.strip_other
  15.5 0.0 collective-permute-done.1.got
  15.5 0.0 copy-done.1
  15.6 1.4 %tilt.1 = (f32[8,216,128]{2,1,0:T(8,128)S(1)}, s16[8,224,128]{2,1,0:T(8,128)(2,1)S(1)}, bf16[2,224,384]{2,1,0:T(8,128)(2,1)S(1)}, bf16[2,224,384]{2,1,0:T(8,128)(2,1)S(1)}) custom-call(bf16[544,256]{1,0:T(8,128)(2,1)S(1)} %get-tuple-element.33.own, bf16[544,256]{1,0:T(8,128)(2,1)S(1)} %collective-permute-done.other, ...), custom_call_target="tpu_custom_call" | custom-call | flops 445906944 | bytes 4194304 | tf_op jit(solution)/shard_map/tilt/pallas_call | solution.py:472
  17.0 0.1 collective-permute-start.3
  17.1 0.5 %collective-permute-start.7 = (bf16[2,224,384]{2,1,0:T(8,128)(2,1)S(1)}, bf16[2,224,384]{2,1,0:T(8,128)(2,1)S(1)}, u32[]{:S(2)}, u32[]{:S(2)}) collective-permute-start(bf16[2,224,384]{2,1,0:T(8,128)(2,1)S(1)} %get-tuple-element.54), channel_id=1, source_target_pairs={{0,1},{1,0},{2,3},{3,2},{4,5},{5,4},{6,7},{7,6},{8,9},{9,8},{10,11... | collective-permute-start | bytes 1032200 | tf_op jit(solution)/shard_map/ppermute | solution.py:393
  17.6 0.0 copy-done
  17.6 1.3 %products.1.refs_5_ = f32[864,384]{1,0:T(8,128)S(1)} custom-call(bf16[27,128,128]{2,1,0:T(8,128)(2,1)S(1)} %copy-done, bf16[2,2016,1152]{2,1,0:T(8,128)(2,1)S(1)} %get-tuple-element.47.x.refs_2_), custom_call_target="tpu_custom_call" | custom-call | flops 764411904 | bytes 4194304 | tf_op jit(solution)/shard_map/products/pallas_call | solution.py:489
  18.8 0.0 collective-permute-done.3.got
  18.9 0.3 blocks.1
  19.1 2.1 %collective-permute-start.4 = (s16[2,224,128]{2,1,0:T(8,128)(2,1)S(1)}, s16[2,224,128]{2,1,0:T(8,128)(2,1)S(1)}, u32[]{:S(2)}, u32[]{:S(2)}) collective-permute-start(s16[2,224,128]{2,1,0:T(8,128)(2,1)S(1)} %get-tuple-element.50), channel_id=1, source_target_pairs={{0,2},{2,0},{4,6},{6,4},{8,10},{10,8},{12,14},{14,12},{1,3},{3,1},... | collective-permute-start | bytes 344072 | tf_op jit(solution)/shard_map/ppermute | solution.py:393
  21.2 1.6 %collective-permute-start.5 = (s16[2,224,128]{2,1,0:T(8,128)(2,1)S(1)}, s16[2,224,128]{2,1,0:T(8,128)(2,1)S(1)}, u32[]{:S(2)}, u32[]{:S(2)}) collective-permute-start(s16[2,224,128]{2,1,0:T(8,128)(2,1)S(1)} %get-tuple-element.51), channel_id=1, source_target_pairs={{0,4},{2,6},{4,0},{6,2},{8,12},{10,14},{12,8},{14,10},{1,5},{3,7},... | collective-permute-start | bytes 344072 | tf_op jit(solution)/shard_map/ppermute | solution.py:393
  22.8 0.0 collective-permute-start.6
  22.8 0.0 collective-permute-done.7.refs_4_
  22.8 4.9 %dgrad.2.refs_6_ = bf16[2,1728,128]{2,1,0:T(8,128)(2,1)} custom-call(bf16[1792,256]{1,0:T(8,128)(2,1)S(1)} %get-tuple-element.35.mask.refs_0_, bf16[27,128,128]{2,1,0:T(8,128)(2,1)S(1)} %copy-done, bf16[2,2016,1152]{2,1,0:T(8,128)(2,1)S(1)} %get-tuple-element.47.x.refs_2_, bf16[2,224,384]{2,1,0:T(8,128)(2,1)S(1)} %get-tuple-element.53.refs_3_, ...), custom_call_target="tpu_custom_call" | custom-call | flops 2675441664 | bytes 4194304 | tf_op jit(solution)/shard_map/dgrad/pallas_call | solution.py:504
  27.7 0.0 collective-permute-done.4.got_y
  27.7 0.0 collective-permute-done.5.got_z
  27.8 0.8 %collective-permute-done.6.got_yz = s16[2,224,128]{2,1,0:T(8,128)(2,1)S(1)} collective-permute-done((s16[2,224,128]{2,1,0:T(8,128)(2,1)S(1)}, s16[2,224,128]{2,1,0:T(8,128)(2,1)S(1)}, u32[]{:S(2)}, u32[]{:S(2)}) %collective-permute-start.6) | collective-permute-done | bytes 114720 | tf_op jit(solution)/shard_map/ppermute | solution.py:393
  28.5 0.1 last.1
  28.6 2.5 %collective-permute-start.8 = (s16[224,128]{1,0:T(8,128)(2,1)S(1)}, s16[224,128]{1,0:T(8,128)(2,1)S(1)}, u32[]{:S(2)}, u32[]{:S(2)}) collective-permute-start(s16[224,128]{1,0:T(8,128)(2,1)S(1)} %get-tuple-element.59), channel_id=1, source_target_pairs={{0,8},{2,10},{4,12},{6,14},{8,0},{10,2},{12,4},{14,6},{1,9},{3,11}... | collective-permute-start | bytes 172040 | tf_op jit(solution)/shard_map/ppermute | solution.py:393
  31.2 2.6 %dgrad.3 = bf16[2,1728,128]{2,1,0:T(8,128)(2,1)} custom-call(bf16[1792,256]{1,0:T(8,128)(2,1)S(1)} %get-tuple-element.35.mask.refs_0_, bf16[27,128,128]{2,1,0:T(8,128)(2,1)S(1)} %copy-done, bf16[2,2016,1152]{2,1,0:T(8,128)(2,1)S(1)} %get-tuple-element.47.x.refs_2_, ...), custom_call_target="tpu_custom_call", output_to_operand_aliasing={{}: (6, {})} | custom-call | flops 891813888 | bytes 4194304 | tf_op jit(solution)/shard_map/dgrad/pallas_call | solution.py:504
  33.8 0.0 collective-permute-done.8.got
  33.8 0.7 %sum.1 = f32[216,128]{1,0:T(8,128)} custom-call(f32[216,128]{1,0:T(8,128)S(1)} %get-tuple-element.62.keep, s16[224,128]{1,0:T(8,128)(2,1)S(1)} %collective-permute-done.8.got), custom_call_target="tpu_custom_call" | custom-call | tf_op jit(solution)/shard_map/sum/pallas_call | solution.py:412
  (2 shorter events, 0.0 us)
Async XLA Ops:
  0.6 9.3 %copy-start.2 = (bf16[352,256]{1,0:T(8,128)(2,1)S(1)}, bf16[352,256]{1,0:T(8,128)(2,1)}, u32[]{:S(2)}) copy-start(bf16[352,256]{1,0:T(8,128)(2,1)} %constant.7.clone.shift) | copy-start | bytes 540676
  2.6 2.3 %collective-permute-start = (bf16[544,256]{1,0:T(8,128)(2,1)S(1)}, bf16[544,256]{1,0:T(8,128)(2,1)S(1)}, u32[]{:S(2)}, u32[]{:S(2)}) collective-permute-start(bf16[544,256]{1,0:T(8,128)(2,1)S(1)} %get-tuple-element.33.own), channel_id=1, source_target_pairs={{0,1},{1,0},{2,3},{3,2},{4,5},{5,4},{6,7},{7,6},{8,9},{9,8},{10,11... | collective-permute-start | bytes 835592 | tf_op jit(solution)/shard_map/ppermute | solution.py:393
  4.8 10.7 %collective-permute-start.2 = (bf16[256,256]{1,0:T(8,128)(2,1)S(1)}, bf16[256,256]{1,0:T(8,128)(2,1)S(1)}, u32[]{:S(2)}, u32[]{:S(2)}) collective-permute-start(bf16[256,256]{1,0:T(8,128)(2,1)S(1)} %get-tuple-element.38), channel_id=1, source_target_pairs={{0,1},{1,0},{2,3},{3,2},{4,5},{5,4},{6,7},{7,6},{8,9},{9,8},{10,11... | collective-permute-start | bytes 393224 | tf_op jit(solution)/shard_map/ppermute | solution.py:393
  5.0 10.5 %collective-permute-start.1 = (bf16[384,256]{1,0:T(8,128)(2,1)S(1)}, bf16[384,256]{1,0:T(8,128)(2,1)S(1)}, u32[]{:S(2)}, u32[]{:S(2)}) collective-permute-start(bf16[384,256]{1,0:T(8,128)(2,1)S(1)} %pad_maximum_fusion), channel_id=1, source_target_pairs={{0,2},{2,4},{4,6},{6,8},{8,10},{10,12},{12,14},{3,1},{5,3},{7,5},{... | collective-permute-start | bytes 589832 | tf_op jit(solution)/shard_map/ppermute | solution.py:450
  9.9 5.7 %copy-start.1 = (bf16[672,224]{1,0:T(8,128)(2,1)S(1)}, bf16[672,224]{1,0:T(8,128)(2,1)}, u32[]{:S(2)}) copy-start(bf16[672,224]{1,0:T(8,128)(2,1)} %constant.8.clone.bands) | copy-start | bytes 903172
  15.5 2.1 %copy-start = (bf16[27,128,128]{2,1,0:T(8,128)(2,1)S(1)}, bf16[27,128,128]{2,1,0:T(8,128)(2,1)}, u32[]{:S(2)}) copy-start(bf16[27,128,128]{2,1,0:T(8,128)(2,1)} %refs_1_.3) | copy-start | bytes 2654212
  17.0 1.9 %collective-permute-start.3 = (s16[8,224,128]{2,1,0:T(8,128)(2,1)S(1)}, s16[8,224,128]{2,1,0:T(8,128)(2,1)S(1)}, u32[]{:S(2)}, u32[]{:S(2)}) collective-permute-start(s16[8,224,128]{2,1,0:T(8,128)(2,1)S(1)} %get-tuple-element.45), channel_id=1, source_target_pairs={{0,1},{1,0},{2,3},{3,2},{4,5},{5,4},{6,7},{7,6},{8,9},{9,8},{10,11... | collective-permute-start | bytes 1376264 | tf_op jit(solution)/shard_map/ppermute | solution.py:393
  17.1 5.7 %collective-permute-start.7 = (bf16[2,224,384]{2,1,0:T(8,128)(2,1)S(1)}, bf16[2,224,384]{2,1,0:T(8,128)(2,1)S(1)}, u32[]{:S(2)}, u32[]{:S(2)}) collective-permute-start(bf16[2,224,384]{2,1,0:T(8,128)(2,1)S(1)} %get-tuple-element.54), channel_id=1, source_target_pairs={{0,1},{1,0},{2,3},{3,2},{4,5},{5,4},{6,7},{7,6},{8,9},{9,8},{10,11... | collective-permute-start | bytes 1032200 | tf_op jit(solution)/shard_map/ppermute | solution.py:393
  19.1 8.6 %collective-permute-start.4 = (s16[2,224,128]{2,1,0:T(8,128)(2,1)S(1)}, s16[2,224,128]{2,1,0:T(8,128)(2,1)S(1)}, u32[]{:S(2)}, u32[]{:S(2)}) collective-permute-start(s16[2,224,128]{2,1,0:T(8,128)(2,1)S(1)} %get-tuple-element.50), channel_id=1, source_target_pairs={{0,2},{2,0},{4,6},{6,4},{8,10},{10,8},{12,14},{14,12},{1,3},{3,1},... | collective-permute-start | bytes 344072 | tf_op jit(solution)/shard_map/ppermute | solution.py:393
  21.2 6.5 %collective-permute-start.5 = (s16[2,224,128]{2,1,0:T(8,128)(2,1)S(1)}, s16[2,224,128]{2,1,0:T(8,128)(2,1)S(1)}, u32[]{:S(2)}, u32[]{:S(2)}) collective-permute-start(s16[2,224,128]{2,1,0:T(8,128)(2,1)S(1)} %get-tuple-element.51), channel_id=1, source_target_pairs={{0,4},{2,6},{4,0},{6,2},{8,12},{10,14},{12,8},{14,10},{1,5},{3,7},... | collective-permute-start | bytes 344072 | tf_op jit(solution)/shard_map/ppermute | solution.py:393
  22.8 5.7 %collective-permute-start.6 = (s16[2,224,128]{2,1,0:T(8,128)(2,1)S(1)}, s16[2,224,128]{2,1,0:T(8,128)(2,1)S(1)}, u32[]{:S(2)}, u32[]{:S(2)}) collective-permute-start(s16[2,224,128]{2,1,0:T(8,128)(2,1)S(1)} %get-tuple-element.52), channel_id=1, source_target_pairs={{0,6},{2,4},{4,2},{6,0},{8,14},{10,12},{12,10},{14,8},{1,7},{3,5},... | collective-permute-start | bytes 344072 | tf_op jit(solution)/shard_map/ppermute | solution.py:393
  28.6 5.1 %collective-permute-start.8 = (s16[224,128]{1,0:T(8,128)(2,1)S(1)}, s16[224,128]{1,0:T(8,128)(2,1)S(1)}, u32[]{:S(2)}, u32[]{:S(2)}) collective-permute-start(s16[224,128]{1,0:T(8,128)(2,1)S(1)} %get-tuple-element.59), channel_id=1, source_target_pairs={{0,8},{2,10},{4,12},{6,14},{8,0},{10,2},{12,4},{14,6},{1,9},{3,11}... | collective-permute-start | bytes 172040 | tf_op jit(solution)/shard_map/ppermute | solution.py:393

commit v8 on v7

--- a/solution.py
+++ b/solution.py
@@ -123,8 +123,9 @@
 
 
 def features_kernel(mask, strips, f_hbm, pad, strip, strip_send, f, sem):
-    load = pltpu.make_async_copy(f_hbm, f, sem)
-    load.start()
+    loads = [pltpu.make_async_copy(f_hbm.at[j], f.at[j], sem.at[j]) for j in range(2)]
+    for load in loads:
+        load.start()
     zero = jnp.zeros((2 * PLANE, C), BF)
     edge = jnp.zeros((32, 2 * C), BF)
     second = jnp.full((16, 2 * C), lax.axis_index("sub").astype(F32), F32).astype(BF)
@@ -134,8 +135,8 @@
     for ref in (strip, strip_send):
         ref[pl.ds(0, 32), :] = edge
         ref[pl.ds(EXT * 16, 32), :] = edge
-    load.wait()
     for j in range(2):
+        loads[j].wait()
         pad[j, pl.ds(2 * PLANE, VOX), :] = f[j] * mask[pl.ds(0, VOX), pl.ds(j * C, C)]
     for p in range(BSIDE):
         rows = pl.ds((p + 2) * PLANE, PLANE)
@@ -286,7 +287,7 @@
                     if k % 3 == 2 - 2 * parity:
                         v = v + more[at, pl.ds(k // 3 * C, C)]
                     ref = keep if block % 2 == parity else send
-                    ref[block // 2, pl.ds(row - block * size, end - row), :] = v * (1.0 / VOX)
+                    ref[block // 2, pl.ds(row - block * size, end - row), :] = v
                     row = end
 
     if code is send:
@@ -364,7 +365,7 @@
 
 
 def sum_kernel(keep, got, out):
-    out[...] = keep[...] + decoded(got, Ellipsis)
+    out[...] = (keep[...] + decoded(got, Ellipsis)) * (1.0 / VOX)
 
 
 VMEM = pl.BlockSpec(memory_space=pltpu.MemorySpace.VMEM)
@@ -441,7 +442,7 @@
         "features",
         [VMEM] * 2 + [HBM],
         [((2, (EXT + 2) * PLANE, C), BF, VMEM)] + [(((EXT + 2) * 16, 2 * C), BF, VMEM)] * 2,
-        [pltpu.VMEM((2, VOX, C), BF), pltpu.SemaphoreType.DMA],
+        [pltpu.VMEM((2, VOX, C), BF), pltpu.SemaphoreType.DMA((2,))],
         flops=10**7,
         size=10**6,
     )(mask, strips, in_hbm(features))
@@ -531,6 +532,7 @@
         even = jnp.where(first, keep, send)
         odd = jnp.where(first, send, keep)
         kernel_term = jnp.stack([even, odd], axis=1).reshape(27 * C, C)
+        kernel_term = kernel_term * (1.0 / VOX)
         weight_grad = lax.psum_scatter(kernel_term, ("space", "sub"), scatter_dimension=0, tiled=True)
         input_grad = dgrad((0, 0, 12, False), (1, 0, 12, False))(None)
     return input_grad, weight_grad

time: 34.6 us -> 34.4 us (level)
  no operation moved by 1% of the time
where the time goes in v8:
time: 34.4 us; the launch traced here: 34.3 us
  Pallas kernels  20.3 us (59%)
  starting transfers between devices  12.3 us (36%)
  waiting for transfers between devices  0.82 us (2%)
  between operations  0.81 us (2%)
    pallas_call x2, Pallas kernels, run(): call((lambda *refs: dgrad_kernel(pieces, *refs[:6], None, *refs[6:])) if...  7.49 us
    ppermute x8, starting transfers between devices, exchange(): return lax.ppermute(value, axis, pairs)  7.42 us
    pallas_call x1, Pallas kernels, on_device(): call(first_kernel, 'first', [VMEM] * 5, [((2, EXT * PLANE, 9 * C), BF, FI...  5.6 us
    ppermute x1, starting transfers between devices, on_device(): lax.ppermute(jnp.concatenate([mine, other[MINE:]], axis=0), ('space', 'su...  4.88 us
    pallas_call x1, Pallas kernels, on_device(): call(prep_kernel, 'prep', [HBM] * 4, [((BSIDE, PLANE, 2 * C), BF, VMEM),...  1.99 us
    pallas_call x1, Pallas kernels, on_device(): call(features_kernel, 'features', [VMEM] * 2 + [HBM], [((2, (EXT + 2) * P...  1.53 us
    pallas_call x1, Pallas kernels, on_device(): call(tilt_kernel if custom else lambda *refs: tilt_kernel(*refs, refs[8])...  1.4 us
    pallas_call x1, Pallas kernels, on_device(): call(products_kernel, 'products', [VMEM] * 2, [((6 * PLANE, 3 * C), F32,...  1.25 us
  transfers between devices with their start and end apart: 9, of which 1 were waited for; matrix products, arithmetic and copies ran while one was open for 0% of the time, Pallas kernels for 47%

profile of v8, /device:TPU:0, one launch (start us, length us, event | category | flops | bytes accessed | tf_op | source)
XLA Modules:
  0.0 34.3 jit_solution(16492834507665814525)
XLA Ops:
  0.6 0.0 copy-start.2
  0.6 2.0 %prep.1 = (bf16[12,144,256]{2,1,0:T(8,128)(2,1)S(1)}, bf16[544,256]{1,0:T(8,128)(2,1)S(1)}, bf16[192,256]{1,0:T(8,128)(2,1)S(1)}, bf16[1792,256]{1,0:T(8,128)(2,1)S(1)}, bf16[64,144]{1,0:T(8,128)(2,1)S(1)}) custom-call(s32[2,6]{1,0:T(2,128)} %nb_hbm.1, s32[2,1728]{1,0:T(2,128)} %act_hbm.1, bf16[64,144]{1,0:T(8,128)(2,1)} %constant.6.clone.strips_hbm, ...), custom_call_target="tpu_custom_call" | custom-call | tf_op jit(solution)/shard_map/prep/pallas_call | solution.py:420
  2.6 0.5 %collective-permute-start = (bf16[544,256]{1,0:T(8,128)(2,1)S(1)}, bf16[544,256]{1,0:T(8,128)(2,1)S(1)}, u32[]{:S(2)}, u32[]{:S(2)}) collective-permute-start(bf16[544,256]{1,0:T(8,128)(2,1)S(1)} %get-tuple-element.33.own), channel_id=1, source_target_pairs={{0,1},{1,0},{2,3},{3,2},{4,5},{5,4},{6,7},{7,6},{8,9},{9,8},{10,11... | collective-permute-start | bytes 835592 | tf_op jit(solution)/shard_map/ppermute | solution.py:394
  3.1 1.5 %features.1 = (bf16[2,2304,128]{2,1,0:T(8,128)(2,1)S(1)}, bf16[256,256]{1,0:T(8,128)(2,1)S(1)}, bf16[256,256]{1,0:T(8,128)(2,1)S(1)}) custom-call(bf16[1792,256]{1,0:T(8,128)(2,1)S(1)} %get-tuple-element.35.mask.refs_0_, bf16[64,144]{1,0:T(8,128)(2,1)S(1)} %get-tuple-element.36.strips, bf16[2,1728,128]{2,1,0:T(8,128)(2,1)} %f_hbm.1), custom_call_target="tpu_custom_call" | custom-call | flops 10000000 | bytes 1000000 | tf_op jit(solution)/shard_map/features/pallas_call | solution.py:440
  4.7 0.1 collective-permute-start.2
  4.8 0.0 collective-permute-done.other
  4.9 4.9 %collective-permute-start.1 = (bf16[384,256]{1,0:T(8,128)(2,1)S(1)}, bf16[384,256]{1,0:T(8,128)(2,1)S(1)}, u32[]{:S(2)}, u32[]{:S(2)}) collective-permute-start(bf16[384,256]{1,0:T(8,128)(2,1)S(1)} %pad_maximum_fusion), channel_id=1, source_target_pairs={{0,2},{2,4},{4,6},{6,8},{8,10},{10,12},{12,14},{3,1},{5,3},{7,5},{... | collective-permute-start | bytes 589832 | tf_op jit(solution)/shard_map/ppermute | solution.py:451
  9.7 0.0 copy-done.2
  9.8 0.0 copy-start.1
  9.8 5.6 %first.1 = (bf16[2,2016,1152]{2,1,0:T(8,128)(2,1)S(1)}, f32[384,1152]{1,0:T(8,128)S(1)}) custom-call(bf16[352,256]{1,0:T(8,128)(2,1)S(1)} %copy-done.2, bf16[12,144,256]{2,1,0:T(8,128)(2,1)S(1)} %get-tuple-element.39.gm, bf16[544,256]{1,0:T(8,128)(2,1)S(1)} %get-tuple-element.33.own, bf16[544,256]{1,0:T(8,128)(2,1)S(1)} %collective-permute-done.other, ...), custom_call_target="tpu_custom_call" | custom-call | flops 3567255552 | bytes 8388608 | tf_op jit(solution)/shard_map/first/pallas_call | solution.py:457
  15.4 0.0 copy-start
  15.4 0.0 collective-permute-done.2.strip_other
  15.4 0.0 collective-permute-done.1.got
  15.4 0.0 copy-done.1
  15.4 1.4 %tilt.1 = (f32[8,216,128]{2,1,0:T(8,128)S(1)}, s16[8,224,128]{2,1,0:T(8,128)(2,1)S(1)}, bf16[2,224,384]{2,1,0:T(8,128)(2,1)S(1)}, bf16[2,224,384]{2,1,0:T(8,128)(2,1)S(1)}) custom-call(bf16[544,256]{1,0:T(8,128)(2,1)S(1)} %get-tuple-element.33.own, bf16[544,256]{1,0:T(8,128)(2,1)S(1)} %collective-permute-done.other, ...), custom_call_target="tpu_custom_call" | custom-call | flops 445906944 | bytes 4194304 | tf_op jit(solution)/shard_map/tilt/pallas_call | solution.py:473
  16.8 0.1 collective-permute-start.3
  16.9 0.5 %collective-permute-start.7 = (bf16[2,224,384]{2,1,0:T(8,128)(2,1)S(1)}, bf16[2,224,384]{2,1,0:T(8,128)(2,1)S(1)}, u32[]{:S(2)}, u32[]{:S(2)}) collective-permute-start(bf16[2,224,384]{2,1,0:T(8,128)(2,1)S(1)} %get-tuple-element.54), channel_id=1, source_target_pairs={{0,1},{1,0},{2,3},{3,2},{4,5},{5,4},{6,7},{7,6},{8,9},{9,8},{10,11... | collective-permute-start | bytes 1032200 | tf_op jit(solution)/shard_map/ppermute | solution.py:394
  17.4 0.0 copy-done
  17.4 1.3 %products.1.refs_5_ = f32[864,384]{1,0:T(8,128)S(1)} custom-call(bf16[27,128,128]{2,1,0:T(8,128)(2,1)S(1)} %copy-done, bf16[2,2016,1152]{2,1,0:T(8,128)(2,1)S(1)} %get-tuple-element.47.x.refs_2_), custom_call_target="tpu_custom_call" | custom-call | flops 764411904 | bytes 4194304 | tf_op jit(solution)/shard_map/products/pallas_call | solution.py:490
  18.7 0.0 collective-permute-done.3.got
  18.7 0.3 blocks.1
  19.0 2.1 %collective-permute-start.4 = (s16[2,224,128]{2,1,0:T(8,128)(2,1)S(1)}, s16[2,224,128]{2,1,0:T(8,128)(2,1)S(1)}, u32[]{:S(2)}, u32[]{:S(2)}) collective-permute-start(s16[2,224,128]{2,1,0:T(8,128)(2,1)S(1)} %get-tuple-element.50), channel_id=1, source_target_pairs={{0,2},{2,0},{4,6},{6,4},{8,10},{10,8},{12,14},{14,12},{1,3},{3,1},... | collective-permute-start | bytes 344072 | tf_op jit(solution)/shard_map/ppermute | solution.py:394
  21.1 1.6 %collective-permute-start.5 = (s16[2,224,128]{2,1,0:T(8,128)(2,1)S(1)}, s16[2,224,128]{2,1,0:T(8,128)(2,1)S(1)}, u32[]{:S(2)}, u32[]{:S(2)}) collective-permute-start(s16[2,224,128]{2,1,0:T(8,128)(2,1)S(1)} %get-tuple-element.51), channel_id=1, source_target_pairs={{0,4},{2,6},{4,0},{6,2},{8,12},{10,14},{12,8},{14,10},{1,5},{3,7},... | collective-permute-start | bytes 344072 | tf_op jit(solution)/shard_map/ppermute | solution.py:394
  22.6 0.0 collective-permute-start.6
  22.6 0.0 collective-permute-done.7.refs_4_
  22.7 4.9 %dgrad.2.refs_6_ = bf16[2,1728,128]{2,1,0:T(8,128)(2,1)} custom-call(bf16[1792,256]{1,0:T(8,128)(2,1)S(1)} %get-tuple-element.35.mask.refs_0_, bf16[27,128,128]{2,1,0:T(8,128)(2,1)S(1)} %copy-done, bf16[2,2016,1152]{2,1,0:T(8,128)(2,1)S(1)} %get-tuple-element.47.x.refs_2_, bf16[2,224,384]{2,1,0:T(8,128)(2,1)S(1)} %get-tuple-element.53.refs_3_, ...), custom_call_target="tpu_custom_call" | custom-call | flops 2675441664 | bytes 4194304 | tf_op jit(solution)/shard_map/dgrad/pallas_call | solution.py:505
  27.6 0.0 collective-permute-done.4.got_y
  27.6 0.0 collective-permute-done.5.got_z
  27.6 0.8 %collective-permute-done.6.got_yz = s16[2,224,128]{2,1,0:T(8,128)(2,1)S(1)} collective-permute-done((s16[2,224,128]{2,1,0:T(8,128)(2,1)S(1)}, s16[2,224,128]{2,1,0:T(8,128)(2,1)S(1)}, u32[]{:S(2)}, u32[]{:S(2)}) %collective-permute-start.6) | collective-permute-done | bytes 114720 | tf_op jit(solution)/shard_map/ppermute | solution.py:394
  28.3 0.1 last.1
  28.5 2.5 %collective-permute-start.8 = (s16[224,128]{1,0:T(8,128)(2,1)S(1)}, s16[224,128]{1,0:T(8,128)(2,1)S(1)}, u32[]{:S(2)}, u32[]{:S(2)}) collective-permute-start(s16[224,128]{1,0:T(8,128)(2,1)S(1)} %get-tuple-element.59), channel_id=1, source_target_pairs={{0,8},{2,10},{4,12},{6,14},{8,0},{10,2},{12,4},{14,6},{1,9},{3,11}... | collective-permute-start | bytes 172040 | tf_op jit(solution)/shard_map/ppermute | solution.py:394
  31.0 2.6 %dgrad.3 = bf16[2,1728,128]{2,1,0:T(8,128)(2,1)} custom-call(bf16[1792,256]{1,0:T(8,128)(2,1)S(1)} %get-tuple-element.35.mask.refs_0_, bf16[27,128,128]{2,1,0:T(8,128)(2,1)S(1)} %copy-done, bf16[2,2016,1152]{2,1,0:T(8,128)(2,1)S(1)} %get-tuple-element.47.x.refs_2_, ...), custom_call_target="tpu_custom_call", output_to_operand_aliasing={{}: (6, {})} | custom-call | flops 891813888 | bytes 4194304 | tf_op jit(solution)/shard_map/dgrad/pallas_call | solution.py:505
  33.6 0.0 collective-permute-done.8.got
  33.6 0.7 %sum.1 = f32[216,128]{1,0:T(8,128)} custom-call(f32[216,128]{1,0:T(8,128)S(1)} %get-tuple-element.62.keep, s16[224,128]{1,0:T(8,128)(2,1)S(1)} %collective-permute-done.8.got), custom_call_target="tpu_custom_call" | custom-call | tf_op jit(solution)/shard_map/sum/pallas_call | solution.py:413
  (2 shorter events, 0.0 us)
Async XLA Ops:
  0.6 9.1 %copy-start.2 = (bf16[352,256]{1,0:T(8,128)(2,1)S(1)}, bf16[352,256]{1,0:T(8,128)(2,1)}, u32[]{:S(2)}) copy-start(bf16[352,256]{1,0:T(8,128)(2,1)} %constant.7.clone.shift) | copy-start | bytes 540676
  2.6 2.2 %collective-permute-start = (bf16[544,256]{1,0:T(8,128)(2,1)S(1)}, bf16[544,256]{1,0:T(8,128)(2,1)S(1)}, u32[]{:S(2)}, u32[]{:S(2)}) collective-permute-start(bf16[544,256]{1,0:T(8,128)(2,1)S(1)} %get-tuple-element.33.own), channel_id=1, source_target_pairs={{0,1},{1,0},{2,3},{3,2},{4,5},{5,4},{6,7},{7,6},{8,9},{9,8},{10,11... | collective-permute-start | bytes 835592 | tf_op jit(solution)/shard_map/ppermute | solution.py:394
  4.7 10.7 %collective-permute-start.2 = (bf16[256,256]{1,0:T(8,128)(2,1)S(1)}, bf16[256,256]{1,0:T(8,128)(2,1)S(1)}, u32[]{:S(2)}, u32[]{:S(2)}) collective-permute-start(bf16[256,256]{1,0:T(8,128)(2,1)S(1)} %get-tuple-element.38), channel_id=1, source_target_pairs={{0,1},{1,0},{2,3},{3,2},{4,5},{5,4},{6,7},{7,6},{8,9},{9,8},{10,11... | collective-permute-start | bytes 393224 | tf_op jit(solution)/shard_map/ppermute | solution.py:394
  4.9 10.5 %collective-permute-start.1 = (bf16[384,256]{1,0:T(8,128)(2,1)S(1)}, bf16[384,256]{1,0:T(8,128)(2,1)S(1)}, u32[]{:S(2)}, u32[]{:S(2)}) collective-permute-start(bf16[384,256]{1,0:T(8,128)(2,1)S(1)} %pad_maximum_fusion), channel_id=1, source_target_pairs={{0,2},{2,4},{4,6},{6,8},{8,10},{10,12},{12,14},{3,1},{5,3},{7,5},{... | collective-permute-start | bytes 589832 | tf_op jit(solution)/shard_map/ppermute | solution.py:451
  9.8 5.7 %copy-start.1 = (bf16[672,224]{1,0:T(8,128)(2,1)S(1)}, bf16[672,224]{1,0:T(8,128)(2,1)}, u32[]{:S(2)}) copy-start(bf16[672,224]{1,0:T(8,128)(2,1)} %constant.8.clone.bands) | copy-start | bytes 903172
  15.4 2.0 %copy-start = (bf16[27,128,128]{2,1,0:T(8,128)(2,1)S(1)}, bf16[27,128,128]{2,1,0:T(8,128)(2,1)}, u32[]{:S(2)}) copy-start(bf16[27,128,128]{2,1,0:T(8,128)(2,1)} %refs_1_.3) | copy-start | bytes 2654212
  16.8 1.9 %collective-permute-start.3 = (s16[8,224,128]{2,1,0:T(8,128)(2,1)S(1)}, s16[8,224,128]{2,1,0:T(8,128)(2,1)S(1)}, u32[]{:S(2)}, u32[]{:S(2)}) collective-permute-start(s16[8,224,128]{2,1,0:T(8,128)(2,1)S(1)} %get-tuple-element.45), channel_id=1, source_target_pairs={{0,1},{1,0},{2,3},{3,2},{4,5},{5,4},{6,7},{7,6},{8,9},{9,8},{10,11... | collective-permute-start | bytes 1376264 | tf_op jit(solution)/shard_map/ppermute | solution.py:394
  16.9 5.7 %collective-permute-start.7 = (bf16[2,224,384]{2,1,0:T(8,128)(2,1)S(1)}, bf16[2,224,384]{2,1,0:T(8,128)(2,1)S(1)}, u32[]{:S(2)}, u32[]{:S(2)}) collective-permute-start(bf16[2,224,384]{2,1,0:T(8,128)(2,1)S(1)} %get-tuple-element.54), channel_id=1, source_target_pairs={{0,1},{1,0},{2,3},{3,2},{4,5},{5,4},{6,7},{7,6},{8,9},{9,8},{10,11... | collective-permute-start | bytes 1032200 | tf_op jit(solution)/shard_map/ppermute | solution.py:394
  19.0 8.6 %collective-permute-start.4 = (s16[2,224,128]{2,1,0:T(8,128)(2,1)S(1)}, s16[2,224,128]{2,1,0:T(8,128)(2,1)S(1)}, u32[]{:S(2)}, u32[]{:S(2)}) collective-permute-start(s16[2,224,128]{2,1,0:T(8,128)(2,1)S(1)} %get-tuple-element.50), channel_id=1, source_target_pairs={{0,2},{2,0},{4,6},{6,4},{8,10},{10,8},{12,14},{14,12},{1,3},{3,1},... | collective-permute-start | bytes 344072 | tf_op jit(solution)/shard_map/ppermute | solution.py:394
  21.1 6.5 %collective-permute-start.5 = (s16[2,224,128]{2,1,0:T(8,128)(2,1)S(1)}, s16[2,224,128]{2,1,0:T(8,128)(2,1)S(1)}, u32[]{:S(2)}, u32[]{:S(2)}) collective-permute-start(s16[2,224,128]{2,1,0:T(8,128)(2,1)S(1)} %get-tuple-element.51), channel_id=1, source_target_pairs={{0,4},{2,6},{4,0},{6,2},{8,12},{10,14},{12,8},{14,10},{1,5},{3,7},... | collective-permute-start | bytes 344072 | tf_op jit(solution)/shard_map/ppermute | solution.py:394
  22.6 5.7 %collective-permute-start.6 = (s16[2,224,128]{2,1,0:T(8,128)(2,1)S(1)}, s16[2,224,128]{2,1,0:T(8,128)(2,1)S(1)}, u32[]{:S(2)}, u32[]{:S(2)}) collective-permute-start(s16[2,224,128]{2,1,0:T(8,128)(2,1)S(1)} %get-tuple-element.52), channel_id=1, source_target_pairs={{0,6},{2,4},{4,2},{6,0},{8,14},{10,12},{12,10},{14,8},{1,7},{3,5},... | collective-permute-start | bytes 344072 | tf_op jit(solution)/shard_map/ppermute | solution.py:394
  28.5 5.1 %collective-permute-start.8 = (s16[224,128]{1,0:T(8,128)(2,1)S(1)}, s16[224,128]{1,0:T(8,128)(2,1)S(1)}, u32[]{:S(2)}, u32[]{:S(2)}) collective-permute-start(s16[224,128]{1,0:T(8,128)(2,1)S(1)} %get-tuple-element.59), channel_id=1, source_target_pairs={{0,8},{2,10},{4,12},{6,14},{8,0},{10,2},{12,4},{14,6},{1,9},{3,11}... | collective-permute-start | bytes 172040 | tf_op jit(solution)/shard_map/ppermute | solution.py:394

commit v9 on v8

--- a/solution.py
+++ b/solution.py
@@ -526,7 +526,7 @@
 
     if custom:
         got, zs, ready = tied(got, zs, ready)
-        weight_grad, input_grad = reduce_blocks(keep, got, [dgrad((0, 0, 12, False), (1, 0, 4, True), (1, 4, 2, False)), dgrad((1, 6, 6, False))])
+        weight_grad, input_grad = reduce_blocks(keep, got, [dgrad((0, 0, 12, False), (1, 0, 4, True), (1, 4, 4, False)), dgrad((1, 8, 4, False))])
     else:
         first = lax.axis_index("sub") == 0
         even = jnp.where(first, keep, send)

time: 34.4 us -> 34.4 us (level)
  transfers between devices with their start and end apart: 9 -> 9, of which waited for: 1 -> 2; matrix products, arithmetic and copies ran while one was open for 0% -> 0% of each run, Pallas kernels for 47% -> 47%
where the time goes in v9:
time: 34.4 us; the launch traced here: 34.3 us
  Pallas kernels  20.3 us (59%)
  starting transfers between devices  12.3 us (36%)
  waiting for transfers between devices  0.86 us (2%)
  between operations  0.8 us (2%)
    pallas_call x2, Pallas kernels, run(): call((lambda *refs: dgrad_kernel(pieces, *refs[:6], None, *refs[6:])) if...  7.45 us
    ppermute x8, starting transfers between devices, exchange(): return lax.ppermute(value, axis, pairs)  7.42 us
    pallas_call x1, Pallas kernels, on_device(): call(first_kernel, 'first', [VMEM] * 5, [((2, EXT * PLANE, 9 * C), BF, FI...  5.6 us
    ppermute x1, starting transfers between devices, on_device(): lax.ppermute(jnp.concatenate([mine, other[MINE:]], axis=0), ('space', 'su...  4.88 us
    pallas_call x1, Pallas kernels, on_device(): call(prep_kernel, 'prep', [HBM] * 4, [((BSIDE, PLANE, 2 * C), BF, VMEM),...  1.99 us
    pallas_call x1, Pallas kernels, on_device(): call(features_kernel, 'features', [VMEM] * 2 + [HBM], [((2, (EXT + 2) * P...  1.53 us
    pallas_call x1, Pallas kernels, on_device(): call(tilt_kernel if custom else lambda *refs: tilt_kernel(*refs, refs[8])...  1.4 us
    pallas_call x1, Pallas kernels, on_device(): call(products_kernel, 'products', [VMEM] * 2, [((6 * PLANE, 3 * C), F32,...  1.25 us
  transfers between devices with their start and end apart: 9, of which 2 were waited for; matrix products, arithmetic and copies ran while one was open for 0% of the time, Pallas kernels for 47%

profile of v9, /device:TPU:0, one launch (start us, length us, event | category | flops | bytes accessed | tf_op | source)
XLA Modules:
  0.0 34.3 jit_solution(8733575717851274863)
XLA Ops:
  0.6 0.0 copy-start.2
  0.6 2.0 %prep.1 = (bf16[12,144,256]{2,1,0:T(8,128)(2,1)S(1)}, bf16[544,256]{1,0:T(8,128)(2,1)S(1)}, bf16[192,256]{1,0:T(8,128)(2,1)S(1)}, bf16[1792,256]{1,0:T(8,128)(2,1)S(1)}, bf16[64,144]{1,0:T(8,128)(2,1)S(1)}) custom-call(s32[2,6]{1,0:T(2,128)} %nb_hbm.1, s32[2,1728]{1,0:T(2,128)} %act_hbm.1, bf16[64,144]{1,0:T(8,128)(2,1)} %constant.6.clone.strips_hbm, ...), custom_call_target="tpu_custom_call" | custom-call | tf_op jit(solution)/shard_map/prep/pallas_call | solution.py:420
  2.6 0.5 %collective-permute-start = (bf16[544,256]{1,0:T(8,128)(2,1)S(1)}, bf16[544,256]{1,0:T(8,128)(2,1)S(1)}, u32[]{:S(2)}, u32[]{:S(2)}) collective-permute-start(bf16[544,256]{1,0:T(8,128)(2,1)S(1)} %get-tuple-element.33.own), channel_id=1, source_target_pairs={{0,1},{1,0},{2,3},{3,2},{4,5},{5,4},{6,7},{7,6},{8,9},{9,8},{10,11... | collective-permute-start | bytes 835592 | tf_op jit(solution)/shard_map/ppermute | solution.py:394
  3.1 1.5 %features.1 = (bf16[2,2304,128]{2,1,0:T(8,128)(2,1)S(1)}, bf16[256,256]{1,0:T(8,128)(2,1)S(1)}, bf16[256,256]{1,0:T(8,128)(2,1)S(1)}) custom-call(bf16[1792,256]{1,0:T(8,128)(2,1)S(1)} %get-tuple-element.35.mask.refs_0_, bf16[64,144]{1,0:T(8,128)(2,1)S(1)} %get-tuple-element.36.strips, bf16[2,1728,128]{2,1,0:T(8,128)(2,1)} %f_hbm.1), custom_call_target="tpu_custom_call" | custom-call | flops 10000000 | bytes 1000000 | tf_op jit(solution)/shard_map/features/pallas_call | solution.py:440
  4.7 0.1 collective-permute-start.2
  4.8 0.0 collective-permute-done.other
  4.9 4.9 %collective-permute-start.1 = (bf16[384,256]{1,0:T(8,128)(2,1)S(1)}, bf16[384,256]{1,0:T(8,128)(2,1)S(1)}, u32[]{:S(2)}, u32[]{:S(2)}) collective-permute-start(bf16[384,256]{1,0:T(8,128)(2,1)S(1)} %pad_maximum_fusion), channel_id=1, source_target_pairs={{0,2},{2,4},{4,6},{6,8},{8,10},{10,12},{12,14},{3,1},{5,3},{7,5},{... | collective-permute-start | bytes 589832 | tf_op jit(solution)/shard_map/ppermute | solution.py:451
  9.7 0.0 copy-done.2
  9.8 0.0 copy-start.1
  9.8 5.6 %first.1 = (bf16[2,2016,1152]{2,1,0:T(8,128)(2,1)S(1)}, f32[384,1152]{1,0:T(8,128)S(1)}) custom-call(bf16[352,256]{1,0:T(8,128)(2,1)S(1)} %copy-done.2, bf16[12,144,256]{2,1,0:T(8,128)(2,1)S(1)} %get-tuple-element.39.gm, bf16[544,256]{1,0:T(8,128)(2,1)S(1)} %get-tuple-element.33.own, bf16[544,256]{1,0:T(8,128)(2,1)S(1)} %collective-permute-done.other, ...), custom_call_target="tpu_custom_call" | custom-call | flops 3567255552 | bytes 8388608 | tf_op jit(solution)/shard_map/first/pallas_call | solution.py:457
  15.4 0.0 copy-start
  15.4 0.0 collective-permute-done.2.strip_other
  15.4 0.0 collective-permute-done.1.got
  15.4 0.0 copy-done.1
  15.4 1.4 %tilt.1 = (f32[8,216,128]{2,1,0:T(8,128)S(1)}, s16[8,224,128]{2,1,0:T(8,128)(2,1)S(1)}, bf16[2,224,384]{2,1,0:T(8,128)(2,1)S(1)}, bf16[2,224,384]{2,1,0:T(8,128)(2,1)S(1)}) custom-call(bf16[544,256]{1,0:T(8,128)(2,1)S(1)} %get-tuple-element.33.own, bf16[544,256]{1,0:T(8,128)(2,1)S(1)} %collective-permute-done.other, ...), custom_call_target="tpu_custom_call" | custom-call | flops 445906944 | bytes 4194304 | tf_op jit(solution)/shard_map/tilt/pallas_call | solution.py:473
  16.8 0.1 collective-permute-start.3
  16.9 0.5 %collective-permute-start.7 = (bf16[2,224,384]{2,1,0:T(8,128)(2,1)S(1)}, bf16[2,224,384]{2,1,0:T(8,128)(2,1)S(1)}, u32[]{:S(2)}, u32[]{:S(2)}) collective-permute-start(bf16[2,224,384]{2,1,0:T(8,128)(2,1)S(1)} %get-tuple-element.54), channel_id=1, source_target_pairs={{0,1},{1,0},{2,3},{3,2},{4,5},{5,4},{6,7},{7,6},{8,9},{9,8},{10,11... | collective-permute-start | bytes 1032200 | tf_op jit(solution)/shard_map/ppermute | solution.py:394
  17.4 0.0 copy-done
  17.4 1.3 %products.1.refs_5_ = f32[864,384]{1,0:T(8,128)S(1)} custom-call(bf16[27,128,128]{2,1,0:T(8,128)(2,1)S(1)} %copy-done, bf16[2,2016,1152]{2,1,0:T(8,128)(2,1)S(1)} %get-tuple-element.47.x.refs_2_), custom_call_target="tpu_custom_call" | custom-call | flops 764411904 | bytes 4194304 | tf_op jit(solution)/shard_map/products/pallas_call | solution.py:490
  18.7 0.0 collective-permute-done.3.got
  18.7 0.3 blocks.1
  19.0 2.1 %collective-permute-start.4 = (s16[2,224,128]{2,1,0:T(8,128)(2,1)S(1)}, s16[2,224,128]{2,1,0:T(8,128)(2,1)S(1)}, u32[]{:S(2)}, u32[]{:S(2)}) collective-permute-start(s16[2,224,128]{2,1,0:T(8,128)(2,1)S(1)} %get-tuple-element.50), channel_id=1, source_target_pairs={{0,2},{2,0},{4,6},{6,4},{8,10},{10,8},{12,14},{14,12},{1,3},{3,1},... | collective-permute-start | bytes 344072 | tf_op jit(solution)/shard_map/ppermute | solution.py:394
  21.1 1.6 %collective-permute-start.5 = (s16[2,224,128]{2,1,0:T(8,128)(2,1)S(1)}, s16[2,224,128]{2,1,0:T(8,128)(2,1)S(1)}, u32[]{:S(2)}, u32[]{:S(2)}) collective-permute-start(s16[2,224,128]{2,1,0:T(8,128)(2,1)S(1)} %get-tuple-element.51), channel_id=1, source_target_pairs={{0,4},{2,6},{4,0},{6,2},{8,12},{10,14},{12,8},{14,10},{1,5},{3,7},... | collective-permute-start | bytes 344072 | tf_op jit(solution)/shard_map/ppermute | solution.py:394
  22.6 0.0 collective-permute-start.6
  22.6 0.0 collective-permute-done.7.refs_4_
  22.7 5.3 %dgrad.2.refs_6_ = bf16[2,1728,128]{2,1,0:T(8,128)(2,1)} custom-call(bf16[1792,256]{1,0:T(8,128)(2,1)S(1)} %get-tuple-element.35.mask.refs_0_, bf16[27,128,128]{2,1,0:T(8,128)(2,1)S(1)} %copy-done, bf16[2,2016,1152]{2,1,0:T(8,128)(2,1)S(1)} %get-tuple-element.47.x.refs_2_, bf16[2,224,384]{2,1,0:T(8,128)(2,1)S(1)} %get-tuple-element.53.refs_3_, ...), custom_call_target="tpu_custom_call" | custom-call | flops 2972712960 | bytes 4194304 | tf_op jit(solution)/shard_map/dgrad/pallas_call | solution.py:505
  27.9 0.0 collective-permute-done.4.got_y
  27.9 0.0 collective-permute-done.5.got_z
  28.0 0.4 %collective-permute-done.6.got_yz = s16[2,224,128]{2,1,0:T(8,128)(2,1)S(1)} collective-permute-done((s16[2,224,128]{2,1,0:T(8,128)(2,1)S(1)}, s16[2,224,128]{2,1,0:T(8,128)(2,1)S(1)}, u32[]{:S(2)}, u32[]{:S(2)}) %collective-permute-start.6) | collective-permute-done | bytes 114720 | tf_op jit(solution)/shard_map/ppermute | solution.py:394
  28.3 0.1 last.1
  28.5 2.5 %collective-permute-start.8 = (s16[224,128]{1,0:T(8,128)(2,1)S(1)}, s16[224,128]{1,0:T(8,128)(2,1)S(1)}, u32[]{:S(2)}, u32[]{:S(2)}) collective-permute-start(s16[224,128]{1,0:T(8,128)(2,1)S(1)} %get-tuple-element.59), channel_id=1, source_target_pairs={{0,8},{2,10},{4,12},{6,14},{8,0},{10,2},{12,4},{14,6},{1,9},{3,11}... | collective-permute-start | bytes 172040 | tf_op jit(solution)/shard_map/ppermute | solution.py:394
  31.0 2.2 %dgrad.3 = bf16[2,1728,128]{2,1,0:T(8,128)(2,1)} custom-call(bf16[1792,256]{1,0:T(8,128)(2,1)S(1)} %get-tuple-element.35.mask.refs_0_, bf16[27,128,128]{2,1,0:T(8,128)(2,1)S(1)} %copy-done, bf16[2,2016,1152]{2,1,0:T(8,128)(2,1)S(1)} %get-tuple-element.47.x.refs_2_, ...), custom_call_target="tpu_custom_call", output_to_operand_aliasing={{}: (6, {})} | custom-call | flops 594542592 | bytes 4194304 | tf_op jit(solution)/shard_map/dgrad/pallas_call | solution.py:505
  33.2 0.4 %collective-permute-done.8.got = s16[224,128]{1,0:T(8,128)(2,1)S(1)} collective-permute-done((s16[224,128]{1,0:T(8,128)(2,1)S(1)}, s16[224,128]{1,0:T(8,128)(2,1)S(1)}, u32[]{:S(2)}, u32[]{:S(2)}) %collective-permute-start.8) | collective-permute-done | bytes 57376 | tf_op jit(solution)/shard_map/ppermute | solution.py:394
  33.6 0.7 %sum.1 = f32[216,128]{1,0:T(8,128)} custom-call(f32[216,128]{1,0:T(8,128)S(1)} %get-tuple-element.62.keep, s16[224,128]{1,0:T(8,128)(2,1)S(1)} %collective-permute-done.8.got), custom_call_target="tpu_custom_call" | custom-call | tf_op jit(solution)/shard_map/sum/pallas_call | solution.py:413
  (2 shorter events, 0.0 us)
Async XLA Ops:
  0.6 9.1 %copy-start.2 = (bf16[352,256]{1,0:T(8,128)(2,1)S(1)}, bf16[352,256]{1,0:T(8,128)(2,1)}, u32[]{:S(2)}) copy-start(bf16[352,256]{1,0:T(8,128)(2,1)} %constant.7.clone.shift) | copy-start | bytes 540676
  2.6 2.2 %collective-permute-start = (bf16[544,256]{1,0:T(8,128)(2,1)S(1)}, bf16[544,256]{1,0:T(8,128)(2,1)S(1)}, u32[]{:S(2)}, u32[]{:S(2)}) collective-permute-start(bf16[544,256]{1,0:T(8,128)(2,1)S(1)} %get-tuple-element.33.own), channel_id=1, source_target_pairs={{0,1},{1,0},{2,3},{3,2},{4,5},{5,4},{6,7},{7,6},{8,9},{9,8},{10,11... | collective-permute-start | bytes 835592 | tf_op jit(solution)/shard_map/ppermute | solution.py:394
  4.7 10.7 %collective-permute-start.2 = (bf16[256,256]{1,0:T(8,128)(2,1)S(1)}, bf16[256,256]{1,0:T(8,128)(2,1)S(1)}, u32[]{:S(2)}, u32[]{:S(2)}) collective-permute-start(bf16[256,256]{1,0:T(8,128)(2,1)S(1)} %get-tuple-element.38), channel_id=1, source_target_pairs={{0,1},{1,0},{2,3},{3,2},{4,5},{5,4},{6,7},{7,6},{8,9},{9,8},{10,11... | collective-permute-start | bytes 393224 | tf_op jit(solution)/shard_map/ppermute | solution.py:394
  4.9 10.5 %collective-permute-start.1 = (bf16[384,256]{1,0:T(8,128)(2,1)S(1)}, bf16[384,256]{1,0:T(8,128)(2,1)S(1)}, u32[]{:S(2)}, u32[]{:S(2)}) collective-permute-start(bf16[384,256]{1,0:T(8,128)(2,1)S(1)} %pad_maximum_fusion), channel_id=1, source_target_pairs={{0,2},{2,4},{4,6},{6,8},{8,10},{10,12},{12,14},{3,1},{5,3},{7,5},{... | collective-permute-start | bytes 589832 | tf_op jit(solution)/shard_map/ppermute | solution.py:451
  9.8 5.7 %copy-start.1 = (bf16[672,224]{1,0:T(8,128)(2,1)S(1)}, bf16[672,224]{1,0:T(8,128)(2,1)}, u32[]{:S(2)}) copy-start(bf16[672,224]{1,0:T(8,128)(2,1)} %constant.8.clone.bands) | copy-start | bytes 903172
  15.4 2.0 %copy-start = (bf16[27,128,128]{2,1,0:T(8,128)(2,1)S(1)}, bf16[27,128,128]{2,1,0:T(8,128)(2,1)}, u32[]{:S(2)}) copy-start(bf16[27,128,128]{2,1,0:T(8,128)(2,1)} %refs_1_.3) | copy-start | bytes 2654212
  16.8 1.9 %collective-permute-start.3 = (s16[8,224,128]{2,1,0:T(8,128)(2,1)S(1)}, s16[8,224,128]{2,1,0:T(8,128)(2,1)S(1)}, u32[]{:S(2)}, u32[]{:S(2)}) collective-permute-start(s16[8,224,128]{2,1,0:T(8,128)(2,1)S(1)} %get-tuple-element.45), channel_id=1, source_target_pairs={{0,1},{1,0},{2,3},{3,2},{4,5},{5,4},{6,7},{7,6},{8,9},{9,8},{10,11... | collective-permute-start | bytes 1376264 | tf_op jit(solution)/shard_map/ppermute | solution.py:394
  16.9 5.7 %collective-permute-start.7 = (bf16[2,224,384]{2,1,0:T(8,128)(2,1)S(1)}, bf16[2,224,384]{2,1,0:T(8,128)(2,1)S(1)}, u32[]{:S(2)}, u32[]{:S(2)}) collective-permute-start(bf16[2,224,384]{2,1,0:T(8,128)(2,1)S(1)} %get-tuple-element.54), channel_id=1, source_target_pairs={{0,1},{1,0},{2,3},{3,2},{4,5},{5,4},{6,7},{7,6},{8,9},{9,8},{10,11... | collective-permute-start | bytes 1032200 | tf_op jit(solution)/shard_map/ppermute | solution.py:394
  19.0 9.0 %collective-permute-start.4 = (s16[2,224,128]{2,1,0:T(8,128)(2,1)S(1)}, s16[2,224,128]{2,1,0:T(8,128)(2,1)S(1)}, u32[]{:S(2)}, u32[]{:S(2)}) collective-permute-start(s16[2,224,128]{2,1,0:T(8,128)(2,1)S(1)} %get-tuple-element.50), channel_id=1, source_target_pairs={{0,2},{2,0},{4,6},{6,4},{8,10},{10,8},{12,14},{14,12},{1,3},{3,1},... | collective-permute-start | bytes 344072 | tf_op jit(solution)/shard_map/ppermute | solution.py:394
  21.1 6.9 %collective-permute-start.5 = (s16[2,224,128]{2,1,0:T(8,128)(2,1)S(1)}, s16[2,224,128]{2,1,0:T(8,128)(2,1)S(1)}, u32[]{:S(2)}, u32[]{:S(2)}) collective-permute-start(s16[2,224,128]{2,1,0:T(8,128)(2,1)S(1)} %get-tuple-element.51), channel_id=1, source_target_pairs={{0,4},{2,6},{4,0},{6,2},{8,12},{10,14},{12,8},{14,10},{1,5},{3,7},... | collective-permute-start | bytes 344072 | tf_op jit(solution)/shard_map/ppermute | solution.py:394
  22.6 5.7 %collective-permute-start.6 = (s16[2,224,128]{2,1,0:T(8,128)(2,1)S(1)}, s16[2,224,128]{2,1,0:T(8,128)(2,1)S(1)}, u32[]{:S(2)}, u32[]{:S(2)}) collective-permute-start(s16[2,224,128]{2,1,0:T(8,128)(2,1)S(1)} %get-tuple-element.52), channel_id=1, source_target_pairs={{0,6},{2,4},{4,2},{6,0},{8,14},{10,12},{12,10},{14,8},{1,7},{3,5},... | collective-permute-start | bytes 344072 | tf_op jit(solution)/shard_map/ppermute | solution.py:394
  28.5 5.1 %collective-permute-start.8 = (s16[224,128]{1,0:T(8,128)(2,1)S(1)}, s16[224,128]{1,0:T(8,128)(2,1)S(1)}, u32[]{:S(2)}, u32[]{:S(2)}) collective-permute-start(s16[224,128]{1,0:T(8,128)(2,1)S(1)} %get-tuple-element.59), channel_id=1, source_target_pairs={{0,8},{2,10},{4,12},{6,14},{8,0},{10,2},{12,4},{14,6},{1,9},{3,11}... | collective-permute-start | bytes 172040 | tf_op jit(solution)/shard_map/ppermute | solution.py:394
